TPU v7x, 32 devices: a whole 2x2x4 slice. The times are simulated.
32 devices in a mesh: seq: 8 (over y, x, core), head: 4 (over z).
Axes of the slice: x: 2, y: 2, z: 4, core: 2. Of those that a mesh axis runs over, the one named last changes fastest.
Arguments:
- projected: bfloat16 [4096, 3, 3072], P(('seq', 'head')), may hold values from -70 to 70
- key_lists: int32 [48, 32, 8], P('head', 'seq'), may hold values from 0 to 31, as said below
- list_counts: int32 [48, 32], P('head', 'seq'), may hold values from 1 to 8
Outputs:
- attended: bfloat16 [4096, 3072], P(('seq', 'head'))
Inputs may be any that keep to these rules, and one draw needn't show every extreme that they name: `key_lists`: entries are key block numbers; no list names its own query block, and the entries of one list are distinct. Entry j of the list of query block b in head h lies on seq shard (b // 4 + o + j) mod 8, o depending on h and b. Over the 12 heads of one head group and the query blocks of one seq shard, exactly 48 entries lie on each seq shard, entries past a list's count included, and the entries that lie on one seq shard name at most two distinct key blocks: at most one whose number within its shard is below 2 and at most one whose number is at least that. In every draw some head group, seq shard and owning seq shard have two.
All inputs are finite; a program needn't handle non-finite values.
Results may differ from a plain program's by a relative error of at most 0.005.
Values may be sent and summed in bfloat16 or wider, within the bound.
No kernel may reach another device: no remote copies, remote signals or barrier semaphores. Data moves between devices by JAX's collectives and lax.ppermute only.
A program may use at most 128 MiB of HBM per device.

v0:
```python
import math

import jax
import jax.numpy as jnp
from jax import lax
from jax.sharding import PartitionSpec as P

NEG_FILL = -1e30


def attend_rows(query_part, gathered, live_cols, head_size):
    row_count, seen_blocks, block_len, doubled = gathered.shape
    key_rows = gathered[..., :head_size].reshape(row_count, seen_blocks * block_len, head_size)
    value_rows = gathered[..., head_size:].reshape(row_count, seen_blocks * block_len, head_size)
    attention_scores = jnp.einsum(
        "rqd,rkd->rqk", query_part, key_rows, preferred_element_type=jnp.float32
    ) * (1.0 / math.sqrt(head_size))
    attention_scores = attention_scores.reshape(row_count, block_len, seen_blocks, block_len)
    attention_scores = jnp.where(live_cols[:, None, :, None], attention_scores, NEG_FILL)
    row_top = jnp.max(attention_scores, axis=(2, 3), keepdims=True)
    exp_scores = jnp.exp(attention_scores - row_top)
    attention_weights = (exp_scores / jnp.sum(exp_scores, axis=(2, 3), keepdims=True)).astype(
        jnp.bfloat16
    )
    attention_weights = attention_weights.reshape(row_count, block_len, seen_blocks * block_len)
    return jnp.einsum(
        "rqk,rkd->rqd", attention_weights, value_rows, preferred_element_type=jnp.float32
    )


def on_device(projected, key_lists, list_counts):
    seq_count = lax.axis_size("seq")
    heads_dev, blocks_dev, list_most = key_lists.shape
    regrouped = lax.all_to_all(projected, "head", split_axis=2, concat_axis=0, tiled=True)
    block_len = regrouped.shape[0] // blocks_dev
    group_width = regrouped.shape[2]
    head_size = group_width // heads_dev
    row_count = heads_dev * blocks_dev
    splitted = regrouped.reshape(blocks_dev, block_len, 3, heads_dev, head_size)
    queries = splitted[:, :, 0].transpose(2, 0, 1, 3).reshape(row_count, block_len, head_size)
    kv_pairs = jnp.concatenate([splitted[:, :, 1], splitted[:, :, 2]], axis=-1)
    kv_pairs = kv_pairs.transpose(2, 0, 1, 3).reshape(row_count, block_len, 2 * head_size)
    entries = key_lists.reshape(row_count * list_most)
    owners = entries // blocks_dev
    row_head = jnp.arange(row_count * list_most, dtype=jnp.int32) // (blocks_dev * list_most)
    capacity = row_count * list_most // seq_count
    wanted = row_head * blocks_dev + entries % blocks_dev
    onehot = (owners[:, None] == jnp.arange(seq_count, dtype=jnp.int32)[None, :]).astype(jnp.int32)
    within = jnp.sum(onehot * (jnp.cumsum(onehot, axis=0) - 1), axis=1)
    slot_ids = owners * capacity + within
    request = (
        jnp.zeros((seq_count * capacity,), jnp.int32)
        .at[slot_ids]
        .set(wanted)
        .reshape(seq_count, capacity)
    )
    asked_for = lax.all_to_all(request, "seq", split_axis=0, concat_axis=0, tiled=True)
    served = jnp.take(kv_pairs, asked_for.reshape(-1), axis=0).reshape(
        seq_count, capacity, block_len, 2 * head_size
    )
    fetched = lax.all_to_all(served, "seq", split_axis=0, concat_axis=0, tiled=True)
    fetched = fetched.reshape(seq_count * capacity, block_len, 2 * head_size)
    entry_slots = slot_ids.reshape(row_count, list_most)
    row_counts = list_counts.reshape(row_count)
    group_rows = 4

    def one_group(group_index):
        start = group_index * group_rows
        query_part = lax.dynamic_slice_in_dim(queries, start, group_rows, 0)
        own_pairs = lax.dynamic_slice_in_dim(kv_pairs, start, group_rows, 0)
        slot_part = lax.dynamic_slice_in_dim(entry_slots, start, group_rows, 0)
        count_part = lax.dynamic_slice_in_dim(row_counts, start, group_rows, 0)
        listed = jnp.take(fetched, slot_part.reshape(-1), axis=0).reshape(
            group_rows, list_most, block_len, 2 * head_size
        )
        gathered = jnp.concatenate([own_pairs[:, None], listed], axis=1)
        live_cols = jnp.concatenate(
            [
                jnp.ones((group_rows, 1), bool),
                jnp.arange(list_most, dtype=jnp.int32)[None, :] < count_part[:, None],
            ],
            axis=1,
        )
        return attend_rows(query_part, gathered, live_cols, head_size).astype(jnp.bfloat16)

    attended = lax.map(one_group, jnp.arange(row_count // group_rows, dtype=jnp.int32))
    attended = attended.reshape(row_count, block_len, head_size)
    laid_out = attended.reshape(heads_dev, blocks_dev * block_len, head_size).transpose(1, 0, 2)
    laid_out = laid_out.reshape(blocks_dev * block_len, group_width)
    return lax.all_to_all(laid_out, "head", split_axis=0, concat_axis=1, tiled=True)


def solution(mesh):
    return jax.shard_map(
        on_device,
        mesh=mesh,
        in_specs=(P(("seq", "head"), None, None), P("head", "seq", None), P("head", "seq")),
        out_specs=P(("seq", "head"), None),
        check_vma=False,
    )
```

profile of v0, /device:TPU:0, one launch (start us, length us, event | category | flops | bytes accessed | tf_op | source)
XLA Modules:
  0.0 541.4 jit_solution(7548757384802746488)
XLA Ops:
  2.4 2.9 scatter_custom_fusion
  6.0 5.2 all-to-all-start.1
  11.2 5.7 %copy.35 = bf16[128,3,3072]{0,1,2:T(4,128)(2,1)} copy(bf16[128,3,3072]{2,0,1:T(8,128)(2,1)} %param.5) | data formatting | bytes 4718592 | tf_op args[0]
  16.9 4.9 all-to-all-start
  23.0 70.0 %all-to-all-done = bf16[128,3,3072]{0,1,2:T(4,128)(2,1)S(1)} async-done(((bf16[128,3,3072]{0,1,2:T(4,128)(2,1)}), bf16[128,3,3072]{0,1,2:T(4,128)(2,1)S(1)}, u32[]{:S(2)}, u32[]{:S(2)}) %all-to-all-start) | async-done | bytes 2359328 | tf_op jit(solution)/shard_map/all_to_all | solution.py:34
  95.7 11.3 %gather_fusion.1 = bf16[384,128,128]{2,1,0:T(8,128)(2,1)} fusion(bf16[48,128,128]{2,1,0:T(8,128)(2,1)S(1)} %bitcast.78, s32[1024]{0:T(1024)S(1)} %pad_clamp_fusion.1), kind=kCustom, calls=%fused_computation.1 | custom fusion | bytes 25167360 | tf_op jit(solution)/shard_map/jit(_take)/gather | solution.py:58
  107.1 10.8 %broadcast_select_fusion.1 = bf16[8,48,128,128]{3,2,1,0:T(8,128)(2,1)} fusion(bf16[8,48,128,128]{3,2,1,0:T(8,128)(2,1)} %bitcast.81, pred[8,48]{1,0:T(8,128)(4,1)S(1)} %compare_and_fusion.1), kind=kLoop, calls=%fused_computation.39 | loop fusion | flops 6291456 | bytes 25166208 | tf_op jit(solution)/shard_map/jit(_take)/select_n | solution.py:58
  117.8 5.7 %all-to-all-start.2 = ((bf16[8,48,128,128]{3,2,1,0:T(8,128)(2,1)}), bf16[8,48,128,128]{3,2,1,0:T(8,128)(2,1)}, u32[]{:S(2)}, u32[]{:S(2)}) async-start(bf16[8,48,128,128]{3,2,1,0:T(8,128)(2,1)} %broadcast_select_fusion.1), calls=%async_computation.2 | async-start | bytes 25165824 | tf_op jit(solution)/shard_map/all_to_all | solution.py:61
  124.8 137.5 %all-to-all-done.2 = bf16[8,48,128,128]{3,2,1,0:T(8,128)(2,1)} async-done(((bf16[8,48,128,128]{3,2,1,0:T(8,128)(2,1)}), bf16[8,48,128,128]{3,2,1,0:T(8,128)(2,1)}, u32[]{:S(2)}, u32[]{:S(2)}) %all-to-all-start.2) | async-done | bytes 12582944 | tf_op jit(solution)/shard_map/all_to_all | solution.py:61
  262.3 256.2 %while.10 = (s32[]{:T(128)}, bf16[12,4,128,64]{2,1,3,0:T(4,128)(2,1)}, s32[12]{0:T(128)S(1)}, s32[48]{0:T(128)S(1)}, bf16[48,128,64]{1,2,0:T(8,128)(2,1)}, /*ind...) while((s32[]{:T(128)}, ...), condition=%wide.region_7.8_spmd, body=%wide.region_4.7_spmd.sunk | while | flops 234721344 | bytes 13664708 | solution.py:86
  263.7 6.3 %gather_fusion = bf16[32,128,128]{2,1,0:T(8,128)(2,1)} fusion(bf16[384,128,128]{2,1,0:T(8,128)(2,1)} %get-tuple-element.162, s32[1024]{0:T(1024)S(1)} %pad_clamp_fusion.3), kind=kCustom, calls=%fused_computation.clone.1 | custom fusion | bytes 2097280 | tf_op jit(solution)/shard_map/while/body/eval_jaxpr/jit(_take)/gather | solution.py:73
  273.1 3.0 fusion.71
  277.9 1.8 fusion.72
  280.8 2.2 fusion.73
  285.0 6.3 %gather_fusion = bf16[32,128,128]{2,1,0:T(8,128)(2,1)} fusion(bf16[384,128,128]{2,1,0:T(8,128)(2,1)} %get-tuple-element.162, s32[1024]{0:T(1024)S(1)} %pad_clamp_fusion.3), kind=kCustom, calls=%fused_computation.clone.1 | custom fusion | bytes 2097280 | tf_op jit(solution)/shard_map/while/body/eval_jaxpr/jit(_take)/gather | solution.py:73
  294.4 3.0 fusion.71
  302.1 2.2 fusion.73
  306.4 6.3 %gather_fusion = bf16[32,128,128]{2,1,0:T(8,128)(2,1)} fusion(bf16[384,128,128]{2,1,0:T(8,128)(2,1)} %get-tuple-element.162, s32[1024]{0:T(1024)S(1)} %pad_clamp_fusion.3), kind=kCustom, calls=%fused_computation.clone.1 | custom fusion | bytes 2097280 | tf_op jit(solution)/shard_map/while/body/eval_jaxpr/jit(_take)/gather | solution.py:73
  315.8 3.0 fusion.71
  323.5 2.2 fusion.73
  327.7 6.3 %gather_fusion = bf16[32,128,128]{2,1,0:T(8,128)(2,1)} fusion(bf16[384,128,128]{2,1,0:T(8,128)(2,1)} %get-tuple-element.162, s32[1024]{0:T(1024)S(1)} %pad_clamp_fusion.3), kind=kCustom, calls=%fused_computation.clone.1 | custom fusion | bytes 2097280 | tf_op jit(solution)/shard_map/while/body/eval_jaxpr/jit(_take)/gather | solution.py:73
  337.1 3.0 fusion.71
  344.8 2.2 fusion.73
  349.1 6.3 %gather_fusion = bf16[32,128,128]{2,1,0:T(8,128)(2,1)} fusion(bf16[384,128,128]{2,1,0:T(8,128)(2,1)} %get-tuple-element.162, s32[1024]{0:T(1024)S(1)} %pad_clamp_fusion.3), kind=kCustom, calls=%fused_computation.clone.1 | custom fusion | bytes 2097280 | tf_op jit(solution)/shard_map/while/body/eval_jaxpr/jit(_take)/gather | solution.py:73
  358.5 3.0 fusion.71
  366.2 2.2 fusion.73
  370.4 6.3 %gather_fusion = bf16[32,128,128]{2,1,0:T(8,128)(2,1)} fusion(bf16[384,128,128]{2,1,0:T(8,128)(2,1)} %get-tuple-element.162, s32[1024]{0:T(1024)S(1)} %pad_clamp_fusion.3), kind=kCustom, calls=%fused_computation.clone.1 | custom fusion | bytes 2097280 | tf_op jit(solution)/shard_map/while/body/eval_jaxpr/jit(_take)/gather | solution.py:73
  379.8 3.0 fusion.71
  387.5 2.2 fusion.73
  391.8 6.3 %gather_fusion = bf16[32,128,128]{2,1,0:T(8,128)(2,1)} fusion(bf16[384,128,128]{2,1,0:T(8,128)(2,1)} %get-tuple-element.162, s32[1024]{0:T(1024)S(1)} %pad_clamp_fusion.3), kind=kCustom, calls=%fused_computation.clone.1 | custom fusion | bytes 2097280 | tf_op jit(solution)/shard_map/while/body/eval_jaxpr/jit(_take)/gather | solution.py:73
  401.1 3.0 fusion.71
  408.9 2.2 fusion.73
  413.1 6.3 %gather_fusion = bf16[32,128,128]{2,1,0:T(8,128)(2,1)} fusion(bf16[384,128,128]{2,1,0:T(8,128)(2,1)} %get-tuple-element.162, s32[1024]{0:T(1024)S(1)} %pad_clamp_fusion.3), kind=kCustom, calls=%fused_computation.clone.1 | custom fusion | bytes 2097280 | tf_op jit(solution)/shard_map/while/body/eval_jaxpr/jit(_take)/gather | solution.py:73
  422.5 3.0 fusion.71
  430.2 2.2 fusion.73
  434.5 6.3 %gather_fusion = bf16[32,128,128]{2,1,0:T(8,128)(2,1)} fusion(bf16[384,128,128]{2,1,0:T(8,128)(2,1)} %get-tuple-element.162, s32[1024]{0:T(1024)S(1)} %pad_clamp_fusion.3), kind=kCustom, calls=%fused_computation.clone.1 | custom fusion | bytes 2097280 | tf_op jit(solution)/shard_map/while/body/eval_jaxpr/jit(_take)/gather | solution.py:73
  443.8 3.0 fusion.71
  451.6 2.2 fusion.73
  455.8 6.3 %gather_fusion = bf16[32,128,128]{2,1,0:T(8,128)(2,1)} fusion(bf16[384,128,128]{2,1,0:T(8,128)(2,1)} %get-tuple-element.162, s32[1024]{0:T(1024)S(1)} %pad_clamp_fusion.3), kind=kCustom, calls=%fused_computation.clone.1 | custom fusion | bytes 2097280 | tf_op jit(solution)/shard_map/while/body/eval_jaxpr/jit(_take)/gather | solution.py:73
  465.2 3.0 fusion.71
  472.9 2.2 fusion.73
  477.2 6.3 %gather_fusion = bf16[32,128,128]{2,1,0:T(8,128)(2,1)} fusion(bf16[384,128,128]{2,1,0:T(8,128)(2,1)} %get-tuple-element.162, s32[1024]{0:T(1024)S(1)} %pad_clamp_fusion.3), kind=kCustom, calls=%fused_computation.clone.1 | custom fusion | bytes 2097280 | tf_op jit(solution)/shard_map/while/body/eval_jaxpr/jit(_take)/gather | solution.py:73
  486.5 3.0 fusion.71
  494.3 2.2 fusion.73
  498.5 6.3 %gather_fusion = bf16[32,128,128]{2,1,0:T(8,128)(2,1)} fusion(bf16[384,128,128]{2,1,0:T(8,128)(2,1)} %get-tuple-element.162, s32[1024]{0:T(1024)S(1)} %pad_clamp_fusion.3), kind=kCustom, calls=%fused_computation.clone.1 | custom fusion | bytes 2097280 | tf_op jit(solution)/shard_map/while/body/eval_jaxpr/jit(_take)/gather | solution.py:73
  507.9 3.0 fusion.71
  515.6 2.2 fusion.73
  520.5 19.7 %all_to_all.48 = bf16[4,128,768]{1,2,0:T(8,128)(2,1)S(1)} all-to-all(bf16[4,128,768]{1,2,0:T(8,128)(2,1)S(1)} %copy.46), channel_id=1, replica_groups=mesh['seq'=8,'head'=4] {'head'}, dimensions={0} | all-to-all | bytes 1572864 | tf_op jit(solution)/shard_map/all_to_all | solution.py:90
  (256 shorter events, 120.1 us)
Async XLA Ops:
  6.0 10.9 %all-to-all-start.1 = ((s32[8,1,48]{2,1,0:T(1,128)}), s32[8,1,48]{2,1,0:T(1,128)S(1)}, u32[]{:S(2)}, u32[]{:S(2)}) async-start(s32[8,1,48]{2,1,0:T(1,128)} %all_to_all.37), calls=%async_computation.1 | async-start | bytes 8192 | tf_op jit(solution)/shard_map/all_to_all | solution.py:57
  16.9 76.2 %all-to-all-start = ((bf16[128,3,3072]{0,1,2:T(4,128)(2,1)}), bf16[128,3,3072]{0,1,2:T(4,128)(2,1)S(1)}, u32[]{:S(2)}, u32[]{:S(2)}) async-start(bf16[128,3,3072]{0,1,2:T(4,128)(2,1)} %copy.35), calls=%async_computation | async-start | bytes 6291456 | tf_op jit(solution)/shard_map/all_to_all | solution.py:34
  117.8 5.8 %copy-start.1 = (s32[12,4]{0,1:T(4,128)S(1)}, s32[12,4]{0,1:T(4,128)}, u32[]{:S(2)}) copy-start(s32[12,4]{0,1:T(4,128)} %param.7) | copy-start | bytes 580
  117.8 6.0 %copy-start = (bf16[12,4,128,64]{2,3,0,1:T(8,128)(2,1)S(1)}, bf16[12,4,128,64]{2,3,0,1:T(8,128)(2,1)}, u32[]{:S(2)}) copy-start(bf16[12,4,128,64]{2,3,0,1:T(8,128)(2,1)} %get-tuple-element.69) | copy-start | bytes 2359300
  117.8 144.5 %all-to-all-start.2 = ((bf16[8,48,128,128]{3,2,1,0:T(8,128)(2,1)}), bf16[8,48,128,128]{3,2,1,0:T(8,128)(2,1)}, u32[]{:S(2)}, u32[]{:S(2)}) async-start(bf16[8,48,128,128]{3,2,1,0:T(8,128)(2,1)} %broadcast_select_fusion.1), calls=%async_computation.2 | async-start | bytes 25165824 | tf_op jit(solution)/shard_map/all_to_all | solution.py:61
where the time goes:
time: 545 us; the launch traced here: 541 us
  waiting for transfers between devices  208 us (38%)
  local copies, waits for them, and re-layouts  178 us (33%)
  other arithmetic  64.3 us (12%)
  matrix products  47.5 us (9%)
  blocking collectives  19.7 us (4%)
  starting transfers between devices  15.7 us (3%)
  loops' own time  8.01 us (1%)
    all_to_all x1, waiting for transfers between devices, on_device(): lax.all_to_all(served, 'seq', split_axis=0, concat_axis=0, tiled=True)  137 us
    gather x24, local copies, waits for them, and re-layouts, one_group(): jnp.take(fetched, slot_part.reshape(-1), axis=0)  95.7 us
    all_to_all x1, waiting for transfers between devices, on_device(): lax.all_to_all(projected, 'head', split_axis=2, concat_axis=0, tiled=True)  70 us
    concatenate x12, other arithmetic, one_group(): gathered = jnp.concatenate([own_pairs[:, None], listed], axis=1)  35.8 us
    dot_general x12, matrix products, attend_rows(): jnp.einsum('rqk,rkd->rqd', attention_weights, value_rows, preferred_eleme...  26.2 us
    sub x12, matrix products, attend_rows(): exp_scores = jnp.exp(attention_scores - row_top)  21.2 us
    all_to_all x1, blocking collectives, on_device(): lax.all_to_all(laid_out, 'head', split_axis=0, concat_axis=1, tiled=True)  19.7 us
    reshape x12, local copies, waits for them, and re-layouts, attend_rows(): gathered[..., :head_size]  17.7 us
  transfers between devices with their start and end apart: 3, of which 2 were waited for; matrix products, arithmetic and copies ran while one was open for 2% of the time, Pallas kernels for 0%

commit v1 on v0

--- a/solution.py
+++ b/solution.py
@@ -1,11 +1,198 @@
+import functools
 import math
 
 import jax
 import jax.numpy as jnp
 from jax import lax
+from jax.experimental import pallas as pl
+from jax.experimental.pallas import tpu as pltpu
+from jax.sharding import Mesh
 from jax.sharding import PartitionSpec as P
 
 NEG_FILL = -1e30
+LOG2E = 1.4426950408889634
+PAIR = 2
+ROWS = 4
+STEP = 3
+SUM_ROWS = 16
+
+
+def pack_kernel(q_ref, k_ref, v_ref, out_ref, *, per_chip, head_size):
+    tokens = q_ref.shape[0]
+    half = tokens // 2
+    lanes = 2 * head_size
+    for pair in range(q_ref.shape[1] // lanes):
+        cols = slice(pair * lanes, (pair + 1) * lanes)
+        q_t = q_ref[:, cols].T
+        v_t = v_ref[:, cols].T
+        k_tile = k_ref[:, cols]
+        for odd in range(2):
+            chip, j = divmod(2 * pair + odd, per_chip)
+            part = slice(odd * head_size, (odd + 1) * head_size)
+            out_ref[chip, j, 0] = q_t[part]
+            out_ref[chip, j, 1] = jnp.concatenate([k_tile[:half, part], k_tile[half:, part]], axis=1)
+            out_ref[chip, j, 2] = v_t[part]
+
+
+def pack(queries, keys, values, *, chips, per_chip, head_size):
+    tokens, width = queries.shape
+    steps = 8
+    spec = pl.BlockSpec((tokens, width // steps), lambda i: (0, i))
+    return pl.pallas_call(
+        functools.partial(pack_kernel, per_chip=per_chip, head_size=head_size),
+        grid=(steps,),
+        in_specs=[spec] * 3,
+        out_specs=pl.BlockSpec(
+            (chips // steps, per_chip, 3, head_size, tokens), lambda i: (i, 0, 0, 0, 0)
+        ),
+        out_shape=jax.ShapeDtypeStruct((chips, per_chip, 3, head_size, tokens), queries.dtype),
+        name="pack",
+    )(queries, keys, values)
+
+
+def attend_kernel(slots_ref, counts_ref, mine_ref, other_ref, out_ref, kv, total, *, scale, list_most):
+    blocks, _, _, head_size, tokens = mine_ref.shape
+    head = pl.program_id(0)
+    for b in range(blocks):
+        kv[b] = mine_ref[b, 0, 1:3]
+        kv[blocks + b] = other_ref[b, 0]
+    entries = 1 + list_most
+    ones = jnp.ones((SUM_ROWS, tokens), jnp.bfloat16)
+    zeros = jnp.zeros((head_size, tokens), jnp.bfloat16)
+
+    def group(g, carry):
+        base = g * ROWS
+        counts = [counts_ref[head * blocks + base + r] for r in range(ROWS)]
+        most = functools.reduce(jnp.maximum, counts)
+        weights = []
+        for r in range(ROWS):
+            q_t = mine_ref[base + r, 0, 0]
+            weights.append(
+                jnp.concatenate(
+                    [jnp.concatenate([q_t, zeros], axis=1), jnp.concatenate([zeros, q_t], axis=1)],
+                    axis=0,
+                )
+            )
+
+        def chunk(first, width, old):
+            tops, result = [], []
+            for r in range(ROWS):
+                row = (head * blocks + base + r) * entries
+                own = slots_ref[row]
+                keys, vals = [], []
+                for e in range(first, first + width):
+                    if e == 0:
+                        slot = own
+                        keys.append(kv[slot, 0])
+                        vals.append(jnp.concatenate([kv[slot, 1], ones], axis=0))
+                    else:
+                        live = e <= counts[r]
+                        slot = jnp.where(live, slots_ref[row + e], own)
+                        factor = jnp.where(live, 1.0, 0.0).astype(jnp.bfloat16)
+                        keys.append(kv[slot, 0])
+                        vals.append(jnp.concatenate([kv[slot, 1], ones], axis=0) * factor)
+                scores = jnp.dot(
+                    jnp.concatenate(keys, axis=0), weights[r], preferred_element_type=jnp.float32
+                )
+                top = jnp.max(scores, axis=0, keepdims=True)
+                top = jnp.maximum(top[:, :tokens], top[:, tokens:])
+                if old is not None:
+                    top = jnp.maximum(top, old[r])
+                both = jnp.concatenate([top, top], axis=1)
+                probs = jnp.exp2((scores - both) * scale).astype(jnp.bfloat16)
+                probs = jnp.concatenate(
+                    [
+                        probs[w * head_size : (w + 1) * head_size, c * tokens : (c + 1) * tokens]
+                        for w in range(width)
+                        for c in range(2)
+                    ],
+                    axis=0,
+                )
+                part = jnp.dot(
+                    jnp.concatenate(vals, axis=1), probs, preferred_element_type=jnp.float32
+                )
+                if old is not None:
+                    part = part + total[r] * jnp.exp2((old[r] - top) * scale)
+                total[r] = part
+                tops.append(top)
+            return tuple(tops)
+
+        tops = chunk(0, STEP, None)
+        for first in range(STEP, entries, STEP):
+            tops = lax.cond(
+                most >= first,
+                functools.partial(chunk, first, min(STEP, entries - first)),
+                lambda old: old,
+                tops,
+            )
+        for r in range(ROWS):
+            whole = total[r]
+            out_ref[base + r, 0] = (whole[:head_size] / whole[head_size : head_size + 1]).astype(
+                out_ref.dtype
+            )
+        return carry
+
+    lax.fori_loop(0, blocks // ROWS, group, 0)
+
+
+def attend(slots, counts, mine, other, *, list_most):
+    blocks, per_chip, _, head_size, tokens = mine.shape
+    return pl.pallas_call(
+        functools.partial(
+            attend_kernel, scale=LOG2E / math.sqrt(head_size), list_most=list_most
+        ),
+        grid_spec=pltpu.PrefetchScalarGridSpec(
+            num_scalar_prefetch=2,
+            grid=(per_chip,),
+            in_specs=[
+                pl.BlockSpec((blocks, 1, 3, head_size, tokens), lambda j, s, c: (0, j, 0, 0, 0)),
+                pl.BlockSpec((blocks, 1, 2, head_size, tokens), lambda j, s, c: (0, j, 0, 0, 0)),
+            ],
+            out_specs=pl.BlockSpec((blocks, 1, head_size, tokens), lambda j, s, c: (0, j, 0, 0)),
+            scratch_shapes=[
+                pltpu.VMEM((2 * blocks, 2, head_size, tokens), jnp.bfloat16),
+                pltpu.VMEM((ROWS, head_size + SUM_ROWS, tokens), jnp.float32),
+            ],
+        ),
+        out_shape=jax.ShapeDtypeStruct((blocks, per_chip, head_size, tokens), mine.dtype),
+        compiler_params=pltpu.CompilerParams(vmem_limit_bytes=48 << 20),
+        name="attend",
+    )(slots, counts, mine, other)
+
+
+def on_pair(projected, key_lists, list_counts, *, chips_seq, head_count):
+    tokens, _, width = projected.shape
+    heads_dev, blocks_dev, list_most = key_lists.shape
+    chips = chips_seq * head_count
+    head_size = width // (heads_dev * head_count)
+    per_chip = heads_dev // chips_seq
+    core = lax.axis_index("core")
+
+    table = jnp.concatenate([key_lists, list_counts[:, :, None]], axis=2)
+    table = lax.all_to_all(
+        table.reshape(chips_seq, per_chip, blocks_dev, list_most + 1),
+        "chip", split_axis=0, concat_axis=0, tiled=True,
+    )
+    table = table.transpose(1, 2, 0, 3).reshape(per_chip * chips, list_most + 1)
+    listed, counts = table[:, :list_most], table[:, list_most]
+    shard = listed // blocks_dev
+    slots = (
+        ((shard % PAIR) != core).astype(jnp.int32) * chips
+        + (listed % blocks_dev) * chips_seq
+        + shard // PAIR
+    )
+    own = jnp.arange(per_chip * chips, dtype=jnp.int32)[:, None] % chips
+    slots = jnp.concatenate([own, slots], axis=1).reshape(-1)
+
+    packed = pack(
+        projected[:, 0], projected[:, 1], projected[:, 2],
+        chips=chips, per_chip=per_chip, head_size=head_size,
+    )
+    mine = lax.all_to_all(packed, ("head", "chip"), split_axis=0, concat_axis=0, tiled=True)
+    other = lax.ppermute(mine[:, :, 1:], "core", [(0, 1), (1, 0)])
+    attended = attend(slots, counts, mine, other, list_most=list_most)
+    back = lax.all_to_all(attended, ("head", "chip"), split_axis=0, concat_axis=0, tiled=True)
+    return back.reshape(width, tokens).T
 
 
 def attend_rows(query_part, gathered, live_cols, head_size):
@@ -90,11 +277,38 @@
     return lax.all_to_all(laid_out, "head", split_axis=0, concat_axis=1, tiled=True)
 
 
+def whole_heads_fit(mesh, projected, key_lists):
+    seq_count, head_count = mesh.shape["seq"], mesh.shape["head"]
+    if seq_count % PAIR:
+        return False
+    chips_seq = seq_count // PAIR
+    chips = chips_seq * head_count
+    group_heads = key_lists.shape[0] // head_count
+    one_block = key_lists.shape[1] == seq_count * head_count
+    return one_block and group_heads % chips_seq == 0 and chips % 8 == 0 and chips % ROWS == 0
+
+
 def solution(mesh):
-    return jax.shard_map(
-        on_device,
-        mesh=mesh,
-        in_specs=(P(("seq", "head"), None, None), P("head", "seq", None), P("head", "seq")),
-        out_specs=P(("seq", "head"), None),
-        check_vma=False,
-    )
+    seq_count, head_count = mesh.shape["seq"], mesh.shape["head"]
+
+    def run(projected, key_lists, list_counts):
+        if not whole_heads_fit(mesh, projected, key_lists):
+            return jax.shard_map(
+                on_device,
+                mesh=mesh,
+                in_specs=(P(("seq", "head"), None, None), P("head", "seq", None), P("head", "seq")),
+                out_specs=P(("seq", "head"), None),
+                check_vma=False,
+            )(projected, key_lists, list_counts)
+        chips_seq = seq_count // PAIR
+        split = Mesh(mesh.devices.reshape(chips_seq, PAIR, head_count), ("chip", "core", "head"))
+        seq = ("chip", "core")
+        return jax.shard_map(
+            functools.partial(on_pair, chips_seq=chips_seq, head_count=head_count),
+            mesh=split,
+            in_specs=(P(seq + ("head",), None, None), P("head", seq, None), P("head", seq)),
+            out_specs=P(seq + ("head",), None),
+            check_vma=False,
+        )(projected, key_lists, list_counts)
+
+    return run

time: 545 us -> 146 us (0.27)
  waiting for transfers between devices: 208 us -> 4.69 us
  local copies, waits for them, and re-layouts: 178 us -> 6.24 us
  blocking collectives: 19.7 us -> 90.5 us
  other arithmetic: 64.3 us -> 0.84 us
  matrix products: 47.5 us -> 0 us
  Pallas kernels: 0 us -> 38.7 us
  starting transfers between devices: 15.7 us -> 3.26 us
  loops' own time: 8.01 us -> 0 us
    all_to_all x3 -> x1, waiting for transfers between devices: 208 us -> 4.68 us  [on_pair(): lax.all_to_all(table.reshape(chips_seq, per_chip, blocks_dev, list_most +...]
    gather x25 -> x0, local copies, waits for them, and re-layouts: 107 us -> none  [the longest x24 95.7 us: one_group(): jnp.take(fetched, slot_part.reshape(-1), axis=0)]
    all_to_all x1 -> x2, blocking collectives: 19.7 us -> 90.5 us  [the longest x1 63.3 us: on_pair(): lax.all_to_all(packed, ('head', 'chip'), split_axis=0, concat_axis=0, til...]
    pallas_call x0 -> x2, Pallas kernels: none -> 38.7 us  [the longest x1 32.3 us: attend(): pl.pallas_call(functools.partial(attend_kernel, scale=LOG2E / math.sqrt(h...]
    concatenate x12 -> x2, other arithmetic: 35.8 us -> 0.78 us  [the longest x1 0.7 us: on_pair(): table = jnp.concatenate([key_lists, list_counts[:, :, None]], axis=2)]
    reshape x41 -> x2, local copies, waits for them, and re-layouts: 33.2 us -> 1.28 us  [the longest x1 1.16 us: on_pair(): return back.reshape(width, tokens).T]
    dot_general x12 -> x0, matrix products: 26.2 us -> none  [attend_rows(): jnp.einsum('rqk,rkd->rqd', attention_weights, value_rows, preferred_eleme...]
    select_n x28 -> x1, other arithmetic: 25.5 us -> 0.01 us  [on_pair(): own = jnp.arange(per_chip * chips, dtype=jnp.int32)[:, None] % chips]
  transfers between devices with their start and end apart: 3 -> 2, of which waited for: 2 -> 1; matrix products, arithmetic and copies ran while one was open for 2% -> 1% of each run, Pallas kernels for 0% -> 0%
where the time goes in v1:
time: 146 us; the launch traced here: 144 us
  blocking collectives  90.5 us (62%)
  Pallas kernels  38.7 us (27%)
  local copies, waits for them, and re-layouts  6.24 us (4%)
  waiting for transfers between devices  4.69 us (3%)
  starting transfers between devices  3.26 us (2%)
    all_to_all x1, blocking collectives, on_pair(): lax.all_to_all(packed, ('head', 'chip'), split_axis=0, concat_axis=0, til...  63.3 us
    pallas_call x1, Pallas kernels, attend(): pl.pallas_call(functools.partial(attend_kernel, scale=LOG2E / math.sqrt(h...  32.3 us
    all_to_all x1, blocking collectives, on_pair(): lax.all_to_all(attended, ('head', 'chip'), split_axis=0, concat_axis=0, t...  27.2 us
    pallas_call x1, Pallas kernels, pack(): pl.pallas_call(functools.partial(pack_kernel, per_chip=per_chip, head_siz...  6.44 us
    all_to_all x1, waiting for transfers between devices, on_pair(): lax.all_to_all(table.reshape(chips_seq, per_chip, blocks_dev, list_most +...  4.68 us
    all_to_all x1, starting transfers between devices, on_pair(): lax.all_to_all(table.reshape(chips_seq, per_chip, blocks_dev, list_most +...  3.26 us
    squeeze x1, local copies, waits for them, and re-layouts, on_pair(): projected[:, 2]  3.05 us
  transfers between devices with their start and end apart: 2, of which 1 were waited for; matrix products, arithmetic and copies ran while one was open for 1% of the time, Pallas kernels for 0%

profile of v1, /device:TPU:0, one launch (start us, length us, event | category | flops | bytes accessed | tf_op | source)
XLA Modules:
  0.0 144.3 jit_solution(2202728889782479668)
XLA Ops:
  0.0 3.1 %slice_bitcast_fusion = (bf16[128,3072]{1,0:T(8,128)(2,1)}, bf16[128,3072]{1,0:T(8,128)(2,1)}, bf16[128,3072]{1,0:T(8,128)(2,1)}) fusion(bf16[128,3,3072]{2,0,1:T(8,128)(2,1)} %param.3), kind=kLoop, calls=%fused_computation | loop fusion | bytes 4718592 | tf_op jit(solution)/shard_map/squeeze | solution.py:188
  3.1 6.4 %pack.1 = bf16[16,3,3,64,128]{4,3,2,1,0:T(8,128)(2,1)} custom-call(bf16[128,3072]{1,0:T(8,128)(2,1)} %get-tuple-element.6.q_ref, bf16[128,3072]{1,0:T(8,128)(2,1)} %get-tuple-element.7.k_ref, bf16[128,3072]{1,0:T(8,128)(2,1)} %get-tuple-element.5.v_ref), custom_call_target="tpu_custom_call" | custom-call | tf_op jit(solution)/shard_map/pack/pallas_call | solution.py:41
  9.5 63.3 %all_to_all.15.mine_ref = bf16[16,3,3,64,128]{4,3,2,1,0:T(8,128)(2,1)S(1)} all-to-all(bf16[16,3,3,64,128]{4,3,2,1,0:T(8,128)(2,1)} %pack.1), channel_id=1, replica_groups=mesh['chip'=4,'core'=2,'head'=4] {'head','chip'}, dimensions={0} | all-to-all | bytes 4718592 | tf_op jit(solution)/shard_map/all_to_all | solution.py:191
  72.8 0.0 copy-start.1
  72.8 0.0 copy-start
  72.8 1.3 slice.26
  74.1 0.0 collective-permute-start
  74.1 0.0 copy-done.1
  74.1 0.1 concatenate.12
  74.2 0.2 copy.22
  74.4 0.0 copy-done
  74.4 0.1 copy.21
  74.5 0.7 pad_add_fusion
  75.2 3.3 %all-to-all-start = ((s32[4,3,4,9]{3,2,1,0:T(4,128)}), s32[4,3,4,9]{3,2,1,0:T(4,128)S(1)}, u32[]{:S(2)}, u32[]{:S(2)}) async-start(s32[4,3,4,9]{3,2,1,0:T(4,128)} %pad_add_fusion), calls=%async_computation | async-start | bytes 49152 | tf_op jit(solution)/shard_map/all_to_all | solution.py:172
  78.5 4.7 %all-to-all-done = s32[4,3,4,9]{3,2,1,0:T(4,128)S(1)} async-done(((s32[4,3,4,9]{3,2,1,0:T(4,128)}), s32[4,3,4,9]{3,2,1,0:T(4,128)S(1)}, u32[]{:S(2)}, u32[]{:S(2)}) %all-to-all-start) | async-done | bytes 1760 | tf_op jit(solution)/shard_map/all_to_all | solution.py:172
  83.2 0.1 fusion.3
  83.3 0.1 pad_add_fusion.1
  83.3 0.1 reshape.42.slots_ref
  83.5 0.2 slice_reduce_fusion.counts_ref
  83.6 0.0 collective-permute-done.other_ref
  83.7 32.3 %attend.1 = bf16[16,3,64,128]{3,2,1,0:T(8,128)(2,1)S(1)} custom-call(s32[432]{0:T(512)S(1)} %reshape.42.slots_ref, s32[48]{0:T(128)S(1)} %slice_reduce_fusion.counts_ref, bf16[16,3,3,64,128]{4,3,2,1,0:T(8,128)(2,1)S(1)} %all_to_all.15.mine_ref, bf16[16,3,2,64,128]{4,3,2,1,0:T(8,128)(2,1)} %collective-permute-done.other_ref), custom_call_target="tpu_custom_call" | custom-call | tf_op jit(solution)/shard_map/attend/pallas_call | solution.py:140
  115.9 27.2 %all_to_all.16 = bf16[16,3,64,128]{3,2,1,0:T(8,128)(2,1)S(1)} all-to-all(bf16[16,3,64,128]{3,2,1,0:T(8,128)(2,1)S(1)} %attend.1), channel_id=1, replica_groups=mesh['chip'=4,'core'=2,'head'=4] {'head','chip'}, dimensions={0} | all-to-all | bytes 1572864 | tf_op jit(solution)/shard_map/all_to_all | solution.py:194
  143.2 1.2 copy.24
  (2 shorter events, 0.0 us)
Async XLA Ops:
  72.8 1.3 copy-start.1
  72.8 1.6 %copy-start = (s32[12,4,8]{0,2,1:T(8,128)S(1)}, s32[12,4,8]{0,2,1:T(8,128)}, u32[]{:S(2)}) copy-start(s32[12,4,8]{0,2,1:T(8,128)} %param.4) | copy-start | bytes 4612
  74.1 9.5 %collective-permute-start = (bf16[16,3,2,64,128]{4,3,2,1,0:T(8,128)(2,1)}, bf16[16,3,2,64,128]{4,3,2,1,0:T(8,128)(2,1)}, u32[]{:S(2)}, u32[]{:S(2)}) collective-permute-start(bf16[16,3,2,64,128]{4,3,2,1,0:T(8,128)(2,1)} %slice.26), channel_id=1, source_target_pairs={{0,4},{4,0},{1,5},{5,1},{2,6},{6,2},{3,7},{7,3},{8,12},{12,8},{9,1... | collective-permute-start | bytes 4718600 | tf_op jit(solution)/shard_map/ppermute | solution.py:192
  75.2 8.0 %all-to-all-start = ((s32[4,3,4,9]{3,2,1,0:T(4,128)}), s32[4,3,4,9]{3,2,1,0:T(4,128)S(1)}, u32[]{:S(2)}, u32[]{:S(2)}) async-start(s32[4,3,4,9]{3,2,1,0:T(4,128)} %pad_add_fusion), calls=%async_computation | async-start | bytes 49152 | tf_op jit(solution)/shard_map/all_to_all | solution.py:172

commit v2 on v1

--- a/solution.py
+++ b/solution.py
@@ -12,8 +12,7 @@
 NEG_FILL = -1e30
 LOG2E = 1.4426950408889634
 PAIR = 2
-ROWS = 4
-STEP = 3
+ROWS = 8
 SUM_ROWS = 16
 
 
@@ -50,7 +49,7 @@
     )(queries, keys, values)
 
 
-def attend_kernel(slots_ref, counts_ref, mine_ref, other_ref, out_ref, kv, total, *, scale, list_most):
+def attend_kernel(slots_ref, counts_ref, mine_ref, other_ref, out_ref, kv, *, scale, list_most):
     blocks, _, _, head_size, tokens = mine_ref.shape
     head = pl.program_id(0)
     for b in range(blocks):
@@ -60,76 +59,55 @@
     ones = jnp.ones((SUM_ROWS, tokens), jnp.bfloat16)
     zeros = jnp.zeros((head_size, tokens), jnp.bfloat16)
 
+    def rows_of(base, counts, seen):
+        scores, values = [], []
+        for r in range(ROWS):
+            row = (head * blocks + base + r) * entries
+            own = slots_ref[row]
+            q_t = mine_ref[base + r, 0, 0]
+            both = [jnp.concatenate([q_t, zeros], axis=1), jnp.concatenate([zeros, q_t], axis=1)]
+            keys, vals = [kv[own, 0]], [jnp.concatenate([kv[own, 1], ones], axis=0)]
+            for e in range(1, seen):
+                live = e <= counts[r]
+                slot = jnp.where(live, slots_ref[row + e], own)
+                factor = jnp.where(live, 1.0, 0.0).astype(jnp.bfloat16)
+                keys.append(kv[slot, 0])
+                vals.append(jnp.concatenate([kv[slot, 1], ones], axis=0) * factor)
+            scores.append(
+                jnp.dot(
+                    jnp.concatenate(keys, axis=0),
+                    jnp.concatenate(both, axis=0),
+                    preferred_element_type=jnp.float32,
+                )
+            )
+            values.append(jnp.concatenate(vals, axis=1))
+        for r in range(ROWS):
+            top = jnp.max(scores[r], axis=0, keepdims=True)
+            top = jnp.maximum(top[:, :tokens], top[:, tokens:])
+            top = jnp.concatenate([top, top], axis=1)
+            probs = jnp.exp2((scores[r] - top) * scale).astype(jnp.bfloat16)
+            probs = [
+                probs[e * head_size : (e + 1) * head_size, c * tokens : (c + 1) * tokens]
+                for e in range(seen)
+                for c in range(2)
+            ]
+            total = jnp.dot(
+                values[r], jnp.concatenate(probs, axis=0), preferred_element_type=jnp.float32
+            )
+            out_ref[base + r, 0] = (total[:head_size] / total[head_size : head_size + 1]).astype(
+                out_ref.dtype
+            )
+
     def group(g, carry):
         base = g * ROWS
         counts = [counts_ref[head * blocks + base + r] for r in range(ROWS)]
-        most = functools.reduce(jnp.maximum, counts)
-        weights = []
-        for r in range(ROWS):
-            q_t = mine_ref[base + r, 0, 0]
-            weights.append(
-                jnp.concatenate(
-                    [jnp.concatenate([q_t, zeros], axis=1), jnp.concatenate([zeros, q_t], axis=1)],
-                    axis=0,
-                )
-            )
-
-        def chunk(first, width, old):
-            tops, result = [], []
-            for r in range(ROWS):
-                row = (head * blocks + base + r) * entries
-                own = slots_ref[row]
-                keys, vals = [], []
-                for e in range(first, first + width):
-                    if e == 0:
-                        slot = own
-                        keys.append(kv[slot, 0])
-                        vals.append(jnp.concatenate([kv[slot, 1], ones], axis=0))
-                    else:
-                        live = e <= counts[r]
-                        slot = jnp.where(live, slots_ref[row + e], own)
-                        factor = jnp.where(live, 1.0, 0.0).astype(jnp.bfloat16)
-                        keys.append(kv[slot, 0])
-                        vals.append(jnp.concatenate([kv[slot, 1], ones], axis=0) * factor)
-                scores = jnp.dot(
-                    jnp.concatenate(keys, axis=0), weights[r], preferred_element_type=jnp.float32
-                )
-                top = jnp.max(scores, axis=0, keepdims=True)
-                top = jnp.maximum(top[:, :tokens], top[:, tokens:])
-                if old is not None:
-                    top = jnp.maximum(top, old[r])
-                both = jnp.concatenate([top, top], axis=1)
-                probs = jnp.exp2((scores - both) * scale).astype(jnp.bfloat16)
-                probs = jnp.concatenate(
-                    [
-                        probs[w * head_size : (w + 1) * head_size, c * tokens : (c + 1) * tokens]
-                        for w in range(width)
-                        for c in range(2)
-                    ],
-                    axis=0,
-                )
-                part = jnp.dot(
-                    jnp.concatenate(vals, axis=1), probs, preferred_element_type=jnp.float32
-                )
-                if old is not None:
-                    part = part + total[r] * jnp.exp2((old[r] - top) * scale)
-                total[r] = part
-                tops.append(top)
-            return tuple(tops)
-
-        tops = chunk(0, STEP, None)
-        for first in range(STEP, entries, STEP):
-            tops = lax.cond(
-                most >= first,
-                functools.partial(chunk, first, min(STEP, entries - first)),
-                lambda old: old,
-                tops,
-            )
-        for r in range(ROWS):
-            whole = total[r]
-            out_ref[base + r, 0] = (whole[:head_size] / whole[head_size : head_size + 1]).astype(
-                out_ref.dtype
-            )
+        seen = 1 + functools.reduce(jnp.maximum, counts)
+        below = 0
+        for size in (*range(3, entries, 2), entries):
+            pl.when((seen > below) & (seen <= size))(
+                functools.partial(rows_of, base, counts, size)
+            )
+            below = size
         return carry
 
     lax.fori_loop(0, blocks // ROWS, group, 0)
@@ -149,10 +127,7 @@
                 pl.BlockSpec((blocks, 1, 2, head_size, tokens), lambda j, s, c: (0, j, 0, 0, 0)),
             ],
             out_specs=pl.BlockSpec((blocks, 1, head_size, tokens), lambda j, s, c: (0, j, 0, 0)),
-            scratch_shapes=[
-                pltpu.VMEM((2 * blocks, 2, head_size, tokens), jnp.bfloat16),
-                pltpu.VMEM((ROWS, head_size + SUM_ROWS, tokens), jnp.float32),
-            ],
+            scratch_shapes=[pltpu.VMEM((2 * blocks, 2, head_size, tokens), jnp.bfloat16)],
         ),
         out_shape=jax.ShapeDtypeStruct((blocks, per_chip, head_size, tokens), mine.dtype),
         compiler_params=pltpu.CompilerParams(vmem_limit_bytes=48 << 20),

time: 146 us -> 122 us (0.84)
  Pallas kernels: 38.7 us -> 19 us
  blocking collectives: 90.5 us -> 86.5 us
    pallas_call x1, Pallas kernels: 32.3 us -> 12.6 us  [attend(): pl.pallas_call(functools.partial(attend_kernel, scale=LOG2E / math.sqrt(h...]
    all_to_all x1, blocking collectives: 27.2 us -> 23.2 us  [on_pair(): lax.all_to_all(attended, ('head', 'chip'), split_axis=0, concat_axis=0, t...]
where the time goes in v2:
time: 122 us; the launch traced here: 121 us
  blocking collectives  86.5 us (71%)
  Pallas kernels  19 us (16%)
  local copies, waits for them, and re-layouts  6.24 us (5%)
  waiting for transfers between devices  4.69 us (4%)
  starting transfers between devices  3.26 us (3%)
    all_to_all x1, blocking collectives, on_pair(): lax.all_to_all(packed, ('head', 'chip'), split_axis=0, concat_axis=0, til...  63.3 us
    all_to_all x1, blocking collectives, on_pair(): lax.all_to_all(attended, ('head', 'chip'), split_axis=0, concat_axis=0, t...  23.2 us
    pallas_call x1, Pallas kernels, attend(): pl.pallas_call(functools.partial(attend_kernel, scale=LOG2E / math.sqrt(h...  12.6 us
    pallas_call x1, Pallas kernels, pack(): pl.pallas_call(functools.partial(pack_kernel, per_chip=per_chip, head_siz...  6.44 us
    all_to_all x1, waiting for transfers between devices, on_pair(): lax.all_to_all(table.reshape(chips_seq, per_chip, blocks_dev, list_most +...  4.68 us
    all_to_all x1, starting transfers between devices, on_pair(): lax.all_to_all(table.reshape(chips_seq, per_chip, blocks_dev, list_most +...  3.26 us
    squeeze x1, local copies, waits for them, and re-layouts, on_pair(): projected[:, 2]  3.05 us
  transfers between devices with their start and end apart: 2, of which 1 were waited for; matrix products, arithmetic and copies ran while one was open for 1% of the time, Pallas kernels for 0%

profile of v2, /device:TPU:0, one launch (start us, length us, event | category | flops | bytes accessed | tf_op | source)
XLA Modules:
  0.0 120.6 jit_solution(15850987109585272164)
XLA Ops:
  0.0 3.1 %slice_bitcast_fusion = (bf16[128,3072]{1,0:T(8,128)(2,1)}, bf16[128,3072]{1,0:T(8,128)(2,1)}, bf16[128,3072]{1,0:T(8,128)(2,1)}) fusion(bf16[128,3,3072]{2,0,1:T(8,128)(2,1)} %param.3), kind=kLoop, calls=%fused_computation | loop fusion | bytes 4718592 | tf_op jit(solution)/shard_map/squeeze | solution.py:163
  3.1 6.4 %pack.1 = bf16[16,3,3,64,128]{4,3,2,1,0:T(8,128)(2,1)} custom-call(bf16[128,3072]{1,0:T(8,128)(2,1)} %get-tuple-element.6.q_ref, bf16[128,3072]{1,0:T(8,128)(2,1)} %get-tuple-element.7.k_ref, bf16[128,3072]{1,0:T(8,128)(2,1)} %get-tuple-element.5.v_ref), custom_call_target="tpu_custom_call" | custom-call | tf_op jit(solution)/shard_map/pack/pallas_call | solution.py:40
  9.5 63.3 %all_to_all.15.mine_ref = bf16[16,3,3,64,128]{4,3,2,1,0:T(8,128)(2,1)S(1)} all-to-all(bf16[16,3,3,64,128]{4,3,2,1,0:T(8,128)(2,1)} %pack.1), channel_id=1, replica_groups=mesh['chip'=4,'core'=2,'head'=4] {'head','chip'}, dimensions={0} | all-to-all | bytes 4718592 | tf_op jit(solution)/shard_map/all_to_all | solution.py:166
  72.8 0.0 copy-start.1
  72.8 0.0 copy-start
  72.8 1.3 %slice.26 = bf16[16,3,2,64,128]{4,3,2,1,0:T(8,128)(2,1)} slice(bf16[16,3,3,64,128]{4,3,2,1,0:T(8,128)(2,1)S(1)} %all_to_all.15.mine_ref), slice={[0:16], [0:3], [1:3], [0:64], [0:128]} | slice | bytes 3145728 | tf_op jit(solution)/shard_map/slice | solution.py:167
  74.1 0.0 collective-permute-start
  74.1 0.0 copy-done.1
  74.1 0.1 concatenate.12
  74.2 0.2 copy.22
  74.4 0.0 copy-done
  74.4 0.1 copy.21
  74.5 0.7 pad_add_fusion
  75.2 3.3 %all-to-all-start = ((s32[4,3,4,9]{3,2,1,0:T(4,128)}), s32[4,3,4,9]{3,2,1,0:T(4,128)S(1)}, u32[]{:S(2)}, u32[]{:S(2)}) async-start(s32[4,3,4,9]{3,2,1,0:T(4,128)} %pad_add_fusion), calls=%async_computation | async-start | bytes 49152 | tf_op jit(solution)/shard_map/all_to_all | solution.py:147
  78.5 4.7 %all-to-all-done = s32[4,3,4,9]{3,2,1,0:T(4,128)S(1)} async-done(((s32[4,3,4,9]{3,2,1,0:T(4,128)}), s32[4,3,4,9]{3,2,1,0:T(4,128)S(1)}, u32[]{:S(2)}, u32[]{:S(2)}) %all-to-all-start) | async-done | bytes 1760 | tf_op jit(solution)/shard_map/all_to_all | solution.py:147
  83.2 0.1 fusion.3
  83.3 0.1 pad_add_fusion.1
  83.3 0.1 reshape.42.slots_ref
  83.5 0.2 slice_reduce_fusion.counts_ref
  83.6 0.0 collective-permute-done.other_ref
  83.7 12.6 %attend.1 = bf16[16,3,64,128]{3,2,1,0:T(8,128)(2,1)S(1)} custom-call(s32[432]{0:T(512)S(1)} %reshape.42.slots_ref, s32[48]{0:T(128)S(1)} %slice_reduce_fusion.counts_ref, bf16[16,3,3,64,128]{4,3,2,1,0:T(8,128)(2,1)S(1)} %all_to_all.15.mine_ref, bf16[16,3,2,64,128]{4,3,2,1,0:T(8,128)(2,1)} %collective-permute-done.other_ref), custom_call_target="tpu_custom_call" | custom-call | tf_op jit(solution)/shard_map/attend/pallas_call | solution.py:118
  96.2 23.2 %all_to_all.16 = bf16[16,3,64,128]{3,2,1,0:T(8,128)(2,1)S(1)} all-to-all(bf16[16,3,64,128]{3,2,1,0:T(8,128)(2,1)S(1)} %attend.1), channel_id=1, replica_groups=mesh['chip'=4,'core'=2,'head'=4] {'head','chip'}, dimensions={0} | all-to-all | bytes 1572864 | tf_op jit(solution)/shard_map/all_to_all | solution.py:169
  119.4 1.2 copy.24
  (2 shorter events, 0.0 us)
Async XLA Ops:
  72.8 1.3 %copy-start.1 = (s32[12,4]{0,1:T(4,128)S(1)}, s32[12,4]{0,1:T(4,128)}, u32[]{:S(2)}) copy-start(s32[12,4]{0,1:T(4,128)} %param.5) | copy-start | bytes 580
  72.8 1.6 %copy-start = (s32[12,4,8]{0,2,1:T(8,128)S(1)}, s32[12,4,8]{0,2,1:T(8,128)}, u32[]{:S(2)}) copy-start(s32[12,4,8]{0,2,1:T(8,128)} %param.4) | copy-start | bytes 4612
  74.1 9.5 %collective-permute-start = (bf16[16,3,2,64,128]{4,3,2,1,0:T(8,128)(2,1)}, bf16[16,3,2,64,128]{4,3,2,1,0:T(8,128)(2,1)}, u32[]{:S(2)}, u32[]{:S(2)}) collective-permute-start(bf16[16,3,2,64,128]{4,3,2,1,0:T(8,128)(2,1)} %slice.26), channel_id=1, source_target_pairs={{0,4},{4,0},{1,5},{5,1},{2,6},{6,2},{3,7},{7,3},{8,12},{12,8},{9,1... | collective-permute-start | bytes 4718600 | tf_op jit(solution)/shard_map/ppermute | solution.py:167
  75.2 8.0 %all-to-all-start = ((s32[4,3,4,9]{3,2,1,0:T(4,128)}), s32[4,3,4,9]{3,2,1,0:T(4,128)S(1)}, u32[]{:S(2)}, u32[]{:S(2)}) async-start(s32[4,3,4,9]{3,2,1,0:T(4,128)} %pad_add_fusion), calls=%async_computation | async-start | bytes 49152 | tf_op jit(solution)/shard_map/all_to_all | solution.py:147

commit v3 on v2

--- a/solution.py
+++ b/solution.py
@@ -16,60 +16,110 @@
 SUM_ROWS = 16
 
 
-def pack_kernel(q_ref, k_ref, v_ref, out_ref, *, per_chip, head_size):
+def head_of(natural, j, chips_seq, per_chip):
+    z, p = divmod(natural, chips_seq)
+    paired = per_chip // 2 * 2
+    group = z * chips_seq * per_chip
+    if j < paired:
+        return group + p * paired + j
+    return group + chips_seq * paired + p
+
+
+def pack_kernel(
+    me_ref, q_ref, k_ref, v_ref, *rest, single, paired, chips_seq, head_count, per_chip
+):
+    apart, own, joined = rest[:head_count], rest[head_count], rest[head_count + 1 : -2]
+    held_one, held = rest[-2:]
     tokens = q_ref.shape[0]
-    half = tokens // 2
-    lanes = 2 * head_size
-    for pair in range(q_ref.shape[1] // lanes):
-        cols = slice(pair * lanes, (pair + 1) * lanes)
+    head_size = held.shape[-2]
+    half, lanes = tokens // 2, 2 * head_size
+    places = {}
+    for natural in range(chips_seq * head_count):
+        for to, heads in ((held_one, single), (held, paired)):
+            for at, j in enumerate(heads):
+                tile, odd = divmod(head_of(natural, j, chips_seq, per_chip), 2)
+                places.setdefault(tile, []).append((natural, to, at, odd))
+    for tile, users in places.items():
+        cols = slice(tile * lanes, (tile + 1) * lanes)
         q_t = q_ref[:, cols].T
         v_t = v_ref[:, cols].T
         k_tile = k_ref[:, cols]
-        for odd in range(2):
-            chip, j = divmod(2 * pair + odd, per_chip)
+        for natural, to, at, odd in users:
             part = slice(odd * head_size, (odd + 1) * head_size)
-            out_ref[chip, j, 0] = q_t[part]
-            out_ref[chip, j, 1] = jnp.concatenate([k_tile[:half, part], k_tile[half:, part]], axis=1)
-            out_ref[chip, j, 2] = v_t[part]
-
-
-def pack(queries, keys, values, *, chips, per_chip, head_size):
+            z, p = divmod(natural, chips_seq)
+            to = to.at[p, z ^ me_ref[0], at]
+            to[0] = jnp.concatenate([k_tile[:half, part], k_tile[half:, part]], axis=1)
+            to[1] = v_t[part]
+            to[2] = q_t[part]
+    for kz in range(head_count):
+        apart[kz][...] = held_one[:, kz]
+    own[...] = held[:, 0]
+    for kp in range(chips_seq):
+        joined[kp][...] = held[me_ref[1] ^ kp, 1:]
+
+
+def pack(me, queries, keys, values, *, chips_seq, head_count, per_chip, head_size):
     tokens, width = queries.shape
-    steps = 8
-    spec = pl.BlockSpec((tokens, width // steps), lambda i: (0, i))
+    whole = pl.BlockSpec((tokens, width), lambda i, me: (0, 0))
+    single, paired = (per_chip - 1,), tuple(range(per_chip - 1))
+    part = (3, head_size, tokens)
+    shapes = [(chips_seq, 1, *part)] * head_count
+    shapes.append((chips_seq, len(paired), *part))
+    shapes += [(head_count - 1, len(paired), *part)] * chips_seq
     return pl.pallas_call(
-        functools.partial(pack_kernel, per_chip=per_chip, head_size=head_size),
-        grid=(steps,),
-        in_specs=[spec] * 3,
-        out_specs=pl.BlockSpec(
-            (chips // steps, per_chip, 3, head_size, tokens), lambda i: (i, 0, 0, 0, 0)
+        functools.partial(
+            pack_kernel,
+            single=single, paired=paired,
+            chips_seq=chips_seq, head_count=head_count, per_chip=per_chip,
         ),
-        out_shape=jax.ShapeDtypeStruct((chips, per_chip, 3, head_size, tokens), queries.dtype),
+        grid_spec=pltpu.PrefetchScalarGridSpec(
+            num_scalar_prefetch=1,
+            grid=(1,),
+            in_specs=[whole] * 3,
+            out_specs=[pl.BlockSpec(s, lambda i, me, n=len(s): (0,) * n) for s in shapes],
+            scratch_shapes=[
+                pltpu.VMEM((chips_seq, head_count, len(heads), *part), queries.dtype)
+                for heads in (single, paired)
+            ],
+        ),
+        out_shape=[jax.ShapeDtypeStruct(s, queries.dtype) for s in shapes],
+        compiler_params=pltpu.CompilerParams(vmem_limit_bytes=48 << 20),
         name="pack",
-    )(queries, keys, values)
-
-
-def attend_kernel(slots_ref, counts_ref, mine_ref, other_ref, out_ref, kv, *, scale, list_most):
-    blocks, _, _, head_size, tokens = mine_ref.shape
-    head = pl.program_id(0)
-    for b in range(blocks):
-        kv[b] = mine_ref[b, 0, 1:3]
-        kv[blocks + b] = other_ref[b, 0]
-    entries = 1 + list_most
+    )(me, queries, keys, values)
+
+
+def attend_kernel(
+    me_ref, table_ref, *rest, scale, entries, chips_seq, head_count, per_chip, j, near
+):
+    mine, other = rest[:head_count], rest[head_count : 2 * head_count]
+    out_ref, q, kv = rest[-3:]
+    blocks, head_size, tokens = q.shape
+    paired = per_chip // 2 * 2
+    head = me_ref[1] * paired + j if j < paired else chips_seq * paired + me_ref[1]
+    head = head + pl.program_id(0)
+    for kz in range(head_count):
+        for p in range(chips_seq):
+            natural = (me_ref[0] ^ kz) * chips_seq + (p ^ me_ref[1] if near and kz else p)
+            q[natural] = mine[kz][p, 0, 2]
+            kv[natural] = mine[kz][p, 0, :2]
+            kv[blocks + natural] = other[kz][p, 0]
     ones = jnp.ones((SUM_ROWS, tokens), jnp.bfloat16)
     zeros = jnp.zeros((head_size, tokens), jnp.bfloat16)
+
+    def row_of(base, r):
+        return r % chips_seq, base // chips_seq + r // chips_seq
 
     def rows_of(base, counts, seen):
         scores, values = [], []
         for r in range(ROWS):
-            row = (head * blocks + base + r) * entries
-            own = slots_ref[row]
-            q_t = mine_ref[base + r, 0, 0]
+            p, z = row_of(base, r)
+            own = base + r
+            q_t = q[own]
             both = [jnp.concatenate([q_t, zeros], axis=1), jnp.concatenate([zeros, q_t], axis=1)]
             keys, vals = [kv[own, 0]], [jnp.concatenate([kv[own, 1], ones], axis=0)]
             for e in range(1, seen):
                 live = e <= counts[r]
-                slot = jnp.where(live, slots_ref[row + e], own)
+                slot = jnp.where(live, table_ref[p, head, z, e - 1], own)
                 factor = jnp.where(live, 1.0, 0.0).astype(jnp.bfloat16)
                 keys.append(kv[slot, 0])
                 vals.append(jnp.concatenate([kv[slot, 1], ones], axis=0) * factor)
@@ -100,7 +150,10 @@
 
     def group(g, carry):
         base = g * ROWS
-        counts = [counts_ref[head * blocks + base + r] for r in range(ROWS)]
+        counts = []
+        for r in range(ROWS):
+            p, z = row_of(base, r)
+            counts.append(table_ref[p, head, z, entries - 1])
         seen = 1 + functools.reduce(jnp.maximum, counts)
         below = 0
         for size in (*range(3, entries, 2), entries):
@@ -113,26 +166,55 @@
     lax.fori_loop(0, blocks // ROWS, group, 0)
 
 
-def attend(slots, counts, mine, other, *, list_most):
-    blocks, per_chip, _, head_size, tokens = mine.shape
+def attend(
+    me, table, mine, other, held, *, entries, j, near, per_chip, chips_seq, head_count
+):
+    blocks = chips_seq * head_count
+    block = mine[0][0].shape[-2:]
+    head_size, tokens = block
+
+    def spec(at, parts):
+        return pl.BlockSpec((chips_seq, 1, parts, *block), lambda i, *_: (0, at + i, 0, 0, 0))
+
+    in_specs = [spec(at, 3) for _, at in mine] + [spec(at, 2) for _, at in other]
+    operands = [me, table] + [array for array, _ in mine + other]
+    dtype = mine[0][0].dtype
+    aliases = {}
+    if held is not None:
+        in_specs.append(pl.BlockSpec(memory_space=pl.ANY))
+        aliases = {len(operands): 0}
+        operands.append(held)
     return pl.pallas_call(
         functools.partial(
-            attend_kernel, scale=LOG2E / math.sqrt(head_size), list_most=list_most
+            attend_kernel,
+            scale=LOG2E / math.sqrt(head_size), entries=entries,
+            chips_seq=chips_seq, head_count=head_count, per_chip=per_chip, j=j, near=near,
         ),
         grid_spec=pltpu.PrefetchScalarGridSpec(
             num_scalar_prefetch=2,
-            grid=(per_chip,),
-            in_specs=[
-                pl.BlockSpec((blocks, 1, 3, head_size, tokens), lambda j, s, c: (0, j, 0, 0, 0)),
-                pl.BlockSpec((blocks, 1, 2, head_size, tokens), lambda j, s, c: (0, j, 0, 0, 0)),
+            grid=(mine[-1][0].shape[1] - mine[-1][1],) if near else (1,),
+            in_specs=in_specs,
+            out_specs=pl.BlockSpec((blocks, 1, *block), lambda i, *_: (0, j + i, 0, 0)),
+            scratch_shapes=[
+                pltpu.VMEM((blocks, *block), dtype),
+                pltpu.VMEM((2 * blocks, 2, *block), dtype),
             ],
-            out_specs=pl.BlockSpec((blocks, 1, head_size, tokens), lambda j, s, c: (0, j, 0, 0)),
-            scratch_shapes=[pltpu.VMEM((2 * blocks, 2, head_size, tokens), jnp.bfloat16)],
         ),
-        out_shape=jax.ShapeDtypeStruct((blocks, per_chip, head_size, tokens), mine.dtype),
+        out_shape=jax.ShapeDtypeStruct((blocks, per_chip, *block), dtype),
+        input_output_aliases=aliases,
         compiler_params=pltpu.CompilerParams(vmem_limit_bytes=48 << 20),
+        cost_estimate=pl.CostEstimate(flops=1, transcendentals=1, bytes_accessed=1),
         name="attend",
-    )(slots, counts, mine, other)
+    )(*operands)
+
+
+def sync(*values):
+    return lax.optimization_barrier(values)
+
+
+def swap(value, axis, k):
+    size = lax.axis_size(axis)
+    return lax.ppermute(value, axis, [(i, i ^ k) for i in range(size)])
 
 
 def on_pair(projected, key_lists, list_counts, *, chips_seq, head_count):
@@ -141,32 +223,79 @@
     chips = chips_seq * head_count
     head_size = width // (heads_dev * head_count)
     per_chip = heads_dev // chips_seq
+    entries = 1 + list_most
     core = lax.axis_index("core")
-
-    table = jnp.concatenate([key_lists, list_counts[:, :, None]], axis=2)
-    table = lax.all_to_all(
-        table.reshape(chips_seq, per_chip, blocks_dev, list_most + 1),
-        "chip", split_axis=0, concat_axis=0, tiled=True,
-    )
-    table = table.transpose(1, 2, 0, 3).reshape(per_chip * chips, list_most + 1)
-    listed, counts = table[:, :list_most], table[:, list_most]
-    shard = listed // blocks_dev
+    me = jnp.stack([lax.axis_index("head"), lax.axis_index("chip")]).astype(jnp.int32)
+
+    shard = key_lists // blocks_dev
     slots = (
         ((shard % PAIR) != core).astype(jnp.int32) * chips
-        + (listed % blocks_dev) * chips_seq
+        + (key_lists % blocks_dev) * chips_seq
         + shard // PAIR
     )
-    own = jnp.arange(per_chip * chips, dtype=jnp.int32)[:, None] % chips
-    slots = jnp.concatenate([own, slots], axis=1).reshape(-1)
-
-    packed = pack(
-        projected[:, 0], projected[:, 1], projected[:, 2],
-        chips=chips, per_chip=per_chip, head_size=head_size,
-    )
-    mine = lax.all_to_all(packed, ("head", "chip"), split_axis=0, concat_axis=0, tiled=True)
-    other = lax.ppermute(mine[:, :, 1:], "core", [(0, 1), (1, 0)])
-    attended = attend(slots, counts, mine, other, list_most=list_most)
-    back = lax.all_to_all(attended, ("head", "chip"), split_axis=0, concat_axis=0, tiled=True)
+    table = jnp.concatenate([slots, list_counts[:, :, None]], axis=2)
+
+    qkv = projected[:, 0], projected[:, 1], projected[:, 2]
+    sizes = dict(chips_seq=chips_seq, head_count=head_count, per_chip=per_chip)
+
+    def over(parts, axis, name):
+        with jax.named_scope(name):
+            return [parts[0]] + [swap(parts[k], axis, k) for k in range(1, len(parts))]
+
+    def over_p(value, name):
+        with jax.named_scope(name):
+            return lax.all_to_all(value, "chip", split_axis=0, concat_axis=0, tiled=True)
+
+    def over_cores(value, name):
+        with jax.named_scope(name):
+            return swap(value, "core", 1)
+
+    def heads(c, mine, other, held, table, near):
+        with jax.named_scope(f"heads{c}"):
+            return attend(me, table, mine, other, held, entries=entries, j=c, near=near, **sizes)
+
+    last, each = per_chip - 1, range(head_count)
+    packed = pack(me, *qkv, head_size=head_size, **sizes)
+    packed, table = sync(packed, table)
+    singles, own, pairs = packed[:head_count], packed[head_count], packed[head_count + 1 :]
+    seen = list_counts[0, 0] > 0
+
+    def last_head(singles, own, table):
+        plane = over_p(jnp.concatenate([jnp.stack(singles, axis=1)[:, :, 0], own], axis=1), "plane")
+        other = over_cores(plane, "cores2")
+        held = heads(
+            last, [(plane, kz) for kz in each], [(other, kz) for kz in each], None, table, False
+        )
+        return plane, other, held
+
+    def none(*operands):
+        shapes = jax.eval_shape(last_head, *operands)
+        return jax.tree.map(lambda s: jnp.zeros(s.shape, s.dtype), shapes)
+
+    pairs = over(pairs, "chip", "p01")
+    singles = over(singles, "head", "z2")
+    table = over_p(jnp.broadcast_to(table[None], (chips_seq, *table.shape)), "lists")
+    singles, pairs, table = sync(singles, pairs, table)
+    with jax.named_scope("z01"):
+        rest = [
+            swap(jnp.stack([part[k - 1] for part in pairs]), "head", k)
+            for k in range(1, head_count)
+        ]
+    plane, other, held = lax.cond(seen, last_head, none, singles, own, table)
+    rest, held = sync(rest, held)
+    mine = [(plane, head_count)] + [(part, 0) for part in rest]
+    other = [(other, head_count)] + [(over_cores(part, "cores01"), 0) for part in rest]
+    held = heads(0, mine, other, held, table, True)
+    back = lax.all_to_all(held, ("head", "chip"), split_axis=0, concat_axis=0, tiled=True)
+    back = back.reshape(head_count, chips_seq, per_chip, head_size, tokens)
+    paired = per_chip // 2 * 2
+    back = jnp.concatenate(
+        [
+            back[:, :, :paired].reshape(head_count, chips_seq * paired, head_size, tokens),
+            back[:, :, paired:].reshape(head_count, -1, head_size, tokens),
+        ],
+        axis=1,
+    )
     return back.reshape(width, tokens).T
 
 
@@ -260,7 +389,10 @@
     chips = chips_seq * head_count
     group_heads = key_lists.shape[0] // head_count
     one_block = key_lists.shape[1] == seq_count * head_count
-    return one_block and group_heads % chips_seq == 0 and chips % 8 == 0 and chips % ROWS == 0
+    powers = all(n & (n - 1) == 0 for n in (chips_seq, head_count))
+    if not (one_block and powers and group_heads % chips_seq == 0 and chips % ROWS == 0):
+        return False
+    return (group_heads // chips_seq) % 2 == 1 and chips_seq % 2 == 0 and ROWS % chips_seq == 0
 
 
 def solution(mesh):

time: 122 us -> 105 us (0.86); the launches traced: 121 us -> 105 us
  blocking collectives: 86.5 us -> 53.3 us
  starting transfers between devices: 3.26 us -> 18.1 us
  Pallas kernels: 19 us -> 16.9 us
  other arithmetic: 0.84 us -> 2.72 us
  waiting for transfers between devices: 4.69 us -> 6.52 us
    all_to_all x2 -> x3, blocking collectives: 86.5 us -> 53.3 us  [the longest x1 27.3 us: on_pair(): lax.all_to_all(held, ('head', 'chip'), split_axis=0, concat_axis=0, tiled...]
    ppermute x1 -> x13, starting transfers between devices: 0.01 us -> 18.1 us  [swap(): return lax.ppermute(value, axis, [(i, i ^ k) for i in range(size)])]
    ppermute x1 -> x13, waiting for transfers between devices: 0.01 us -> 6.52 us  [swap(): return lax.ppermute(value, axis, [(i, i ^ k) for i in range(size)])]
    all_to_all x1 -> x0, waiting for transfers between devices: 4.68 us -> none  [on_pair(): lax.all_to_all(table.reshape(chips_seq, per_chip, blocks_dev, list_most +...]
    pallas_call x1, Pallas kernels: 6.44 us -> 2.27 us  [pack(): pl.pallas_call(functools.partial(pack_kernel, single=single, paired=paire...]
    all_to_all x1 -> x0, starting transfers between devices: 3.26 us -> none  [on_pair(): lax.all_to_all(table.reshape(chips_seq, per_chip, blocks_dev, list_most +...]
    pallas_call x1 -> x2, Pallas kernels: 12.6 us -> 14.7 us  [attend(): pl.pallas_call(functools.partial(attend_kernel, scale=LOG2E / math.sqrt(h...]
    another operation x0 -> x4, other arithmetic: none -> 1.73 us  [the longest x3 1.65 us: on_pair(): jnp.stack([part[k - 1] for part in pairs])]
  transfers between devices with their start and end apart: 2 -> 13, of which waited for: 1 -> 5; matrix products, arithmetic and copies ran while one was open for 1% -> 3% of each run, Pallas kernels for 0% -> 6%
where the time goes in v3:
time: 105 us
  blocking collectives  53.3 us (51%)
  starting transfers between devices  18.1 us (17%)
  Pallas kernels  16.9 us (16%)
  waiting for transfers between devices  6.52 us (6%)
  local copies, waits for them, and re-layouts  6.19 us (6%)
  other arithmetic  2.72 us (3%)
    all_to_all x1, blocking collectives, on_pair(): lax.all_to_all(held, ('head', 'chip'), split_axis=0, concat_axis=0, tiled...  27.3 us
    all_to_all x2, blocking collectives, over_p(): lax.all_to_all(value, 'chip', split_axis=0, concat_axis=0, tiled=True)  26 us
    ppermute x13, starting transfers between devices, swap(): return lax.ppermute(value, axis, [(i, i ^ k) for i in range(size)])  18.1 us
    pallas_call x2, Pallas kernels, attend(): pl.pallas_call(functools.partial(attend_kernel, scale=LOG2E / math.sqrt(h...  14.7 us
    ppermute x13, waiting for transfers between devices, swap(): return lax.ppermute(value, axis, [(i, i ^ k) for i in range(size)])  6.52 us
    pallas_call x1, Pallas kernels, pack(): pl.pallas_call(functools.partial(pack_kernel, single=single, paired=paire...  2.27 us
  transfers between devices with their start and end apart: 13, of which 5 were waited for; matrix products, arithmetic and copies ran while one was open for 3% of the time, Pallas kernels for 6%

profile of v3, /device:TPU:0, one launch (start us, length us, event | category | flops | bytes accessed | tf_op | source)
XLA Modules:
  0.0 104.9 jit_solution(10904993700467351938)
XLA Ops:
  0.0 1.8 %slice_bitcast_fusion = (bf16[128,3072]{1,0:T(8,128)(2,1)S(1)}, bf16[128,3072]{1,0:T(8,128)(2,1)S(1)}, bf16[128,3072]{1,0:T(8,128)(2,1)S(1)}) fusion(bf16[128,3,3072]{2,0,1:T(8,128)(2,1)} %param.5), kind=kLoop, calls=%fused_computation.3 | loop fusion | bytes 4718592 | tf_op jit(solution)/shard_map/squeeze | solution.py:238
  1.8 0.1 pad_add_fusion.1.me_ref
  1.9 2.3 %pack.1 = (bf16[4,1,3,64,128]{4,3,2,1,0:T(8,128)(2,1)}, bf16[4,1,3,64,128]{4,3,2,1,0:T(8,128)(2,1)S(1)}, bf16[4,1,3,64,128]{4,3,2,1,0:T(8,128)(2,1)}, bf16[4,1,3...) custom-call(s32[2]{0:T(128)S(1)} %pad_add_fusion.1.me_ref, ...), custom_call_target="tpu_custom_call" | custom-call | tf_op jit(solution)/shard_map/pack/pallas_call | solution.py:69
  4.2 3.0 %collective-permute-start.1 = (bf16[4,1,3,64,128]{4,3,2,1,0:T(8,128)(2,1)S(1)}, bf16[4,1,3,64,128]{4,3,2,1,0:T(8,128)(2,1)S(1)}, u32[]{:S(2)}, u32[]{:S(2)}) collective-permute-start(bf16[4,1,3,64,128]{4,3,2,1,0:T(8,128)(2,1)S(1)} %get-tuple-element.71), channel_id=1, source_target_pairs={{0,1},{1,0},{2,3},{3,2},{4,5},{5,4},{6,7},{7,6},{8,9},{9,8},{10,11... | collective-permute-start | bytes 589832 | tf_op jit(solution)/shard_map/z2/ppermute | solution.py:217
  7.2 1.5 %collective-permute-start.4 = (bf16[3,2,3,64,128]{4,3,2,1,0:T(8,128)(2,1)S(1)}, bf16[3,2,3,64,128]{4,3,2,1,0:T(8,128)(2,1)S(1)}, u32[]{:S(2)}, u32[]{:S(2)}) collective-permute-start(bf16[3,2,3,64,128]{4,3,2,1,0:T(8,128)(2,1)S(1)} %get-tuple-element.75), channel_id=1, source_target_pairs={{0,8},{8,0},{16,24},{24,16},{1,9},{9,1},{17,25},{25,17},{2,10},{10... | collective-permute-start | bytes 884744 | tf_op jit(solution)/shard_map/p01/ppermute | solution.py:217
  8.7 1.5 %collective-permute-start.5 = (bf16[3,2,3,64,128]{4,3,2,1,0:T(8,128)(2,1)S(1)}, bf16[3,2,3,64,128]{4,3,2,1,0:T(8,128)(2,1)S(1)}, u32[]{:S(2)}, u32[]{:S(2)}) collective-permute-start(bf16[3,2,3,64,128]{4,3,2,1,0:T(8,128)(2,1)S(1)} %get-tuple-element.76), channel_id=1, source_target_pairs={{0,16},{8,24},{16,0},{24,8},{1,17},{9,25},{17,1},{25,9},{2,18},{10... | collective-permute-start | bytes 884744 | tf_op jit(solution)/shard_map/p01/ppermute | solution.py:217
  10.2 0.5 collective-permute-start.6
  10.7 2.6 %collective-permute-start.2 = (bf16[4,1,3,64,128]{4,3,2,1,0:T(8,128)(2,1)}, bf16[4,1,3,64,128]{4,3,2,1,0:T(8,128)(2,1)S(1)}, u32[]{:S(2)}, u32[]{:S(2)}) collective-permute-start(bf16[4,1,3,64,128]{4,3,2,1,0:T(8,128)(2,1)} %get-tuple-element.72), channel_id=1, source_target_pairs={{0,2},{1,3},{2,0},{3,1},{4,6},{5,7},{6,4},{7,5},{8,10},{9,11},{10,... | collective-permute-start | bytes 589832 | tf_op jit(solution)/shard_map/z2/ppermute | solution.py:217
  13.3 0.0 collective-permute-done.1
  13.3 0.7 copy-done.2
  14.0 3.6 %collective-permute-start.3 = (bf16[4,1,3,64,128]{4,3,2,1,0:T(8,128)(2,1)}, bf16[4,1,3,64,128]{4,3,2,1,0:T(8,128)(2,1)S(1)}, u32[]{:S(2)}, u32[]{:S(2)}) collective-permute-start(bf16[4,1,3,64,128]{4,3,2,1,0:T(8,128)(2,1)} %get-tuple-element.73), channel_id=1, source_target_pairs={{0,3},{1,2},{2,1},{3,0},{4,7},{5,6},{6,5},{7,4},{8,11},{9,10},{10,... | collective-permute-start | bytes 589832 | tf_op jit(solution)/shard_map/z2/ppermute | solution.py:217
  17.7 0.1 reshape.22
  17.8 8.2 %all_to_all.15 = s32[4,1,432]{2,1,0:T(1,128)S(1)} all-to-all(s32[4,1,432]{2,1,0:T(1,128)S(1)} %reshape.22), channel_id=1, replica_groups=mesh['chip'=4,'core'=2,'head'=4] {'chip'}, dimensions={0} | all-to-all | bytes 13824 | tf_op jit(solution)/shard_map/lists/all_to_all | solution.py:247
  26.0 0.5 broadcast.29
  26.5 0.7 reduce
  27.2 0.1 reshape.23
  27.3 0.0 collective-permute-done.3
  27.4 0.0 collective-permute-done.4
  27.4 0.7 copy-done.6
  28.2 0.0 copy-start
  28.2 0.8 pad_maximum_fusion.4
  29.0 2.1 %collective-permute-start.9 = (bf16[4,2,3,64,128]{4,3,2,1,0:T(8,128)(2,1)}, bf16[4,2,3,64,128]{4,3,2,1,0:T(8,128)(2,1)S(1)}, u32[]{:S(2)}, u32[]{:S(2)}) collective-permute-start(bf16[4,2,3,64,128]{4,3,2,1,0:T(8,128)(2,1)} %pad_maximum_fusion.4), channel_id=1, source_target_pairs={{0,3},{1,2},{2,1},{3,0},{4,7},{5,6},{6,5},{7,4},{8,11},{9,10},{10,... | collective-permute-start | bytes 1179656 | tf_op jit(solution)/shard_map/z01/ppermute | solution.py:217
  31.1 0.8 pad_maximum_fusion.3
  31.9 2.5 %collective-permute-start.8 = (bf16[4,2,3,64,128]{4,3,2,1,0:T(8,128)(2,1)}, bf16[4,2,3,64,128]{4,3,2,1,0:T(8,128)(2,1)S(1)}, u32[]{:S(2)}, u32[]{:S(2)}) collective-permute-start(bf16[4,2,3,64,128]{4,3,2,1,0:T(8,128)(2,1)} %pad_maximum_fusion.3), channel_id=1, source_target_pairs={{0,2},{1,3},{2,0},{3,1},{4,6},{5,7},{6,4},{7,5},{8,10},{9,11},{10,... | collective-permute-start | bytes 1179656 | tf_op jit(solution)/shard_map/z01/ppermute | solution.py:217
  34.5 0.1 pad_maximum_fusion.2
  34.5 0.2 collective-permute-start.7
  34.7 0.5 slice.57
  36.0 27.3 %conditional.1 = (bf16[4,6,3,64,128]{4,3,2,1,0:T(8,128)(2,1)}, bf16[4,6,3,64,128]{4,3,2,1,0:T(8,128)(2,1)}, bf16[16,3,64,128]{3,2,1,0:T(8,128)(2,1)S(1)}) conditional(s32[]{:T(128)} %bitcast.20, () %tuple.18, (bf16[4,1,3,64,128]{4,3,2,1,0:T(8,128)(2,1)S(1)}, bf16[4,1,3,64,128]{4,3,2,1,0:T(8,128)(2,1)S(1)}, bf16[4,1,3,64,128]{4,3,2,1,0:T(8,128)(2,1)S(1)}, ...), branch_computations={%region_0.1_spmd, %region_1.2_spmd} | conditional | flops 1769473 | bytes 11023937 | solution.py:284
  36.0 0.1 maximum_bitcast_fusion
  36.1 0.1 pad_maximum_fusion
  36.2 17.8 %all_to_all.14.rest_0_.rest_1_.rest_2_.rest_3_ = bf16[4,6,3,64,128]{4,3,2,1,0:T(8,128)(2,1)} all-to-all(bf16[4,6,3,64,128]{4,3,2,1,0:T(8,128)(2,1)S(1)} %pad_maximum_fusion), channel_id=1, replica_groups=mesh['chip'=4,'core'=2,'head'=4] {'chip'}, dimensions={0} | all-to-all | bytes 2359296 | tf_op jit(solution)/shard_map/cond/branch_1_fun/plane/all_to_all | solution.py:247
  54.0 0.0 collective-permute-start
  54.0 0.2 copy.27.table_ref
  54.2 3.0 %collective-permute-done.rest_4_.rest_5_.rest_6_.rest_7_ = bf16[4,6,3,64,128]{4,3,2,1,0:T(8,128)(2,1)} collective-permute-done((bf16[4,6,3,64,128]{4,3,2,1,0:T(8,128)(2,1)}, bf16[4,6,3,64,128]{4,3,2,1,0:T(8,128)(2,1)}, u32[]{:S(2)}, u32[]{:S(2)}) %collective-permute-start) | collective-permute-done | bytes 1179680 | tf_op jit(solution)/shard_map/cond/branch_1_fun/cores2/ppermute | solution.py:217
  57.2 5.9 %attend.2 = bf16[16,3,64,128]{3,2,1,0:T(8,128)(2,1)S(1)} custom-call(s32[2]{0:T(128)S(1)} %get-tuple-element.24.me_ref, s32[4,12,4,9]{3,2,1,0:T(4,128)S(1)} %copy.27.table_ref, bf16[4,6,3,64,128]{4,3,2,1,0:T(8,128)(2,1)} %all_to_all.14.rest_0_.rest_1_.rest_2_.rest_3_, bf16[4,6,3,64,128]{4,3,2,1,0:T(8,128)(2,1)} %all_to_all.14.rest_0_.rest_1_.rest_2_.rest_3_, ...), custom_call_target="tpu_custom_call" | custom-call | flops 1 | bytes 1 | tf_op jit(solution)/shard_map/cond/branch_1_fun/heads2/attend/pallas_call | solution.py:187
  63.3 0.0 collective-permute-done.9.rest_3_
  63.3 1.4 %collective-permute-done.8.rest_2_ = bf16[4,2,3,64,128]{4,3,2,1,0:T(8,128)(2,1)S(1)} collective-permute-done((bf16[4,2,3,64,128]{4,3,2,1,0:T(8,128)(2,1)}, bf16[4,2,3,64,128]{4,3,2,1,0:T(8,128)(2,1)S(1)}, u32[]{:S(2)}, u32[]{:S(2)}) %collective-permute-start.8) | collective-permute-done | bytes 393248 | tf_op jit(solution)/shard_map/z01/ppermute | solution.py:217
  64.7 0.0 collective-permute-start.10
  64.7 0.5 collective-permute-start.11
  65.2 0.0 collective-permute-start.12
  65.2 0.2 copy.28.table_ref
  65.4 1.0 collective-permute-done.10.rest_5_
  66.4 0.6 collective-permute-done.11.rest_6_
  67.0 0.6 collective-permute-done.12.rest_7_
  67.5 8.7 %attend.3 = bf16[16,3,64,128]{3,2,1,0:T(8,128)(2,1)S(1)} custom-call(s32[2]{0:T(128)S(1)} %pad_add_fusion.1.me_ref, s32[4,12,4,9]{3,2,1,0:T(4,128)S(1)} %copy.28.table_ref, bf16[4,6,3,64,128]{4,3,2,1,0:T(8,128)(2,1)} %get-tuple-element.85.rest_0_, bf16[4,2,3,64,128]{4,3,2,1,0:T(8,128)(2,1)S(1)} %collective-permute-done.7.rest_1_, ...), custom_call_target="tpu_custom_call", output_to_operand_aliasing={{}: (10, {})} | custom-call | flops 1 | bytes 1 | tf_op jit(solution)/shard_map/heads0/attend/pallas_call | solution.py:187
  76.3 27.3 %all_to_all.16 = bf16[16,3,64,128]{3,2,1,0:T(8,128)(2,1)S(1)} all-to-all(bf16[16,3,64,128]{3,2,1,0:T(8,128)(2,1)S(1)} %attend.3), channel_id=1, replica_groups=mesh['chip'=4,'core'=2,'head'=4] {'head','chip'}, dimensions={0} | all-to-all | bytes 1572864 | tf_op jit(solution)/shard_map/all_to_all | solution.py:289
  103.7 0.1 pad_maximum_fusion.1
  103.8 1.2 %copy.30 = bf16[128,3072]{1,0:T(8,128)(2,1)} copy(bf16[128,3072]{0,1:T(8,128)(2,1)S(1)} %bitcast.40) | data formatting | bytes 1572864 | tf_op jit(solution)/shard_map/transpose | solution.py:299
  (29 shorter events, 0.2 us)
Async XLA Ops:
  0.0 1.9 %copy-start.8 = (s32[12,4,8]{0,2,1:T(8,128)S(1)}, s32[12,4,8]{0,2,1:T(8,128)}, u32[]{:S(2)}) copy-start(s32[12,4,8]{0,2,1:T(8,128)} %param.6) | copy-start | bytes 4612
  0.0 1.9 %copy-start.9 = (s32[12,4]{0,1:T(4,128)S(1)}, s32[12,4]{0,1:T(4,128)}, u32[]{:S(2)}) copy-start(s32[12,4]{0,1:T(4,128)} %param.7) | copy-start | bytes 580
  4.2 9.1 %collective-permute-start.1 = (bf16[4,1,3,64,128]{4,3,2,1,0:T(8,128)(2,1)S(1)}, bf16[4,1,3,64,128]{4,3,2,1,0:T(8,128)(2,1)S(1)}, u32[]{:S(2)}, u32[]{:S(2)}) collective-permute-start(bf16[4,1,3,64,128]{4,3,2,1,0:T(8,128)(2,1)S(1)} %get-tuple-element.71), channel_id=1, source_target_pairs={{0,1},{1,0},{2,3},{3,2},{4,5},{5,4},{6,7},{7,6},{8,9},{9,8},{10,11... | collective-permute-start | bytes 589832 | tf_op jit(solution)/shard_map/z2/ppermute | solution.py:217
  7.2 20.1 %collective-permute-start.4 = (bf16[3,2,3,64,128]{4,3,2,1,0:T(8,128)(2,1)S(1)}, bf16[3,2,3,64,128]{4,3,2,1,0:T(8,128)(2,1)S(1)}, u32[]{:S(2)}, u32[]{:S(2)}) collective-permute-start(bf16[3,2,3,64,128]{4,3,2,1,0:T(8,128)(2,1)S(1)} %get-tuple-element.75), channel_id=1, source_target_pairs={{0,8},{8,0},{16,24},{24,16},{1,9},{9,1},{17,25},{25,17},{2,10},{10... | collective-permute-start | bytes 884744 | tf_op jit(solution)/shard_map/p01/ppermute | solution.py:217
  8.7 18.6 %collective-permute-start.5 = (bf16[3,2,3,64,128]{4,3,2,1,0:T(8,128)(2,1)S(1)}, bf16[3,2,3,64,128]{4,3,2,1,0:T(8,128)(2,1)S(1)}, u32[]{:S(2)}, u32[]{:S(2)}) collective-permute-start(bf16[3,2,3,64,128]{4,3,2,1,0:T(8,128)(2,1)S(1)} %get-tuple-element.76), channel_id=1, source_target_pairs={{0,16},{8,24},{16,0},{24,8},{1,17},{9,25},{17,1},{25,9},{2,18},{10... | collective-permute-start | bytes 884744 | tf_op jit(solution)/shard_map/p01/ppermute | solution.py:217
  10.2 17.1 %collective-permute-start.6 = (bf16[3,2,3,64,128]{4,3,2,1,0:T(8,128)(2,1)S(1)}, bf16[3,2,3,64,128]{4,3,2,1,0:T(8,128)(2,1)S(1)}, u32[]{:S(2)}, u32[]{:S(2)}) collective-permute-start(bf16[3,2,3,64,128]{4,3,2,1,0:T(8,128)(2,1)S(1)} %get-tuple-element.77), channel_id=1, source_target_pairs={{0,24},{8,16},{16,8},{24,0},{1,25},{9,17},{17,9},{25,1},{2,26},{10... | collective-permute-start | bytes 884744 | tf_op jit(solution)/shard_map/p01/ppermute | solution.py:217
  10.7 16.6 %collective-permute-start.2 = (bf16[4,1,3,64,128]{4,3,2,1,0:T(8,128)(2,1)}, bf16[4,1,3,64,128]{4,3,2,1,0:T(8,128)(2,1)S(1)}, u32[]{:S(2)}, u32[]{:S(2)}) collective-permute-start(bf16[4,1,3,64,128]{4,3,2,1,0:T(8,128)(2,1)} %get-tuple-element.72), channel_id=1, source_target_pairs={{0,2},{1,3},{2,0},{3,1},{4,6},{5,7},{6,4},{7,5},{8,10},{9,11},{10,... | collective-permute-start | bytes 589832 | tf_op jit(solution)/shard_map/z2/ppermute | solution.py:217
  13.3 0.7 copy-start.2
  14.0 13.3 %collective-permute-start.3 = (bf16[4,1,3,64,128]{4,3,2,1,0:T(8,128)(2,1)}, bf16[4,1,3,64,128]{4,3,2,1,0:T(8,128)(2,1)S(1)}, u32[]{:S(2)}, u32[]{:S(2)}) collective-permute-start(bf16[4,1,3,64,128]{4,3,2,1,0:T(8,128)(2,1)} %get-tuple-element.73), channel_id=1, source_target_pairs={{0,3},{1,2},{2,1},{3,0},{4,7},{5,6},{6,5},{7,4},{8,11},{9,10},{10,... | collective-permute-start | bytes 589832 | tf_op jit(solution)/shard_map/z2/ppermute | solution.py:217
  27.3 0.8 copy-start.4
  27.3 0.7 copy-start.6
  28.2 7.8 %copy-start = (bf16[4,2,3,64,128]{4,3,2,1,0:T(8,128)(2,1)S(1)}, bf16[4,2,3,64,128]{4,3,2,1,0:T(8,128)(2,1)}, u32[]{:S(2)}) copy-start(bf16[4,2,3,64,128]{4,3,2,1,0:T(8,128)(2,1)} %get-tuple-element.84) | copy-start | bytes 1179652
  28.2 7.8 %copy-start.1 = (bf16[4,1,3,64,128]{4,3,2,1,0:T(8,128)(2,1)S(1)}, bf16[4,1,3,64,128]{4,3,2,1,0:T(8,128)(2,1)}, u32[]{:S(2)}) copy-start(bf16[4,1,3,64,128]{4,3,2,1,0:T(8,128)(2,1)} %get-tuple-element.80) | copy-start | bytes 589828
  28.2 7.8 %copy-start.3 = (bf16[4,1,3,64,128]{4,3,2,1,0:T(8,128)(2,1)S(1)}, bf16[4,1,3,64,128]{4,3,2,1,0:T(8,128)(2,1)}, u32[]{:S(2)}) copy-start(bf16[4,1,3,64,128]{4,3,2,1,0:T(8,128)(2,1)} %copy-done.2) | copy-start | bytes 589828
  28.2 7.8 %copy-start.5 = (bf16[4,1,3,64,128]{4,3,2,1,0:T(8,128)(2,1)S(1)}, bf16[4,1,3,64,128]{4,3,2,1,0:T(8,128)(2,1)}, u32[]{:S(2)}) copy-start(bf16[4,1,3,64,128]{4,3,2,1,0:T(8,128)(2,1)} %copy-done.4) | copy-start | bytes 589828
  28.2 7.8 %copy-start.7 = (bf16[4,1,3,64,128]{4,3,2,1,0:T(8,128)(2,1)S(1)}, bf16[4,1,3,64,128]{4,3,2,1,0:T(8,128)(2,1)}, u32[]{:S(2)}) copy-start(bf16[4,1,3,64,128]{4,3,2,1,0:T(8,128)(2,1)} %copy-done.6) | copy-start | bytes 589828
  29.0 34.3 %collective-permute-start.9 = (bf16[4,2,3,64,128]{4,3,2,1,0:T(8,128)(2,1)}, bf16[4,2,3,64,128]{4,3,2,1,0:T(8,128)(2,1)S(1)}, u32[]{:S(2)}, u32[]{:S(2)}) collective-permute-start(bf16[4,2,3,64,128]{4,3,2,1,0:T(8,128)(2,1)} %pad_maximum_fusion.4), channel_id=1, source_target_pairs={{0,3},{1,2},{2,1},{3,0},{4,7},{5,6},{6,5},{7,4},{8,11},{9,10},{10,... | collective-permute-start | bytes 1179656 | tf_op jit(solution)/shard_map/z01/ppermute | solution.py:217
  31.9 32.8 %collective-permute-start.8 = (bf16[4,2,3,64,128]{4,3,2,1,0:T(8,128)(2,1)}, bf16[4,2,3,64,128]{4,3,2,1,0:T(8,128)(2,1)S(1)}, u32[]{:S(2)}, u32[]{:S(2)}) collective-permute-start(bf16[4,2,3,64,128]{4,3,2,1,0:T(8,128)(2,1)} %pad_maximum_fusion.3), channel_id=1, source_target_pairs={{0,2},{1,3},{2,0},{3,1},{4,6},{5,7},{6,4},{7,5},{8,10},{9,11},{10,... | collective-permute-start | bytes 1179656 | tf_op jit(solution)/shard_map/z01/ppermute | solution.py:217
  34.5 30.2 %collective-permute-start.7 = (bf16[4,2,3,64,128]{4,3,2,1,0:T(8,128)(2,1)S(1)}, bf16[4,2,3,64,128]{4,3,2,1,0:T(8,128)(2,1)S(1)}, u32[]{:S(2)}, u32[]{:S(2)}) collective-permute-start(bf16[4,2,3,64,128]{4,3,2,1,0:T(8,128)(2,1)S(1)} %pad_maximum_fusion.2), channel_id=1, source_target_pairs={{0,1},{1,0},{2,3},{3,2},{4,5},{5,4},{6,7},{7,6},{8,9},{9,8},{10,11... | collective-permute-start | bytes 1179656 | tf_op jit(solution)/shard_map/z01/ppermute | solution.py:217
  54.0 3.2 %collective-permute-start = (bf16[4,6,3,64,128]{4,3,2,1,0:T(8,128)(2,1)}, bf16[4,6,3,64,128]{4,3,2,1,0:T(8,128)(2,1)}, u32[]{:S(2)}, u32[]{:S(2)}) collective-permute-start(bf16[4,6,3,64,128]{4,3,2,1,0:T(8,128)(2,1)} %all_to_all.14.rest_0_.rest_1_.rest_2_.rest_3_), channel_id=1, source_target_pairs={{0,4},{4,0},{1,5},{5,1},{2,6},{6,2},{3,7},{7,3},{8,12},{12,8},{9,1... | collective-permute-start | bytes 3538952 | tf_op jit(solution)/shard_map/cond/branch_1_fun/cores2/ppermute | solution.py:217
  64.7 1.7 %collective-permute-start.10 = (bf16[4,2,3,64,128]{4,3,2,1,0:T(8,128)(2,1)S(1)}, bf16[4,2,3,64,128]{4,3,2,1,0:T(8,128)(2,1)S(1)}, u32[]{:S(2)}, u32[]{:S(2)}) collective-permute-start(bf16[4,2,3,64,128]{4,3,2,1,0:T(8,128)(2,1)S(1)} %collective-permute-done.7.rest_1_), channel_id=1, source_target_pairs={{0,4},{4,0},{1,5},{5,1},{2,6},{6,2},{3,7},{7,3},{8,12},{12,8},{9,1... | collective-permute-start | bytes 1179656 | tf_op jit(solution)/shard_map/cores01/ppermute | solution.py:217
  64.7 2.3 %collective-permute-start.11 = (bf16[4,2,3,64,128]{4,3,2,1,0:T(8,128)(2,1)S(1)}, bf16[4,2,3,64,128]{4,3,2,1,0:T(8,128)(2,1)S(1)}, u32[]{:S(2)}, u32[]{:S(2)}) collective-permute-start(bf16[4,2,3,64,128]{4,3,2,1,0:T(8,128)(2,1)S(1)} %collective-permute-done.8.rest_2_), channel_id=1, source_target_pairs={{0,4},{4,0},{1,5},{5,1},{2,6},{6,2},{3,7},{7,3},{8,12},{12,8},{9,1... | collective-permute-start | bytes 1179656 | tf_op jit(solution)/shard_map/cores01/ppermute | solution.py:217
  65.2 2.3 %collective-permute-start.12 = (bf16[4,2,3,64,128]{4,3,2,1,0:T(8,128)(2,1)S(1)}, bf16[4,2,3,64,128]{4,3,2,1,0:T(8,128)(2,1)S(1)}, u32[]{:S(2)}, u32[]{:S(2)}) collective-permute-start(bf16[4,2,3,64,128]{4,3,2,1,0:T(8,128)(2,1)S(1)} %collective-permute-done.9.rest_3_), channel_id=1, source_target_pairs={{0,4},{4,0},{1,5},{5,1},{2,6},{6,2},{3,7},{7,3},{8,12},{12,8},{9,1... | collective-permute-start | bytes 1179656 | tf_op jit(solution)/shard_map/cores01/ppermute | solution.py:217

commit v4 on v3

--- a/solution.py
+++ b/solution.py
@@ -26,10 +26,12 @@
 
 
 def pack_kernel(
-    me_ref, q_ref, k_ref, v_ref, *rest, single, paired, chips_seq, head_count, per_chip
+    me_ref, q_ref, k_ref, v_ref, lists_ref, used_ref, *rest,
+    single, paired, chips_seq, head_count, per_chip
 ):
-    apart, own, joined = rest[:head_count], rest[head_count], rest[head_count + 1 : -2]
-    held_one, held = rest[-2:]
+    apart, own, joined = rest[:head_count], rest[head_count], rest[head_count + 1 : -3]
+    held_one, held, table = rest[-3:]
+    table[...] = jnp.zeros_like(table)
     tokens = q_ref.shape[0]
     head_size = held.shape[-2]
     half, lanes = tokens // 2, 2 * head_size
@@ -52,20 +54,40 @@
             to[1] = v_t[part]
             to[2] = q_t[part]
     for kz in range(head_count):
-        apart[kz][...] = held_one[:, kz]
+        apart[-1 - kz][...] = held_one[:, kz]
     own[...] = held[:, 0]
     for kp in range(chips_seq):
-        joined[kp][...] = held[me_ref[1] ^ kp, 1:]
-
-
-def pack(me, queries, keys, values, *, chips_seq, head_count, per_chip, head_size):
+        p, many = me_ref[1] ^ kp, len(paired)
+        for at, head in enumerate([p * many + j for j in paired] + [chips_seq * many + p]):
+            listed = lists_ref[head]
+            shard = listed // head_count
+            slots = (shard % PAIR != me_ref[2]).astype(jnp.int32) * (chips_seq * head_count)
+            slots += listed % head_count * chips_seq + shard // PAIR
+            table[at * head_count : (at + 1) * head_count, : listed.shape[1]] = slots.astype(
+                jnp.float32
+            )
+            table[pl.ds(per_chip * head_count + at, 1), :head_count] = used_ref[
+                pl.ds(head, 1)
+            ].astype(jnp.float32)
+        lists = table[...].astype(joined[kp].dtype)
+        rows = joined[kp].shape[0] - lists.shape[0]
+        joined[kp][:rows] = held[me_ref[1] ^ kp, 1:].reshape(rows, tokens)
+        joined[kp][rows:] = lists
+
+
+def list_rows(per_chip, head_count):
+    return pl.cdiv(per_chip * (head_count + 1), 16) * 16
+
+
+def pack(me, queries, keys, values, lists, used, *, chips_seq, head_count, per_chip, head_size):
     tokens, width = queries.shape
     whole = pl.BlockSpec((tokens, width), lambda i, me: (0, 0))
     single, paired = (per_chip - 1,), tuple(range(per_chip - 1))
     part = (3, head_size, tokens)
     shapes = [(chips_seq, 1, *part)] * head_count
     shapes.append((chips_seq, len(paired), *part))
-    shapes += [(head_count - 1, len(paired), *part)] * chips_seq
+    rows = (head_count - 1) * len(paired) * math.prod(part[:-1]) + list_rows(per_chip, head_count)
+    shapes += [(rows, tokens)] * chips_seq
     return pl.pallas_call(
         functools.partial(
             pack_kernel,
@@ -75,17 +97,22 @@
         grid_spec=pltpu.PrefetchScalarGridSpec(
             num_scalar_prefetch=1,
             grid=(1,),
-            in_specs=[whole] * 3,
+            in_specs=[
+                *[whole] * 3,
+                pl.BlockSpec(lists.shape, lambda i, me: (0, 0, 0)),
+                pl.BlockSpec(used.shape, lambda i, me: (0, 0)),
+            ],
             out_specs=[pl.BlockSpec(s, lambda i, me, n=len(s): (0,) * n) for s in shapes],
             scratch_shapes=[
                 pltpu.VMEM((chips_seq, head_count, len(heads), *part), queries.dtype)
                 for heads in (single, paired)
-            ],
+            ]
+            + [pltpu.VMEM((list_rows(per_chip, head_count), tokens), jnp.float32)],
         ),
         out_shape=[jax.ShapeDtypeStruct(s, queries.dtype) for s in shapes],
         compiler_params=pltpu.CompilerParams(vmem_limit_bytes=48 << 20),
         name="pack",
-    )(me, queries, keys, values)
+    )(me, queries, keys, values, lists, used)
 
 
 def attend_kernel(
@@ -94,9 +121,9 @@
     mine, other = rest[:head_count], rest[head_count : 2 * head_count]
     out_ref, q, kv = rest[-3:]
     blocks, head_size, tokens = q.shape
-    paired = per_chip // 2 * 2
-    head = me_ref[1] * paired + j if j < paired else chips_seq * paired + me_ref[1]
-    head = head + pl.program_id(0)
+    head = j + pl.program_id(0)
+    counted = per_chip * head_count + head
+    head = head * head_count
     for kz in range(head_count):
         for p in range(chips_seq):
             natural = (me_ref[0] ^ kz) * chips_seq + (p ^ me_ref[1] if near and kz else p)
@@ -107,7 +134,7 @@
     zeros = jnp.zeros((head_size, tokens), jnp.bfloat16)
 
     def row_of(base, r):
-        return r % chips_seq, base // chips_seq + r // chips_seq
+        return r % chips_seq ^ me_ref[1], base // chips_seq + r // chips_seq
 
     def rows_of(base, counts, seen):
         scores, values = [], []
@@ -119,7 +146,7 @@
             keys, vals = [kv[own, 0]], [jnp.concatenate([kv[own, 1], ones], axis=0)]
             for e in range(1, seen):
                 live = e <= counts[r]
-                slot = jnp.where(live, table_ref[p, head, z, e - 1], own)
+                slot = jnp.where(live, table_ref[p, head + z, e - 1], own)
                 factor = jnp.where(live, 1.0, 0.0).astype(jnp.bfloat16)
                 keys.append(kv[slot, 0])
                 vals.append(jnp.concatenate([kv[slot, 1], ones], axis=0) * factor)
@@ -153,7 +180,7 @@
         counts = []
         for r in range(ROWS):
             p, z = row_of(base, r)
-            counts.append(table_ref[p, head, z, entries - 1])
+            counts.append(table_ref[p, counted, z])
         seen = 1 + functools.reduce(jnp.maximum, counts)
         below = 0
         for size in (*range(3, entries, 2), entries):
@@ -220,27 +247,17 @@
 def on_pair(projected, key_lists, list_counts, *, chips_seq, head_count):
     tokens, _, width = projected.shape
     heads_dev, blocks_dev, list_most = key_lists.shape
-    chips = chips_seq * head_count
     head_size = width // (heads_dev * head_count)
     per_chip = heads_dev // chips_seq
     entries = 1 + list_most
-    core = lax.axis_index("core")
-    me = jnp.stack([lax.axis_index("head"), lax.axis_index("chip")]).astype(jnp.int32)
-
-    shard = key_lists // blocks_dev
-    slots = (
-        ((shard % PAIR) != core).astype(jnp.int32) * chips
-        + (key_lists % blocks_dev) * chips_seq
-        + shard // PAIR
-    )
-    table = jnp.concatenate([slots, list_counts[:, :, None]], axis=2)
+    me = jnp.stack([lax.axis_index(a) for a in ("head", "chip", "core")]).astype(jnp.int32)
 
     qkv = projected[:, 0], projected[:, 1], projected[:, 2]
     sizes = dict(chips_seq=chips_seq, head_count=head_count, per_chip=per_chip)
 
     def over(parts, axis, name):
         with jax.named_scope(name):
-            return [parts[0]] + [swap(parts[k], axis, k) for k in range(1, len(parts))]
+            return [parts[0]] + [swap(parts[k], axis, k) for k in reversed(range(1, len(parts)))][::-1]
 
     def over_p(value, name):
         with jax.named_scope(name):
@@ -255,9 +272,8 @@
             return attend(me, table, mine, other, held, entries=entries, j=c, near=near, **sizes)
 
     last, each = per_chip - 1, range(head_count)
-    packed = pack(me, *qkv, head_size=head_size, **sizes)
-    packed, table = sync(packed, table)
-    singles, own, pairs = packed[:head_count], packed[head_count], packed[head_count + 1 :]
+    packed = pack(me, *qkv, key_lists, list_counts, head_size=head_size, **sizes)
+    singles, own, pairs = packed[head_count - 1 :: -1], packed[head_count], packed[head_count + 1 :]
     seen = list_counts[0, 0] > 0
 
     def last_head(singles, own, table):
@@ -274,15 +290,18 @@
 
     pairs = over(pairs, "chip", "p01")
     singles = over(singles, "head", "z2")
-    table = over_p(jnp.broadcast_to(table[None], (chips_seq, *table.shape)), "lists")
-    singles, pairs, table = sync(singles, pairs, table)
+    rows = pairs[0].shape[0] - list_rows(per_chip, head_count)
+    table = jnp.stack([part[rows:, :entries] for part in pairs]).astype(jnp.int32)
+    shape = (head_count - 1, per_chip - 1, 3, head_size, tokens)
+    pairs = [part[:rows].reshape(shape) for part in pairs]
     with jax.named_scope("z01"):
-        rest = [
-            swap(jnp.stack([part[k - 1] for part in pairs]), "head", k)
-            for k in range(1, head_count)
-        ]
+        rest_sent = [
+            jnp.stack([part[k - 1] for part in pairs]) for k in reversed(range(1, head_count))
+        ][::-1]
+        rest = [swap(rest_sent[k - 1], "head", k) for k in reversed(range(1, head_count))][::-1]
+    singles = sync(singles, rest_sent)[0]
     plane, other, held = lax.cond(seen, last_head, none, singles, own, table)
-    rest, held = sync(rest, held)
+    rest = [sync(part, held)[0] for part in rest]
     mine = [(plane, head_count)] + [(part, 0) for part in rest]
     other = [(other, head_count)] + [(over_cores(part, "cores01"), 0) for part in rest]
     held = heads(0, mine, other, held, table, True)
@@ -392,7 +411,9 @@
     powers = all(n & (n - 1) == 0 for n in (chips_seq, head_count))
     if not (one_block and powers and group_heads % chips_seq == 0 and chips % ROWS == 0):
         return False
-    return (group_heads // chips_seq) % 2 == 1 and chips_seq % 2 == 0 and ROWS % chips_seq == 0
+    small = max(PAIR * chips, key_lists.shape[2]) <= 256
+    odd = (group_heads // chips_seq) % 2 == 1
+    return small and odd and chips_seq % 2 == 0 and ROWS % chips_seq == 0
 
 
 def solution(mesh):

time: 105 us -> 103 us (0.981)
  waiting for transfers between devices: 6.52 us -> 14.4 us
  blocking collectives: 53.3 us -> 49.1 us
  Pallas kernels: 16.9 us -> 14.3 us
  other arithmetic: 2.72 us -> 0.53 us
  starting transfers between devices: 18.1 us -> 16.5 us
    all_to_all x2 -> x1, blocking collectives: 26 us -> 15.7 us  [over_p(): lax.all_to_all(value, 'chip', split_axis=0, concat_axis=0, tiled=True)]
    ppermute x13, waiting for transfers between devices: 6.52 us -> 14.4 us  [swap(): return lax.ppermute(value, axis, [(i, i ^ k) for i in range(size)])]
    all_to_all x1, blocking collectives: 27.3 us -> 33.4 us  [on_pair(): lax.all_to_all(held, ('head', 'chip'), split_axis=0, concat_axis=0, tiled...]
    pallas_call x2, Pallas kernels: 14.7 us -> 12.7 us  [attend(): pl.pallas_call(functools.partial(attend_kernel, scale=LOG2E / math.sqrt(h...]
    ppermute x13, starting transfers between devices: 18.1 us -> 16.5 us  [swap(): return lax.ppermute(value, axis, [(i, i ^ k) for i in range(size)])]
    another operation x3 -> x2, other arithmetic: 1.65 us -> 0.16 us  [on_pair(): jnp.stack([part[k - 1] for part in pairs])]
    unnamed x23 -> x4, local copies, waits for them, and re-layouts: 1.61 us -> 2.19 us
  transfers between devices with their start and end apart: 13 -> 13, of which waited for: 5 -> 6; matrix products, arithmetic and copies ran while one was open for 3% -> 2% of each run, Pallas kernels for 6% -> 6%
where the time goes in v4:
time: 103 us; the launch traced here: 102 us
  blocking collectives  49.1 us (48%)
  starting transfers between devices  16.5 us (16%)
  waiting for transfers between devices  14.4 us (14%)
  Pallas kernels  14.3 us (14%)
  local copies, waits for them, and re-layouts  6.46 us (6%)
    all_to_all x1, blocking collectives, on_pair(): lax.all_to_all(held, ('head', 'chip'), split_axis=0, concat_axis=0, tiled...  33.4 us
    ppermute x13, starting transfers between devices, swap(): return lax.ppermute(value, axis, [(i, i ^ k) for i in range(size)])  16.5 us
    all_to_all x1, blocking collectives, over_p(): lax.all_to_all(value, 'chip', split_axis=0, concat_axis=0, tiled=True)  15.7 us
    ppermute x13, waiting for transfers between devices, swap(): return lax.ppermute(value, axis, [(i, i ^ k) for i in range(size)])  14.4 us
    pallas_call x2, Pallas kernels, attend(): pl.pallas_call(functools.partial(attend_kernel, scale=LOG2E / math.sqrt(h...  12.7 us
    unnamed x4, local copies, waits for them, and re-layouts  2.19 us
  transfers between devices with their start and end apart: 13, of which 6 were waited for; matrix products, arithmetic and copies ran while one was open for 2% of the time, Pallas kernels for 6%

profile of v4, /device:TPU:0, one launch (start us, length us, event | category | flops | bytes accessed | tf_op | source)
XLA Modules:
  0.0 102.3 jit_solution(11138670296420855776)
XLA Ops:
  0.0 0.8 copy.14.used_ref
  0.8 0.8 copy.13.lists_ref
  1.6 1.8 %slice_bitcast_fusion = (bf16[128,3072]{1,0:T(8,128)(2,1)S(1)}, bf16[128,3072]{1,0:T(8,128)(2,1)S(1)}, bf16[128,3072]{1,0:T(8,128)(2,1)S(1)}) fusion(bf16[128,3,3072]{2,0,1:T(8,128)(2,1)} %param.5), kind=kLoop, calls=%fused_computation.3 | loop fusion | bytes 4718592 | tf_op jit(solution)/shard_map/squeeze | solution.py:255
  3.3 0.1 pad_add_fusion.me_ref
  3.4 1.6 %pack.1 = (bf16[4,1,3,64,128]{4,3,2,1,0:T(8,128)(2,1)S(1)}, bf16[4,1,3,64,128]{4,3,2,1,0:T(8,128)(2,1)S(1)}, bf16[4,1,3,64,128]{4,3,2,1,0:T(8,128)(2,1)S(1)}, bf...) custom-call(s32[3]{0:T(128)S(1)} %pad_add_fusion.me_ref, ...), custom_call_target="tpu_custom_call" | custom-call | tf_op jit(solution)/shard_map/pack/pallas_call | solution.py:91
  5.0 3.1 %collective-permute-start.4 = (bf16[4,1,3,64,128]{4,3,2,1,0:T(8,128)(2,1)S(1)}, bf16[4,1,3,64,128]{4,3,2,1,0:T(8,128)(2,1)S(1)}, u32[]{:S(2)}, u32[]{:S(2)}) collective-permute-start(bf16[4,1,3,64,128]{4,3,2,1,0:T(8,128)(2,1)S(1)} %get-tuple-element.50), channel_id=1, source_target_pairs={{0,1},{1,0},{2,3},{3,2},{4,5},{5,4},{6,7},{7,6},{8,9},{9,8},{10,11... | collective-permute-start | bytes 589832 | tf_op jit(solution)/shard_map/z2/ppermute | solution.py:244
  8.1 2.6 %collective-permute-start.5 = (bf16[4,1,3,64,128]{4,3,2,1,0:T(8,128)(2,1)S(1)}, bf16[4,1,3,64,128]{4,3,2,1,0:T(8,128)(2,1)S(1)}, u32[]{:S(2)}, u32[]{:S(2)}) collective-permute-start(bf16[4,1,3,64,128]{4,3,2,1,0:T(8,128)(2,1)S(1)} %get-tuple-element.51), channel_id=1, source_target_pairs={{0,2},{1,3},{2,0},{3,1},{4,6},{5,7},{6,4},{7,5},{8,10},{9,11},{10,... | collective-permute-start | bytes 589832 | tf_op jit(solution)/shard_map/z2/ppermute | solution.py:244
  10.7 0.0 collective-permute-start.6
  10.7 1.7 %collective-permute-start.1 = (bf16[1168,128]{1,0:T(8,128)(2,1)S(1)}, bf16[1168,128]{1,0:T(8,128)(2,1)S(1)}, u32[]{:S(2)}, u32[]{:S(2)}) collective-permute-start(bf16[1168,128]{1,0:T(8,128)(2,1)S(1)} %get-tuple-element.46), channel_id=1, source_target_pairs={{0,8},{8,0},{16,24},{24,16},{1,9},{9,1},{17,25},{25,17},{2,10},{10... | collective-permute-start | bytes 897032 | tf_op jit(solution)/shard_map/p01/ppermute | solution.py:244
  12.4 1.5 %collective-permute-start.2 = (bf16[1168,128]{1,0:T(8,128)(2,1)S(1)}, bf16[1168,128]{1,0:T(8,128)(2,1)S(1)}, u32[]{:S(2)}, u32[]{:S(2)}) collective-permute-start(bf16[1168,128]{1,0:T(8,128)(2,1)S(1)} %get-tuple-element.47), channel_id=1, source_target_pairs={{0,16},{8,24},{16,0},{24,8},{1,17},{9,25},{17,1},{25,9},{2,18},{10... | collective-permute-start | bytes 897032 | tf_op jit(solution)/shard_map/p01/ppermute | solution.py:244
  13.9 1.2 %slice.125 = s32[1,1]{0,1:T(1,128)} slice(s32[12,4]{0,1:T(4,128)} %param.7), slice={[0:1], [0:1]} | slice | bytes 8 | tf_op jit(solution)/shard_map/slice | solution.py:277
  15.8 3.2 %collective-permute-done.1 = bf16[1168,128]{1,0:T(8,128)(2,1)S(1)} collective-permute-done((bf16[1168,128]{1,0:T(8,128)(2,1)S(1)}, bf16[1168,128]{1,0:T(8,128)(2,1)S(1)}, u32[]{:S(2)}, u32[]{:S(2)}) %collective-permute-start.1) | collective-permute-done | bytes 299040 | tf_op jit(solution)/shard_map/p01/ppermute | solution.py:244
  18.9 2.4 %collective-permute-start.3 = (bf16[1168,128]{1,0:T(8,128)(2,1)S(1)}, bf16[1168,128]{1,0:T(8,128)(2,1)S(1)}, u32[]{:S(2)}, u32[]{:S(2)}) collective-permute-start(bf16[1168,128]{1,0:T(8,128)(2,1)S(1)} %get-tuple-element.48), channel_id=1, source_target_pairs={{0,24},{8,16},{16,8},{24,0},{1,25},{9,17},{17,9},{25,1},{2,26},{10... | collective-permute-start | bytes 897032 | tf_op jit(solution)/shard_map/p01/ppermute | solution.py:244
  21.4 0.0 collective-permute-done.2
  21.4 5.7 %collective-permute-done.3 = bf16[1168,128]{1,0:T(8,128)(2,1)S(1)} collective-permute-done((bf16[1168,128]{1,0:T(8,128)(2,1)S(1)}, bf16[1168,128]{1,0:T(8,128)(2,1)S(1)}, u32[]{:S(2)}, u32[]{:S(2)}) %collective-permute-start.3) | collective-permute-done | bytes 299040 | tf_op jit(solution)/shard_map/p01/ppermute | solution.py:244
  27.2 0.1 pad_maximum_fusion.2
  27.3 0.4 collective-permute-start.7
  27.7 3.5 %collective-permute-start.8 = (bf16[4,2,3,64,128]{4,3,2,1,0:T(8,128)(2,1)S(1)}, bf16[4,2,3,64,128]{4,3,2,1,0:T(8,128)(2,1)S(1)}, u32[]{:S(2)}, u32[]{:S(2)}) collective-permute-start(bf16[4,2,3,64,128]{4,3,2,1,0:T(8,128)(2,1)S(1)} %get-tuple-element.94), channel_id=1, source_target_pairs={{0,2},{1,3},{2,0},{3,1},{4,6},{5,7},{6,4},{7,5},{8,10},{9,11},{10,... | collective-permute-start | bytes 1179656 | tf_op jit(solution)/shard_map/z01/ppermute | solution.py:244
  31.2 0.1 pad_maximum_fusion.4
  31.3 0.0 collective-permute-done.4
  31.3 0.6 collective-permute-start.9
  31.9 0.0 collective-permute-done.5
  31.9 0.0 collective-permute-done.6
  32.0 0.0 copy-start
  32.0 0.6 copy-done
  32.6 25.7 %conditional.1 = (bf16[4,6,3,64,128]{4,3,2,1,0:T(8,128)(2,1)}, bf16[4,6,3,64,128]{4,3,2,1,0:T(8,128)(2,1)}, bf16[16,3,64,128]{3,2,1,0:T(8,128)(2,1)S(1)}) conditional(s32[]{:T(128)} %bitcast.23, () %tuple.17, (bf16[4,1,3,64,128]{4,3,2,1,0:T(8,128)(2,1)S(1)}, bf16[4,1,3,64,128]{4,3,2,1,0:T(8,128)(2,1)S(1)}, bf16[4,1,3,64,128]{4,3,2,1,0:T(8,128)(2,1)S(1)}, ...), branch_computations={%region_0.0_spmd, %region_1.0_spmd} | conditional | flops 1769473 | bytes 11010113 | solution.py:303
  32.6 0.1 maximum_bitcast_fusion
  32.7 0.1 pad_maximum_fusion
  32.8 15.7 %all_to_all.9.rest_0_.rest_1_.rest_2_.rest_3_ = bf16[4,6,3,64,128]{4,3,2,1,0:T(8,128)(2,1)} all-to-all(bf16[4,6,3,64,128]{4,3,2,1,0:T(8,128)(2,1)S(1)} %pad_maximum_fusion), channel_id=1, replica_groups=mesh['chip'=4,'core'=2,'head'=4] {'chip'}, dimensions={0} | all-to-all | bytes 2359296 | tf_op jit(solution)/shard_map/cond/branch_1_fun/plane/all_to_all | solution.py:264
  48.5 0.0 collective-permute-start
  48.5 3.2 %collective-permute-done.rest_4_.rest_5_.rest_6_.rest_7_ = bf16[4,6,3,64,128]{4,3,2,1,0:T(8,128)(2,1)} collective-permute-done((bf16[4,6,3,64,128]{4,3,2,1,0:T(8,128)(2,1)}, bf16[4,6,3,64,128]{4,3,2,1,0:T(8,128)(2,1)}, u32[]{:S(2)}, u32[]{:S(2)}) %collective-permute-start) | collective-permute-done | bytes 1179680 | tf_op jit(solution)/shard_map/cond/branch_1_fun/cores2/ppermute | solution.py:244
  51.7 6.3 %attend.2 = bf16[16,3,64,128]{3,2,1,0:T(8,128)(2,1)S(1)} custom-call(s32[3]{0:T(128)S(1)} %get-tuple-element.24.me_ref, s32[4,16,9]{2,1,0:T(8,128)S(1)} %get-tuple-element.25.table_ref, bf16[4,6,3,64,128]{4,3,2,1,0:T(8,128)(2,1)} %all_to_all.9.rest_0_.rest_1_.rest_2_.rest_3_, bf16[4,6,3,64,128]{4,3,2,1,0:T(8,128)(2,1)} %all_to_all.9.rest_0_.rest_1_.rest_2_.rest_3_, ...), custom_call_target="tpu_custom_call" | custom-call | flops 1 | bytes 1 | tf_op jit(solution)/shard_map/cond/branch_1_fun/heads2/attend/pallas_call | solution.py:214
  58.2 0.0 collective-permute-done.9.rest_3_
  58.3 0.0 collective-permute-done.8.rest_2_
  58.3 0.0 collective-permute-done.7.rest_1_
  58.3 0.1 collective-permute-start.10
  58.4 0.5 collective-permute-start.11
  58.9 0.1 collective-permute-start.12
  58.9 1.1 %collective-permute-done.10.rest_5_ = bf16[4,2,3,64,128]{4,3,2,1,0:T(8,128)(2,1)S(1)} collective-permute-done((bf16[4,2,3,64,128]{4,3,2,1,0:T(8,128)(2,1)S(1)}, bf16[4,2,3,64,128]{4,3,2,1,0:T(8,128)(2,1)S(1)}, u32[]{:S(2)}, u32[]{:S(2)}) %collective-permute-start.10) | collective-permute-done | bytes 393248 | tf_op jit(solution)/shard_map/cores01/ppermute | solution.py:244
  60.1 0.6 collective-permute-done.11.rest_6_
  60.6 0.6 collective-permute-done.12.rest_7_
  61.2 6.4 %attend.3 = bf16[16,3,64,128]{3,2,1,0:T(8,128)(2,1)S(1)} custom-call(s32[3]{0:T(128)S(1)} %pad_add_fusion.me_ref, s32[4,16,9]{2,1,0:T(8,128)} %copy-done, bf16[4,6,3,64,128]{4,3,2,1,0:T(8,128)(2,1)} %get-tuple-element.58.rest_0_, bf16[4,2,3,64,128]{4,3,2,1,0:T(8,128)(2,1)S(1)} %collective-permute-done.7.rest_1_, ...), custom_call_target="tpu_custom_call", output_to_operand_aliasing={{}: (10, {})} | custom-call | flops 1 | bytes 1 | tf_op jit(solution)/shard_map/heads0/attend/pallas_call | solution.py:214
  67.6 33.4 %all_to_all.10 = bf16[16,3,64,128]{3,2,1,0:T(8,128)(2,1)S(1)} all-to-all(bf16[16,3,64,128]{3,2,1,0:T(8,128)(2,1)S(1)} %attend.3), channel_id=1, replica_groups=mesh['chip'=4,'core'=2,'head'=4] {'head','chip'}, dimensions={0} | all-to-all | bytes 1572864 | tf_op jit(solution)/shard_map/all_to_all | solution.py:308
  101.0 0.1 pad_maximum_fusion.1
  101.1 1.2 %copy.20 = bf16[128,3072]{1,0:T(8,128)(2,1)} copy(bf16[128,3072]{0,1:T(8,128)(2,1)S(1)} %bitcast.55) | data formatting | bytes 1572864 | tf_op jit(solution)/shard_map/transpose | solution.py:318
  (11 shorter events, 0.2 us)
Async XLA Ops:
  5.0 26.3 %collective-permute-start.4 = (bf16[4,1,3,64,128]{4,3,2,1,0:T(8,128)(2,1)S(1)}, bf16[4,1,3,64,128]{4,3,2,1,0:T(8,128)(2,1)S(1)}, u32[]{:S(2)}, u32[]{:S(2)}) collective-permute-start(bf16[4,1,3,64,128]{4,3,2,1,0:T(8,128)(2,1)S(1)} %get-tuple-element.50), channel_id=1, source_target_pairs={{0,1},{1,0},{2,3},{3,2},{4,5},{5,4},{6,7},{7,6},{8,9},{9,8},{10,11... | collective-permute-start | bytes 589832 | tf_op jit(solution)/shard_map/z2/ppermute | solution.py:244
  8.1 23.9 %collective-permute-start.5 = (bf16[4,1,3,64,128]{4,3,2,1,0:T(8,128)(2,1)S(1)}, bf16[4,1,3,64,128]{4,3,2,1,0:T(8,128)(2,1)S(1)}, u32[]{:S(2)}, u32[]{:S(2)}) collective-permute-start(bf16[4,1,3,64,128]{4,3,2,1,0:T(8,128)(2,1)S(1)} %get-tuple-element.51), channel_id=1, source_target_pairs={{0,2},{1,3},{2,0},{3,1},{4,6},{5,7},{6,4},{7,5},{8,10},{9,11},{10,... | collective-permute-start | bytes 589832 | tf_op jit(solution)/shard_map/z2/ppermute | solution.py:244
  10.7 21.3 %collective-permute-start.6 = (bf16[4,1,3,64,128]{4,3,2,1,0:T(8,128)(2,1)S(1)}, bf16[4,1,3,64,128]{4,3,2,1,0:T(8,128)(2,1)S(1)}, u32[]{:S(2)}, u32[]{:S(2)}) collective-permute-start(bf16[4,1,3,64,128]{4,3,2,1,0:T(8,128)(2,1)S(1)} %get-tuple-element.52), channel_id=1, source_target_pairs={{0,3},{1,2},{2,1},{3,0},{4,7},{5,6},{6,5},{7,4},{8,11},{9,10},{10,... | collective-permute-start | bytes 589832 | tf_op jit(solution)/shard_map/z2/ppermute | solution.py:244
  10.7 8.3 %collective-permute-start.1 = (bf16[1168,128]{1,0:T(8,128)(2,1)S(1)}, bf16[1168,128]{1,0:T(8,128)(2,1)S(1)}, u32[]{:S(2)}, u32[]{:S(2)}) collective-permute-start(bf16[1168,128]{1,0:T(8,128)(2,1)S(1)} %get-tuple-element.46), channel_id=1, source_target_pairs={{0,8},{8,0},{16,24},{24,16},{1,9},{9,1},{17,25},{25,17},{2,10},{10... | collective-permute-start | bytes 897032 | tf_op jit(solution)/shard_map/p01/ppermute | solution.py:244
  12.4 9.0 %collective-permute-start.2 = (bf16[1168,128]{1,0:T(8,128)(2,1)S(1)}, bf16[1168,128]{1,0:T(8,128)(2,1)S(1)}, u32[]{:S(2)}, u32[]{:S(2)}) collective-permute-start(bf16[1168,128]{1,0:T(8,128)(2,1)S(1)} %get-tuple-element.47), channel_id=1, source_target_pairs={{0,16},{8,24},{16,0},{24,8},{1,17},{9,25},{17,1},{25,9},{2,18},{10... | collective-permute-start | bytes 897032 | tf_op jit(solution)/shard_map/p01/ppermute | solution.py:244
  18.9 8.2 %collective-permute-start.3 = (bf16[1168,128]{1,0:T(8,128)(2,1)S(1)}, bf16[1168,128]{1,0:T(8,128)(2,1)S(1)}, u32[]{:S(2)}, u32[]{:S(2)}) collective-permute-start(bf16[1168,128]{1,0:T(8,128)(2,1)S(1)} %get-tuple-element.48), channel_id=1, source_target_pairs={{0,24},{8,16},{16,8},{24,0},{1,25},{9,17},{17,9},{25,1},{2,26},{10... | collective-permute-start | bytes 897032 | tf_op jit(solution)/shard_map/p01/ppermute | solution.py:244
  27.3 30.9 %collective-permute-start.7 = (bf16[4,2,3,64,128]{4,3,2,1,0:T(8,128)(2,1)S(1)}, bf16[4,2,3,64,128]{4,3,2,1,0:T(8,128)(2,1)S(1)}, u32[]{:S(2)}, u32[]{:S(2)}) collective-permute-start(bf16[4,2,3,64,128]{4,3,2,1,0:T(8,128)(2,1)S(1)} %get-tuple-element.93), channel_id=1, source_target_pairs={{0,1},{1,0},{2,3},{3,2},{4,5},{5,4},{6,7},{7,6},{8,9},{9,8},{10,11... | collective-permute-start | bytes 1179656 | tf_op jit(solution)/shard_map/z01/ppermute | solution.py:244
  27.7 30.5 %collective-permute-start.8 = (bf16[4,2,3,64,128]{4,3,2,1,0:T(8,128)(2,1)S(1)}, bf16[4,2,3,64,128]{4,3,2,1,0:T(8,128)(2,1)S(1)}, u32[]{:S(2)}, u32[]{:S(2)}) collective-permute-start(bf16[4,2,3,64,128]{4,3,2,1,0:T(8,128)(2,1)S(1)} %get-tuple-element.94), channel_id=1, source_target_pairs={{0,2},{1,3},{2,0},{3,1},{4,6},{5,7},{6,4},{7,5},{8,10},{9,11},{10,... | collective-permute-start | bytes 1179656 | tf_op jit(solution)/shard_map/z01/ppermute | solution.py:244
  31.3 27.0 %collective-permute-start.9 = (bf16[4,2,3,64,128]{4,3,2,1,0:T(8,128)(2,1)S(1)}, bf16[4,2,3,64,128]{4,3,2,1,0:T(8,128)(2,1)S(1)}, u32[]{:S(2)}, u32[]{:S(2)}) collective-permute-start(bf16[4,2,3,64,128]{4,3,2,1,0:T(8,128)(2,1)S(1)} %pad_maximum_fusion.4), channel_id=1, source_target_pairs={{0,3},{1,2},{2,1},{3,0},{4,7},{5,6},{6,5},{7,4},{8,11},{9,10},{10,... | collective-permute-start | bytes 1179656 | tf_op jit(solution)/shard_map/z01/ppermute | solution.py:244
  32.0 0.6 copy-start
  48.5 3.2 %collective-permute-start = (bf16[4,6,3,64,128]{4,3,2,1,0:T(8,128)(2,1)}, bf16[4,6,3,64,128]{4,3,2,1,0:T(8,128)(2,1)}, u32[]{:S(2)}, u32[]{:S(2)}) collective-permute-start(bf16[4,6,3,64,128]{4,3,2,1,0:T(8,128)(2,1)} %all_to_all.9.rest_0_.rest_1_.rest_2_.rest_3_), channel_id=1, source_target_pairs={{0,4},{4,0},{1,5},{5,1},{2,6},{6,2},{3,7},{7,3},{8,12},{12,8},{9,1... | collective-permute-start | bytes 3538952 | tf_op jit(solution)/shard_map/cond/branch_1_fun/cores2/ppermute | solution.py:244
  58.3 1.8 %collective-permute-start.10 = (bf16[4,2,3,64,128]{4,3,2,1,0:T(8,128)(2,1)S(1)}, bf16[4,2,3,64,128]{4,3,2,1,0:T(8,128)(2,1)S(1)}, u32[]{:S(2)}, u32[]{:S(2)}) collective-permute-start(bf16[4,2,3,64,128]{4,3,2,1,0:T(8,128)(2,1)S(1)} %collective-permute-done.7.rest_1_), channel_id=1, source_target_pairs={{0,4},{4,0},{1,5},{5,1},{2,6},{6,2},{3,7},{7,3},{8,12},{12,8},{9,1... | collective-permute-start | bytes 1179656 | tf_op jit(solution)/shard_map/cores01/ppermute | solution.py:244
  58.4 2.3 %collective-permute-start.11 = (bf16[4,2,3,64,128]{4,3,2,1,0:T(8,128)(2,1)S(1)}, bf16[4,2,3,64,128]{4,3,2,1,0:T(8,128)(2,1)S(1)}, u32[]{:S(2)}, u32[]{:S(2)}) collective-permute-start(bf16[4,2,3,64,128]{4,3,2,1,0:T(8,128)(2,1)S(1)} %collective-permute-done.8.rest_2_), channel_id=1, source_target_pairs={{0,4},{4,0},{1,5},{5,1},{2,6},{6,2},{3,7},{7,3},{8,12},{12,8},{9,1... | collective-permute-start | bytes 1179656 | tf_op jit(solution)/shard_map/cores01/ppermute | solution.py:244
  58.9 2.3 %collective-permute-start.12 = (bf16[4,2,3,64,128]{4,3,2,1,0:T(8,128)(2,1)S(1)}, bf16[4,2,3,64,128]{4,3,2,1,0:T(8,128)(2,1)S(1)}, u32[]{:S(2)}, u32[]{:S(2)}) collective-permute-start(bf16[4,2,3,64,128]{4,3,2,1,0:T(8,128)(2,1)S(1)} %collective-permute-done.9.rest_3_), channel_id=1, source_target_pairs={{0,4},{4,0},{1,5},{5,1},{2,6},{6,2},{3,7},{7,3},{8,12},{12,8},{9,1... | collective-permute-start | bytes 1179656 | tf_op jit(solution)/shard_map/cores01/ppermute | solution.py:244

commit v5 on v4

--- a/solution.py
+++ b/solution.py
@@ -31,7 +31,16 @@
 ):
     apart, own, joined = rest[:head_count], rest[head_count], rest[head_count + 1 : -3]
     held_one, held, table = rest[-3:]
+    blocks, list_most, heads = lists_ref.shape
     table[...] = jnp.zeros_like(table)
+    for b in range(blocks):
+        listed = lists_ref[b]
+        shard = listed // head_count
+        slots = (shard % PAIR != me_ref[2]).astype(jnp.int32) * (chips_seq * head_count)
+        slots += listed % head_count * chips_seq + shard // PAIR
+        table[b * list_most : (b + 1) * list_most, :heads] = slots.astype(jnp.float32)
+    table[blocks * list_most : blocks * (list_most + 1), :heads] = used_ref[...].astype(jnp.float32)
+    lists = table[...].T[: list_rows(heads)].astype(joined[0].dtype)
     tokens = q_ref.shape[0]
     head_size = held.shape[-2]
     half, lanes = tokens // 2, 2 * head_size
@@ -57,26 +66,13 @@
         apart[-1 - kz][...] = held_one[:, kz]
     own[...] = held[:, 0]
     for kp in range(chips_seq):
-        p, many = me_ref[1] ^ kp, len(paired)
-        for at, head in enumerate([p * many + j for j in paired] + [chips_seq * many + p]):
-            listed = lists_ref[head]
-            shard = listed // head_count
-            slots = (shard % PAIR != me_ref[2]).astype(jnp.int32) * (chips_seq * head_count)
-            slots += listed % head_count * chips_seq + shard // PAIR
-            table[at * head_count : (at + 1) * head_count, : listed.shape[1]] = slots.astype(
-                jnp.float32
-            )
-            table[pl.ds(per_chip * head_count + at, 1), :head_count] = used_ref[
-                pl.ds(head, 1)
-            ].astype(jnp.float32)
-        lists = table[...].astype(joined[kp].dtype)
         rows = joined[kp].shape[0] - lists.shape[0]
         joined[kp][:rows] = held[me_ref[1] ^ kp, 1:].reshape(rows, tokens)
         joined[kp][rows:] = lists
 
 
-def list_rows(per_chip, head_count):
-    return pl.cdiv(per_chip * (head_count + 1), 16) * 16
+def list_rows(heads):
+    return pl.cdiv(heads, 16) * 16
 
 
 def pack(me, queries, keys, values, lists, used, *, chips_seq, head_count, per_chip, head_size):
@@ -86,7 +82,7 @@
     part = (3, head_size, tokens)
     shapes = [(chips_seq, 1, *part)] * head_count
     shapes.append((chips_seq, len(paired), *part))
-    rows = (head_count - 1) * len(paired) * math.prod(part[:-1]) + list_rows(per_chip, head_count)
+    rows = (head_count - 1) * len(paired) * math.prod(part[:-1]) + list_rows(lists.shape[2])
     shapes += [(rows, tokens)] * chips_seq
     return pl.pallas_call(
         functools.partial(
@@ -107,7 +103,7 @@
                 pltpu.VMEM((chips_seq, head_count, len(heads), *part), queries.dtype)
                 for heads in (single, paired)
             ]
-            + [pltpu.VMEM((list_rows(per_chip, head_count), tokens), jnp.float32)],
+            + [pltpu.VMEM((tokens, tokens), jnp.float32)],
         ),
         out_shape=[jax.ShapeDtypeStruct(s, queries.dtype) for s in shapes],
         compiler_params=pltpu.CompilerParams(vmem_limit_bytes=48 << 20),
@@ -121,9 +117,10 @@
     mine, other = rest[:head_count], rest[head_count : 2 * head_count]
     out_ref, q, kv = rest[-3:]
     blocks, head_size, tokens = q.shape
-    head = j + pl.program_id(0)
-    counted = per_chip * head_count + head
-    head = head * head_count
+    paired = per_chip // 2 * 2
+    head = me_ref[1] * paired + j if j < paired else chips_seq * paired + me_ref[1]
+    head = head + pl.program_id(0)
+    most = entries - 1
     for kz in range(head_count):
         for p in range(chips_seq):
             natural = (me_ref[0] ^ kz) * chips_seq + (p ^ me_ref[1] if near and kz else p)
@@ -146,7 +143,7 @@
             keys, vals = [kv[own, 0]], [jnp.concatenate([kv[own, 1], ones], axis=0)]
             for e in range(1, seen):
                 live = e <= counts[r]
-                slot = jnp.where(live, table_ref[p, head + z, e - 1], own)
+                slot = jnp.where(live, table_ref[p, head, z * most + e - 1], own)
                 factor = jnp.where(live, 1.0, 0.0).astype(jnp.bfloat16)
                 keys.append(kv[slot, 0])
                 vals.append(jnp.concatenate([kv[slot, 1], ones], axis=0) * factor)
@@ -180,7 +177,7 @@
         counts = []
         for r in range(ROWS):
             p, z = row_of(base, r)
-            counts.append(table_ref[p, counted, z])
+            counts.append(table_ref[p, head, head_count * most + z])
         seen = 1 + functools.reduce(jnp.maximum, counts)
         below = 0
         for size in (*range(3, entries, 2), entries):
@@ -272,7 +269,7 @@
             return attend(me, table, mine, other, held, entries=entries, j=c, near=near, **sizes)
 
     last, each = per_chip - 1, range(head_count)
-    packed = pack(me, *qkv, key_lists, list_counts, head_size=head_size, **sizes)
+    packed = pack(me, *qkv, key_lists.transpose(1, 2, 0), list_counts.T, head_size=head_size, **sizes)
     singles, own, pairs = packed[head_count - 1 :: -1], packed[head_count], packed[head_count + 1 :]
     seen = list_counts[0, 0] > 0
 
@@ -290,8 +287,8 @@
 
     pairs = over(pairs, "chip", "p01")
     singles = over(singles, "head", "z2")
-    rows = pairs[0].shape[0] - list_rows(per_chip, head_count)
-    table = jnp.stack([part[rows:, :entries] for part in pairs]).astype(jnp.int32)
+    rows = pairs[0].shape[0] - list_rows(heads_dev)
+    table = jnp.stack([part[rows:] for part in pairs]).astype(jnp.int32)
     shape = (head_count - 1, per_chip - 1, 3, head_size, tokens)
     pairs = [part[:rows].reshape(shape) for part in pairs]
     with jax.named_scope("z01"):
@@ -413,7 +410,9 @@
         return False
     small = max(PAIR * chips, key_lists.shape[2]) <= 256
     odd = (group_heads // chips_seq) % 2 == 1
-    return small and odd and chips_seq % 2 == 0 and ROWS % chips_seq == 0
+    tokens = projected.shape[0] // (seq_count * head_count)
+    fit = head_count * (key_lists.shape[2] + 1) <= tokens and group_heads <= tokens
+    return small and odd and fit and chips_seq % 2 == 0 and ROWS % chips_seq == 0
 
 
 def solution(mesh):

time: 103 us -> 101 us (0.981)
  local copies, waits for them, and re-layouts: 6.46 us -> 4.22 us
    unnamed x4 -> x6, local copies, waits for them, and re-layouts: 2.19 us -> 0.62 us
    ppermute x13, waiting for transfers between devices: 14.4 us -> 15.4 us  [swap(): return lax.ppermute(value, axis, [(i, i ^ k) for i in range(size)])]
  transfers between devices with their start and end apart: 13 -> 13, of which waited for: 6 -> 7; matrix products, arithmetic and copies ran while one was open for 2% -> 1% of each run, Pallas kernels for 6% -> 6%
where the time goes in v5:
time: 101 us; the launch traced here: 100 us
  blocking collectives  48.6 us (48%)
  starting transfers between devices  16.4 us (16%)
  waiting for transfers between devices  15.4 us (15%)
  Pallas kernels  13.8 us (14%)
  local copies, waits for them, and re-layouts  4.22 us (4%)
    all_to_all x1, blocking collectives, on_pair(): lax.all_to_all(held, ('head', 'chip'), split_axis=0, concat_axis=0, tiled...  32.9 us
    ppermute x13, starting transfers between devices, swap(): return lax.ppermute(value, axis, [(i, i ^ k) for i in range(size)])  16.4 us
    all_to_all x1, blocking collectives, over_p(): lax.all_to_all(value, 'chip', split_axis=0, concat_axis=0, tiled=True)  15.7 us
    ppermute x13, waiting for transfers between devices, swap(): return lax.ppermute(value, axis, [(i, i ^ k) for i in range(size)])  15.4 us
    pallas_call x2, Pallas kernels, attend(): pl.pallas_call(functools.partial(attend_kernel, scale=LOG2E / math.sqrt(h...  12.3 us
  transfers between devices with their start and end apart: 13, of which 7 were waited for; matrix products, arithmetic and copies ran while one was open for 1% of the time, Pallas kernels for 6%

profile of v5, /device:TPU:0, one launch (start us, length us, event | category | flops | bytes accessed | tf_op | source)
XLA Modules:
  0.0 100.0 jit_solution(5477306696698199310)
XLA Ops:
  0.0 0.0 copy-start
  0.0 0.0 copy-start.1
  0.0 1.8 %slice_bitcast_fusion = (bf16[128,3072]{1,0:T(8,128)(2,1)S(1)}, bf16[128,3072]{1,0:T(8,128)(2,1)S(1)}, bf16[128,3072]{1,0:T(8,128)(2,1)S(1)}) fusion(bf16[128,3,3072]{2,0,1:T(8,128)(2,1)} %param.5), kind=kLoop, calls=%fused_computation.3 | loop fusion | bytes 4718592 | tf_op jit(solution)/shard_map/squeeze | solution.py:252
  1.8 0.1 pad_add_fusion.me_ref
  1.9 0.0 copy-done
  1.9 0.0 copy-done.1
  1.9 1.5 %pack.1 = (bf16[4,1,3,64,128]{4,3,2,1,0:T(8,128)(2,1)S(1)}, bf16[4,1,3,64,128]{4,3,2,1,0:T(8,128)(2,1)S(1)}, bf16[4,1,3,64,128]{4,3,2,1,0:T(8,128)(2,1)S(1)}, bf...) custom-call(s32[3]{0:T(128)S(1)} %pad_add_fusion.me_ref, ...), custom_call_target="tpu_custom_call" | custom-call | tf_op jit(solution)/shard_map/pack/pallas_call | solution.py:87
  3.4 3.1 %collective-permute-start.4 = (bf16[4,1,3,64,128]{4,3,2,1,0:T(8,128)(2,1)S(1)}, bf16[4,1,3,64,128]{4,3,2,1,0:T(8,128)(2,1)S(1)}, u32[]{:S(2)}, u32[]{:S(2)}) collective-permute-start(bf16[4,1,3,64,128]{4,3,2,1,0:T(8,128)(2,1)S(1)} %get-tuple-element.50), channel_id=1, source_target_pairs={{0,1},{1,0},{2,3},{3,2},{4,5},{5,4},{6,7},{7,6},{8,9},{9,8},{10,11... | collective-permute-start | bytes 589832 | tf_op jit(solution)/shard_map/z2/ppermute | solution.py:241
  6.5 2.6 %collective-permute-start.5 = (bf16[4,1,3,64,128]{4,3,2,1,0:T(8,128)(2,1)S(1)}, bf16[4,1,3,64,128]{4,3,2,1,0:T(8,128)(2,1)S(1)}, u32[]{:S(2)}, u32[]{:S(2)}) collective-permute-start(bf16[4,1,3,64,128]{4,3,2,1,0:T(8,128)(2,1)S(1)} %get-tuple-element.51), channel_id=1, source_target_pairs={{0,2},{1,3},{2,0},{3,1},{4,6},{5,7},{6,4},{7,5},{8,10},{9,11},{10,... | collective-permute-start | bytes 589832 | tf_op jit(solution)/shard_map/z2/ppermute | solution.py:241
  9.1 0.0 collective-permute-start.6
  9.1 1.7 %collective-permute-start.1 = (bf16[1168,128]{1,0:T(8,128)(2,1)S(1)}, bf16[1168,128]{1,0:T(8,128)(2,1)S(1)}, u32[]{:S(2)}, u32[]{:S(2)}) collective-permute-start(bf16[1168,128]{1,0:T(8,128)(2,1)S(1)} %get-tuple-element.46), channel_id=1, source_target_pairs={{0,8},{8,0},{16,24},{24,16},{1,9},{9,1},{17,25},{25,17},{2,10},{10... | collective-permute-start | bytes 897032 | tf_op jit(solution)/shard_map/p01/ppermute | solution.py:241
  10.8 1.5 %collective-permute-start.2 = (bf16[1168,128]{1,0:T(8,128)(2,1)S(1)}, bf16[1168,128]{1,0:T(8,128)(2,1)S(1)}, u32[]{:S(2)}, u32[]{:S(2)}) collective-permute-start(bf16[1168,128]{1,0:T(8,128)(2,1)S(1)} %get-tuple-element.47), channel_id=1, source_target_pairs={{0,16},{8,24},{16,0},{24,8},{1,17},{9,25},{17,1},{25,9},{2,18},{10... | collective-permute-start | bytes 897032 | tf_op jit(solution)/shard_map/p01/ppermute | solution.py:241
  12.3 0.5 slice.125
  13.5 3.8 %collective-permute-done.1 = bf16[1168,128]{1,0:T(8,128)(2,1)S(1)} collective-permute-done((bf16[1168,128]{1,0:T(8,128)(2,1)S(1)}, bf16[1168,128]{1,0:T(8,128)(2,1)S(1)}, u32[]{:S(2)}, u32[]{:S(2)}) %collective-permute-start.1) | collective-permute-done | bytes 299040 | tf_op jit(solution)/shard_map/p01/ppermute | solution.py:241
  17.3 2.4 %collective-permute-start.3 = (bf16[1168,128]{1,0:T(8,128)(2,1)S(1)}, bf16[1168,128]{1,0:T(8,128)(2,1)S(1)}, u32[]{:S(2)}, u32[]{:S(2)}) collective-permute-start(bf16[1168,128]{1,0:T(8,128)(2,1)S(1)} %get-tuple-element.48), channel_id=1, source_target_pairs={{0,24},{8,16},{16,8},{24,0},{1,25},{9,17},{17,9},{25,1},{2,26},{10... | collective-permute-start | bytes 897032 | tf_op jit(solution)/shard_map/p01/ppermute | solution.py:241
  19.8 0.0 collective-permute-done.2
  19.9 5.7 %collective-permute-done.3 = bf16[1168,128]{1,0:T(8,128)(2,1)S(1)} collective-permute-done((bf16[1168,128]{1,0:T(8,128)(2,1)S(1)}, bf16[1168,128]{1,0:T(8,128)(2,1)S(1)}, u32[]{:S(2)}, u32[]{:S(2)}) %collective-permute-start.3) | collective-permute-done | bytes 299040 | tf_op jit(solution)/shard_map/p01/ppermute | solution.py:241
  25.6 0.1 pad_maximum_fusion.2
  25.7 0.4 collective-permute-start.7
  26.1 3.5 %collective-permute-start.8 = (bf16[4,2,3,64,128]{4,3,2,1,0:T(8,128)(2,1)S(1)}, bf16[4,2,3,64,128]{4,3,2,1,0:T(8,128)(2,1)S(1)}, u32[]{:S(2)}, u32[]{:S(2)}) collective-permute-start(bf16[4,2,3,64,128]{4,3,2,1,0:T(8,128)(2,1)S(1)} %get-tuple-element.94), channel_id=1, source_target_pairs={{0,2},{1,3},{2,0},{3,1},{4,6},{5,7},{6,4},{7,5},{8,10},{9,11},{10,... | collective-permute-start | bytes 1179656 | tf_op jit(solution)/shard_map/z01/ppermute | solution.py:241
  29.6 0.1 pad_maximum_fusion.4
  29.7 0.0 collective-permute-done.4
  29.7 0.6 collective-permute-start.9
  30.3 0.0 collective-permute-done.5
  30.3 0.0 collective-permute-done.6
  30.4 0.0 copy-start.2
  30.4 0.6 copy-done.2
  31.0 25.2 %conditional.1 = (bf16[4,6,3,64,128]{4,3,2,1,0:T(8,128)(2,1)}, bf16[4,6,3,64,128]{4,3,2,1,0:T(8,128)(2,1)}, bf16[16,3,64,128]{3,2,1,0:T(8,128)(2,1)S(1)}) conditional(s32[]{:T(128)} %bitcast.25, () %tuple.17, (bf16[4,1,3,64,128]{4,3,2,1,0:T(8,128)(2,1)S(1)}, bf16[4,1,3,64,128]{4,3,2,1,0:T(8,128)(2,1)S(1)}, bf16[4,1,3,64,128]{4,3,2,1,0:T(8,128)(2,1)S(1)}, ...), branch_computations={%region_0.0_spmd, %region_1.0_spmd} | conditional | flops 1769473 | bytes 11010113 | solution.py:300
  31.0 0.1 maximum_bitcast_fusion
  31.1 0.1 pad_maximum_fusion
  31.2 15.7 %all_to_all.9.rest_0_.rest_1_.rest_2_.rest_3_ = bf16[4,6,3,64,128]{4,3,2,1,0:T(8,128)(2,1)} all-to-all(bf16[4,6,3,64,128]{4,3,2,1,0:T(8,128)(2,1)S(1)} %pad_maximum_fusion), channel_id=1, replica_groups=mesh['chip'=4,'core'=2,'head'=4] {'chip'}, dimensions={0} | all-to-all | bytes 2359296 | tf_op jit(solution)/shard_map/cond/branch_1_fun/plane/all_to_all | solution.py:261
  46.9 0.0 collective-permute-start
  46.9 3.2 %collective-permute-done.rest_4_.rest_5_.rest_6_.rest_7_ = bf16[4,6,3,64,128]{4,3,2,1,0:T(8,128)(2,1)} collective-permute-done((bf16[4,6,3,64,128]{4,3,2,1,0:T(8,128)(2,1)}, bf16[4,6,3,64,128]{4,3,2,1,0:T(8,128)(2,1)}, u32[]{:S(2)}, u32[]{:S(2)}) %collective-permute-start) | collective-permute-done | bytes 1179680 | tf_op jit(solution)/shard_map/cond/branch_1_fun/cores2/ppermute | solution.py:241
  50.1 5.9 %attend.2 = bf16[16,3,64,128]{3,2,1,0:T(8,128)(2,1)S(1)} custom-call(s32[3]{0:T(128)S(1)} %get-tuple-element.24.me_ref, s32[4,16,128]{2,1,0:T(8,128)S(1)} %get-tuple-element.25.table_ref, bf16[4,6,3,64,128]{4,3,2,1,0:T(8,128)(2,1)} %all_to_all.9.rest_0_.rest_1_.rest_2_.rest_3_, bf16[4,6,3,64,128]{4,3,2,1,0:T(8,128)(2,1)} %all_to_all.9.rest_0_.rest_1_.rest_2_.rest_3_, ...), custom_call_target="tpu_custom_call" | custom-call | flops 1 | bytes 1 | tf_op jit(solution)/shard_map/cond/branch_1_fun/heads2/attend/pallas_call | solution.py:211
  56.2 0.0 collective-permute-done.9.rest_3_
  56.2 0.3 collective-permute-done.8.rest_2_
  56.5 0.0 collective-permute-done.7.rest_1_
  56.5 0.0 collective-permute-start.10
  56.5 0.5 collective-permute-start.11
  57.0 0.0 collective-permute-start.12
  57.0 1.2 %collective-permute-done.10.rest_5_ = bf16[4,2,3,64,128]{4,3,2,1,0:T(8,128)(2,1)S(1)} collective-permute-done((bf16[4,2,3,64,128]{4,3,2,1,0:T(8,128)(2,1)S(1)}, bf16[4,2,3,64,128]{4,3,2,1,0:T(8,128)(2,1)S(1)}, u32[]{:S(2)}, u32[]{:S(2)}) %collective-permute-start.10) | collective-permute-done | bytes 393248 | tf_op jit(solution)/shard_map/cores01/ppermute | solution.py:241
  58.2 0.6 collective-permute-done.11.rest_6_
  58.8 0.6 collective-permute-done.12.rest_7_
  59.4 6.4 %attend.3 = bf16[16,3,64,128]{3,2,1,0:T(8,128)(2,1)S(1)} custom-call(s32[3]{0:T(128)S(1)} %pad_add_fusion.me_ref, s32[4,16,128]{2,1,0:T(8,128)} %copy-done.2, bf16[4,6,3,64,128]{4,3,2,1,0:T(8,128)(2,1)} %get-tuple-element.58.rest_0_, bf16[4,2,3,64,128]{4,3,2,1,0:T(8,128)(2,1)S(1)} %collective-permute-done.7.rest_1_, ...), custom_call_target="tpu_custom_call", output_to_operand_aliasing={{}: (10, {})} | custom-call | flops 1 | bytes 1 | tf_op jit(solution)/shard_map/heads0/attend/pallas_call | solution.py:211
  65.8 32.9 %all_to_all.10 = bf16[16,3,64,128]{3,2,1,0:T(8,128)(2,1)S(1)} all-to-all(bf16[16,3,64,128]{3,2,1,0:T(8,128)(2,1)S(1)} %attend.3), channel_id=1, replica_groups=mesh['chip'=4,'core'=2,'head'=4] {'head','chip'}, dimensions={0} | all-to-all | bytes 1572864 | tf_op jit(solution)/shard_map/all_to_all | solution.py:305
  98.7 0.1 pad_maximum_fusion.1
  98.8 1.2 %copy.16 = bf16[128,3072]{1,0:T(8,128)(2,1)} copy(bf16[128,3072]{0,1:T(8,128)(2,1)S(1)} %bitcast.59) | data formatting | bytes 1572864 | tf_op jit(solution)/shard_map/transpose | solution.py:315
  (11 shorter events, 0.2 us)
Async XLA Ops:
  0.0 1.9 %copy-start = (s32[12,4,8]{0,2,1:T(8,128)S(1)}, s32[12,4,8]{0,2,1:T(8,128)}, u32[]{:S(2)}) copy-start(s32[12,4,8]{0,2,1:T(8,128)} %param.6) | copy-start | bytes 4612
  0.0 1.9 %copy-start.1 = (s32[12,4]{0,1:T(4,128)S(1)}, s32[12,4]{0,1:T(4,128)}, u32[]{:S(2)}) copy-start(s32[12,4]{0,1:T(4,128)} %param.7) | copy-start | bytes 580
  3.4 26.3 %collective-permute-start.4 = (bf16[4,1,3,64,128]{4,3,2,1,0:T(8,128)(2,1)S(1)}, bf16[4,1,3,64,128]{4,3,2,1,0:T(8,128)(2,1)S(1)}, u32[]{:S(2)}, u32[]{:S(2)}) collective-permute-start(bf16[4,1,3,64,128]{4,3,2,1,0:T(8,128)(2,1)S(1)} %get-tuple-element.50), channel_id=1, source_target_pairs={{0,1},{1,0},{2,3},{3,2},{4,5},{5,4},{6,7},{7,6},{8,9},{9,8},{10,11... | collective-permute-start | bytes 589832 | tf_op jit(solution)/shard_map/z2/ppermute | solution.py:241
  6.5 23.9 %collective-permute-start.5 = (bf16[4,1,3,64,128]{4,3,2,1,0:T(8,128)(2,1)S(1)}, bf16[4,1,3,64,128]{4,3,2,1,0:T(8,128)(2,1)S(1)}, u32[]{:S(2)}, u32[]{:S(2)}) collective-permute-start(bf16[4,1,3,64,128]{4,3,2,1,0:T(8,128)(2,1)S(1)} %get-tuple-element.51), channel_id=1, source_target_pairs={{0,2},{1,3},{2,0},{3,1},{4,6},{5,7},{6,4},{7,5},{8,10},{9,11},{10,... | collective-permute-start | bytes 589832 | tf_op jit(solution)/shard_map/z2/ppermute | solution.py:241
  9.1 21.3 %collective-permute-start.6 = (bf16[4,1,3,64,128]{4,3,2,1,0:T(8,128)(2,1)S(1)}, bf16[4,1,3,64,128]{4,3,2,1,0:T(8,128)(2,1)S(1)}, u32[]{:S(2)}, u32[]{:S(2)}) collective-permute-start(bf16[4,1,3,64,128]{4,3,2,1,0:T(8,128)(2,1)S(1)} %get-tuple-element.52), channel_id=1, source_target_pairs={{0,3},{1,2},{2,1},{3,0},{4,7},{5,6},{6,5},{7,4},{8,11},{9,10},{10,... | collective-permute-start | bytes 589832 | tf_op jit(solution)/shard_map/z2/ppermute | solution.py:241
  9.1 8.3 %collective-permute-start.1 = (bf16[1168,128]{1,0:T(8,128)(2,1)S(1)}, bf16[1168,128]{1,0:T(8,128)(2,1)S(1)}, u32[]{:S(2)}, u32[]{:S(2)}) collective-permute-start(bf16[1168,128]{1,0:T(8,128)(2,1)S(1)} %get-tuple-element.46), channel_id=1, source_target_pairs={{0,8},{8,0},{16,24},{24,16},{1,9},{9,1},{17,25},{25,17},{2,10},{10... | collective-permute-start | bytes 897032 | tf_op jit(solution)/shard_map/p01/ppermute | solution.py:241
  10.8 9.0 %collective-permute-start.2 = (bf16[1168,128]{1,0:T(8,128)(2,1)S(1)}, bf16[1168,128]{1,0:T(8,128)(2,1)S(1)}, u32[]{:S(2)}, u32[]{:S(2)}) collective-permute-start(bf16[1168,128]{1,0:T(8,128)(2,1)S(1)} %get-tuple-element.47), channel_id=1, source_target_pairs={{0,16},{8,24},{16,0},{24,8},{1,17},{9,25},{17,1},{25,9},{2,18},{10... | collective-permute-start | bytes 897032 | tf_op jit(solution)/shard_map/p01/ppermute | solution.py:241
  17.3 8.2 %collective-permute-start.3 = (bf16[1168,128]{1,0:T(8,128)(2,1)S(1)}, bf16[1168,128]{1,0:T(8,128)(2,1)S(1)}, u32[]{:S(2)}, u32[]{:S(2)}) collective-permute-start(bf16[1168,128]{1,0:T(8,128)(2,1)S(1)} %get-tuple-element.48), channel_id=1, source_target_pairs={{0,24},{8,16},{16,8},{24,0},{1,25},{9,17},{17,9},{25,1},{2,26},{10... | collective-permute-start | bytes 897032 | tf_op jit(solution)/shard_map/p01/ppermute | solution.py:241
  25.7 30.8 %collective-permute-start.7 = (bf16[4,2,3,64,128]{4,3,2,1,0:T(8,128)(2,1)S(1)}, bf16[4,2,3,64,128]{4,3,2,1,0:T(8,128)(2,1)S(1)}, u32[]{:S(2)}, u32[]{:S(2)}) collective-permute-start(bf16[4,2,3,64,128]{4,3,2,1,0:T(8,128)(2,1)S(1)} %get-tuple-element.93), channel_id=1, source_target_pairs={{0,1},{1,0},{2,3},{3,2},{4,5},{5,4},{6,7},{7,6},{8,9},{9,8},{10,11... | collective-permute-start | bytes 1179656 | tf_op jit(solution)/shard_map/z01/ppermute | solution.py:241
  26.1 30.4 %collective-permute-start.8 = (bf16[4,2,3,64,128]{4,3,2,1,0:T(8,128)(2,1)S(1)}, bf16[4,2,3,64,128]{4,3,2,1,0:T(8,128)(2,1)S(1)}, u32[]{:S(2)}, u32[]{:S(2)}) collective-permute-start(bf16[4,2,3,64,128]{4,3,2,1,0:T(8,128)(2,1)S(1)} %get-tuple-element.94), channel_id=1, source_target_pairs={{0,2},{1,3},{2,0},{3,1},{4,6},{5,7},{6,4},{7,5},{8,10},{9,11},{10,... | collective-permute-start | bytes 1179656 | tf_op jit(solution)/shard_map/z01/ppermute | solution.py:241
  29.7 26.5 %collective-permute-start.9 = (bf16[4,2,3,64,128]{4,3,2,1,0:T(8,128)(2,1)S(1)}, bf16[4,2,3,64,128]{4,3,2,1,0:T(8,128)(2,1)S(1)}, u32[]{:S(2)}, u32[]{:S(2)}) collective-permute-start(bf16[4,2,3,64,128]{4,3,2,1,0:T(8,128)(2,1)S(1)} %pad_maximum_fusion.4), channel_id=1, source_target_pairs={{0,3},{1,2},{2,1},{3,0},{4,7},{5,6},{6,5},{7,4},{8,11},{9,10},{10,... | collective-permute-start | bytes 1179656 | tf_op jit(solution)/shard_map/z01/ppermute | solution.py:241
  30.4 0.6 copy-start.2
  46.9 3.2 %collective-permute-start = (bf16[4,6,3,64,128]{4,3,2,1,0:T(8,128)(2,1)}, bf16[4,6,3,64,128]{4,3,2,1,0:T(8,128)(2,1)}, u32[]{:S(2)}, u32[]{:S(2)}) collective-permute-start(bf16[4,6,3,64,128]{4,3,2,1,0:T(8,128)(2,1)} %all_to_all.9.rest_0_.rest_1_.rest_2_.rest_3_), channel_id=1, source_target_pairs={{0,4},{4,0},{1,5},{5,1},{2,6},{6,2},{3,7},{7,3},{8,12},{12,8},{9,1... | collective-permute-start | bytes 3538952 | tf_op jit(solution)/shard_map/cond/branch_1_fun/cores2/ppermute | solution.py:241
  56.5 1.7 %collective-permute-start.10 = (bf16[4,2,3,64,128]{4,3,2,1,0:T(8,128)(2,1)S(1)}, bf16[4,2,3,64,128]{4,3,2,1,0:T(8,128)(2,1)S(1)}, u32[]{:S(2)}, u32[]{:S(2)}) collective-permute-start(bf16[4,2,3,64,128]{4,3,2,1,0:T(8,128)(2,1)S(1)} %collective-permute-done.7.rest_1_), channel_id=1, source_target_pairs={{0,4},{4,0},{1,5},{5,1},{2,6},{6,2},{3,7},{7,3},{8,12},{12,8},{9,1... | collective-permute-start | bytes 1179656 | tf_op jit(solution)/shard_map/cores01/ppermute | solution.py:241
  56.5 2.3 %collective-permute-start.11 = (bf16[4,2,3,64,128]{4,3,2,1,0:T(8,128)(2,1)S(1)}, bf16[4,2,3,64,128]{4,3,2,1,0:T(8,128)(2,1)S(1)}, u32[]{:S(2)}, u32[]{:S(2)}) collective-permute-start(bf16[4,2,3,64,128]{4,3,2,1,0:T(8,128)(2,1)S(1)} %collective-permute-done.8.rest_2_), channel_id=1, source_target_pairs={{0,4},{4,0},{1,5},{5,1},{2,6},{6,2},{3,7},{7,3},{8,12},{12,8},{9,1... | collective-permute-start | bytes 1179656 | tf_op jit(solution)/shard_map/cores01/ppermute | solution.py:241
  57.0 2.3 %collective-permute-start.12 = (bf16[4,2,3,64,128]{4,3,2,1,0:T(8,128)(2,1)S(1)}, bf16[4,2,3,64,128]{4,3,2,1,0:T(8,128)(2,1)S(1)}, u32[]{:S(2)}, u32[]{:S(2)}) collective-permute-start(bf16[4,2,3,64,128]{4,3,2,1,0:T(8,128)(2,1)S(1)} %collective-permute-done.9.rest_3_), channel_id=1, source_target_pairs={{0,4},{4,0},{1,5},{5,1},{2,6},{6,2},{3,7},{7,3},{8,12},{12,8},{9,1... | collective-permute-start | bytes 1179656 | tf_op jit(solution)/shard_map/cores01/ppermute | solution.py:241

commit v6 on v5

--- a/solution.py
+++ b/solution.py
@@ -190,9 +190,7 @@
     lax.fori_loop(0, blocks // ROWS, group, 0)
 
 
-def attend(
-    me, table, mine, other, held, *, entries, j, near, per_chip, chips_seq, head_count
-):
+def attend(me, table, mine, other, *, entries, j, near, per_chip, chips_seq, head_count):
     blocks = chips_seq * head_count
     block = mine[0][0].shape[-2:]
     head_size, tokens = block
@@ -203,11 +201,7 @@
     in_specs = [spec(at, 3) for _, at in mine] + [spec(at, 2) for _, at in other]
     operands = [me, table] + [array for array, _ in mine + other]
     dtype = mine[0][0].dtype
-    aliases = {}
-    if held is not None:
-        in_specs.append(pl.BlockSpec(memory_space=pl.ANY))
-        aliases = {len(operands): 0}
-        operands.append(held)
+    count = mine[-1][0].shape[1] - mine[-1][1] if near else 1
     return pl.pallas_call(
         functools.partial(
             attend_kernel,
@@ -216,16 +210,15 @@
         ),
         grid_spec=pltpu.PrefetchScalarGridSpec(
             num_scalar_prefetch=2,
-            grid=(mine[-1][0].shape[1] - mine[-1][1],) if near else (1,),
+            grid=(count,),
             in_specs=in_specs,
-            out_specs=pl.BlockSpec((blocks, 1, *block), lambda i, *_: (0, j + i, 0, 0)),
+            out_specs=pl.BlockSpec((blocks, 1, *block), lambda i, *_: (0, i, 0, 0)),
             scratch_shapes=[
                 pltpu.VMEM((blocks, *block), dtype),
                 pltpu.VMEM((2 * blocks, 2, *block), dtype),
             ],
         ),
-        out_shape=jax.ShapeDtypeStruct((blocks, per_chip, *block), dtype),
-        input_output_aliases=aliases,
+        out_shape=jax.ShapeDtypeStruct((blocks, count, *block), dtype),
         compiler_params=pltpu.CompilerParams(vmem_limit_bytes=48 << 20),
         cost_estimate=pl.CostEstimate(flops=1, transcendentals=1, bytes_accessed=1),
         name="attend",
@@ -264,9 +257,9 @@
         with jax.named_scope(name):
             return swap(value, "core", 1)
 
-    def heads(c, mine, other, held, table, near):
+    def heads(c, mine, other, table, near):
         with jax.named_scope(f"heads{c}"):
-            return attend(me, table, mine, other, held, entries=entries, j=c, near=near, **sizes)
+            return attend(me, table, mine, other, entries=entries, j=c, near=near, **sizes)
 
     last, each = per_chip - 1, range(head_count)
     packed = pack(me, *qkv, key_lists.transpose(1, 2, 0), list_counts.T, head_size=head_size, **sizes)
@@ -277,7 +270,7 @@
         plane = over_p(jnp.concatenate([jnp.stack(singles, axis=1)[:, :, 0], own], axis=1), "plane")
         other = over_cores(plane, "cores2")
         held = heads(
-            last, [(plane, kz) for kz in each], [(other, kz) for kz in each], None, table, False
+            last, [(plane, kz) for kz in each], [(other, kz) for kz in each], table, False
         )
         return plane, other, held
 
@@ -301,16 +294,13 @@
     rest = [sync(part, held)[0] for part in rest]
     mine = [(plane, head_count)] + [(part, 0) for part in rest]
     other = [(other, head_count)] + [(over_cores(part, "cores01"), 0) for part in rest]
-    held = heads(0, mine, other, held, table, True)
-    back = lax.all_to_all(held, ("head", "chip"), split_axis=0, concat_axis=0, tiled=True)
-    back = back.reshape(head_count, chips_seq, per_chip, head_size, tokens)
-    paired = per_chip // 2 * 2
+    held = [heads(0, mine, other, table, True), held]
+    held = [
+        lax.all_to_all(part, ("head", "chip"), split_axis=0, concat_axis=0, tiled=True)
+        for part in held
+    ]
     back = jnp.concatenate(
-        [
-            back[:, :, :paired].reshape(head_count, chips_seq * paired, head_size, tokens),
-            back[:, :, paired:].reshape(head_count, -1, head_size, tokens),
-        ],
-        axis=1,
+        [part.reshape(head_count, -1, head_size, tokens) for part in held], axis=1
     )
     return back.reshape(width, tokens).T
 
@@ -412,7 +402,7 @@
     odd = (group_heads // chips_seq) % 2 == 1
     tokens = projected.shape[0] // (seq_count * head_count)
     fit = head_count * (key_lists.shape[2] + 1) <= tokens and group_heads <= tokens
-    return small and odd and fit and chips_seq % 2 == 0 and ROWS % chips_seq == 0
+    return small and odd and fit and group_heads > chips_seq and chips_seq % 2 == 0 and ROWS % chips_seq == 0
 
 
 def solution(mesh):

time: 101 us -> 96.1 us (0.951)
  blocking collectives: 48.6 us -> 38.6 us
  starting transfers between devices: 16.4 us -> 22.2 us
  Pallas kernels: 13.8 us -> 15.1 us
    all_to_all x1, blocking collectives: 32.9 us -> 22.9 us  [on_pair(): lax.all_to_all(part, ('head', 'chip'), split_axis=0, concat_axis=0, tiled...]
    all_to_all x0 -> x1, starting transfers between devices: none -> 5.65 us  [on_pair(): lax.all_to_all(part, ('head', 'chip'), split_axis=0, concat_axis=0, tiled...]
    pallas_call x2, Pallas kernels: 12.3 us -> 13.6 us  [attend(): pl.pallas_call(functools.partial(attend_kernel, scale=LOG2E / math.sqrt(h...]
  transfers between devices with their start and end apart: 13 -> 14, of which waited for: 7 -> 6; matrix products, arithmetic and copies ran while one was open for 1% -> 1% of each run, Pallas kernels for 6% -> 14%
where the time goes in v6:
time: 96.1 us; the launch traced here: 95.9 us
  blocking collectives  38.6 us (40%)
  starting transfers between devices  22.2 us (23%)
  Pallas kernels  15.1 us (16%)
  waiting for transfers between devices  15 us (16%)
  local copies, waits for them, and re-layouts  3.56 us (4%)
    all_to_all x1, blocking collectives, on_pair(): lax.all_to_all(part, ('head', 'chip'), split_axis=0, concat_axis=0, tiled...  22.9 us
    ppermute x13, starting transfers between devices, swap(): return lax.ppermute(value, axis, [(i, i ^ k) for i in range(size)])  16.5 us
    all_to_all x1, blocking collectives, over_p(): lax.all_to_all(value, 'chip', split_axis=0, concat_axis=0, tiled=True)  15.7 us
    ppermute x13, waiting for transfers between devices, swap(): return lax.ppermute(value, axis, [(i, i ^ k) for i in range(size)])  15 us
    pallas_call x2, Pallas kernels, attend(): pl.pallas_call(functools.partial(attend_kernel, scale=LOG2E / math.sqrt(h...  13.6 us
    all_to_all x1, starting transfers between devices, on_pair(): lax.all_to_all(part, ('head', 'chip'), split_axis=0, concat_axis=0, tiled...  5.65 us
  transfers between devices with their start and end apart: 14, of which 6 were waited for; matrix products, arithmetic and copies ran while one was open for 1% of the time, Pallas kernels for 14%

profile of v6, /device:TPU:0, one launch (start us, length us, event | category | flops | bytes accessed | tf_op | source)
XLA Modules:
  0.0 95.9 jit_solution(6815536149091481081)
XLA Ops:
  0.0 0.0 copy-start
  0.0 0.0 copy-start.1
  0.0 1.8 %slice_bitcast_fusion = (bf16[128,3072]{1,0:T(8,128)(2,1)S(1)}, bf16[128,3072]{1,0:T(8,128)(2,1)S(1)}, bf16[128,3072]{1,0:T(8,128)(2,1)S(1)}) fusion(bf16[128,3,3072]{2,0,1:T(8,128)(2,1)} %param.5), kind=kLoop, calls=%fused_computation.3 | loop fusion | bytes 4718592 | tf_op jit(solution)/shard_map/squeeze | solution.py:245
  1.8 0.1 pad_add_fusion.me_ref
  1.9 0.0 copy-done
  1.9 0.0 copy-done.1
  1.9 1.5 %pack.1 = (bf16[4,1,3,64,128]{4,3,2,1,0:T(8,128)(2,1)S(1)}, bf16[4,1,3,64,128]{4,3,2,1,0:T(8,128)(2,1)S(1)}, bf16[4,1,3,64,128]{4,3,2,1,0:T(8,128)(2,1)S(1)}, bf...) custom-call(s32[3]{0:T(128)S(1)} %pad_add_fusion.me_ref, ...), custom_call_target="tpu_custom_call" | custom-call | tf_op jit(solution)/shard_map/pack/pallas_call | solution.py:87
  3.4 3.1 %collective-permute-start.4 = (bf16[4,1,3,64,128]{4,3,2,1,0:T(8,128)(2,1)S(1)}, bf16[4,1,3,64,128]{4,3,2,1,0:T(8,128)(2,1)S(1)}, u32[]{:S(2)}, u32[]{:S(2)}) collective-permute-start(bf16[4,1,3,64,128]{4,3,2,1,0:T(8,128)(2,1)S(1)} %get-tuple-element.50), channel_id=1, source_target_pairs={{0,1},{1,0},{2,3},{3,2},{4,5},{5,4},{6,7},{7,6},{8,9},{9,8},{10,11... | collective-permute-start | bytes 589832 | tf_op jit(solution)/shard_map/z2/ppermute | solution.py:234
  6.5 2.6 %collective-permute-start.5 = (bf16[4,1,3,64,128]{4,3,2,1,0:T(8,128)(2,1)S(1)}, bf16[4,1,3,64,128]{4,3,2,1,0:T(8,128)(2,1)S(1)}, u32[]{:S(2)}, u32[]{:S(2)}) collective-permute-start(bf16[4,1,3,64,128]{4,3,2,1,0:T(8,128)(2,1)S(1)} %get-tuple-element.51), channel_id=1, source_target_pairs={{0,2},{1,3},{2,0},{3,1},{4,6},{5,7},{6,4},{7,5},{8,10},{9,11},{10,... | collective-permute-start | bytes 589832 | tf_op jit(solution)/shard_map/z2/ppermute | solution.py:234
  9.1 0.0 collective-permute-start.6
  9.1 1.7 %collective-permute-start.1 = (bf16[1168,128]{1,0:T(8,128)(2,1)S(1)}, bf16[1168,128]{1,0:T(8,128)(2,1)S(1)}, u32[]{:S(2)}, u32[]{:S(2)}) collective-permute-start(bf16[1168,128]{1,0:T(8,128)(2,1)S(1)} %get-tuple-element.46), channel_id=1, source_target_pairs={{0,8},{8,0},{16,24},{24,16},{1,9},{9,1},{17,25},{25,17},{2,10},{10... | collective-permute-start | bytes 897032 | tf_op jit(solution)/shard_map/p01/ppermute | solution.py:234
  10.8 1.5 %collective-permute-start.2 = (bf16[1168,128]{1,0:T(8,128)(2,1)S(1)}, bf16[1168,128]{1,0:T(8,128)(2,1)S(1)}, u32[]{:S(2)}, u32[]{:S(2)}) collective-permute-start(bf16[1168,128]{1,0:T(8,128)(2,1)S(1)} %get-tuple-element.47), channel_id=1, source_target_pairs={{0,16},{8,24},{16,0},{24,8},{1,17},{9,25},{17,1},{25,9},{2,18},{10... | collective-permute-start | bytes 897032 | tf_op jit(solution)/shard_map/p01/ppermute | solution.py:234
  12.3 0.5 slice.119
  13.5 3.8 %collective-permute-done.1 = bf16[1168,128]{1,0:T(8,128)(2,1)S(1)} collective-permute-done((bf16[1168,128]{1,0:T(8,128)(2,1)S(1)}, bf16[1168,128]{1,0:T(8,128)(2,1)S(1)}, u32[]{:S(2)}, u32[]{:S(2)}) %collective-permute-start.1) | collective-permute-done | bytes 299040 | tf_op jit(solution)/shard_map/p01/ppermute | solution.py:234
  17.3 2.4 %collective-permute-start.3 = (bf16[1168,128]{1,0:T(8,128)(2,1)S(1)}, bf16[1168,128]{1,0:T(8,128)(2,1)S(1)}, u32[]{:S(2)}, u32[]{:S(2)}) collective-permute-start(bf16[1168,128]{1,0:T(8,128)(2,1)S(1)} %get-tuple-element.48), channel_id=1, source_target_pairs={{0,24},{8,16},{16,8},{24,0},{1,25},{9,17},{17,9},{25,1},{2,26},{10... | collective-permute-start | bytes 897032 | tf_op jit(solution)/shard_map/p01/ppermute | solution.py:234
  19.8 0.0 collective-permute-done.2
  19.8 5.7 %collective-permute-done.3 = bf16[1168,128]{1,0:T(8,128)(2,1)S(1)} collective-permute-done((bf16[1168,128]{1,0:T(8,128)(2,1)S(1)}, bf16[1168,128]{1,0:T(8,128)(2,1)S(1)}, u32[]{:S(2)}, u32[]{:S(2)}) %collective-permute-start.3) | collective-permute-done | bytes 299040 | tf_op jit(solution)/shard_map/p01/ppermute | solution.py:234
  25.6 0.1 pad_maximum_fusion.2
  25.7 0.4 collective-permute-start.7
  26.1 3.5 %collective-permute-start.8 = (bf16[4,2,3,64,128]{4,3,2,1,0:T(8,128)(2,1)S(1)}, bf16[4,2,3,64,128]{4,3,2,1,0:T(8,128)(2,1)S(1)}, u32[]{:S(2)}, u32[]{:S(2)}) collective-permute-start(bf16[4,2,3,64,128]{4,3,2,1,0:T(8,128)(2,1)S(1)} %get-tuple-element.94), channel_id=1, source_target_pairs={{0,2},{1,3},{2,0},{3,1},{4,6},{5,7},{6,4},{7,5},{8,10},{9,11},{10,... | collective-permute-start | bytes 1179656 | tf_op jit(solution)/shard_map/z01/ppermute | solution.py:234
  29.6 0.1 pad_maximum_fusion.4
  29.7 0.0 collective-permute-done.4
  29.7 0.6 collective-permute-start.9
  30.3 0.0 collective-permute-done.5
  30.3 0.0 collective-permute-done.6
  30.4 25.1 %conditional.1 = (bf16[4,6,3,64,128]{4,3,2,1,0:T(8,128)(2,1)}, bf16[4,6,3,64,128]{4,3,2,1,0:T(8,128)(2,1)}, bf16[16,1,64,128]{3,2,1,0:T(8,128)(2,1)}) conditional(s32[]{:T(128)} %bitcast.25, () %tuple.17, (bf16[4,1,3,64,128]{4,3,2,1,0:T(8,128)(2,1)S(1)}, bf16[4,1,3,64,128]{4,3,2,1,0:T(8,128)(2,1)S(1)}, bf16[4,1,3,64,128]{4,3,2,1,0:T(8,128)(2,1)S(1)}, ...), branch_computations={%region_0.0_spmd, %region_1.0_spmd} | conditional | flops 1769473 | bytes 11010113 | solution.py:293
  30.4 0.1 maximum_bitcast_fusion
  30.5 0.1 pad_maximum_fusion
  30.6 15.7 %all_to_all.14.rest_0_.rest_1_.rest_2_.rest_3_ = bf16[4,6,3,64,128]{4,3,2,1,0:T(8,128)(2,1)} all-to-all(bf16[4,6,3,64,128]{4,3,2,1,0:T(8,128)(2,1)S(1)} %pad_maximum_fusion), channel_id=1, replica_groups=mesh['chip'=4,'core'=2,'head'=4] {'chip'}, dimensions={0} | all-to-all | bytes 2359296 | tf_op jit(solution)/shard_map/cond/branch_1_fun/plane/all_to_all | solution.py:254
  46.3 0.0 collective-permute-start
  46.3 3.2 %collective-permute-done.rest_4_.rest_5_.rest_6_.rest_7_ = bf16[4,6,3,64,128]{4,3,2,1,0:T(8,128)(2,1)} collective-permute-done((bf16[4,6,3,64,128]{4,3,2,1,0:T(8,128)(2,1)}, bf16[4,6,3,64,128]{4,3,2,1,0:T(8,128)(2,1)}, u32[]{:S(2)}, u32[]{:S(2)}) %collective-permute-start) | collective-permute-done | bytes 1179680 | tf_op jit(solution)/shard_map/cond/branch_1_fun/cores2/ppermute | solution.py:234
  49.5 5.9 %attend.2 = bf16[16,1,64,128]{3,2,1,0:T(8,128)(2,1)} custom-call(s32[3]{0:T(128)S(1)} %get-tuple-element.24.me_ref, s32[4,16,128]{2,1,0:T(8,128)S(1)} %get-tuple-element.25.table_ref, bf16[4,6,3,64,128]{4,3,2,1,0:T(8,128)(2,1)} %all_to_all.14.rest_0_.rest_1_.rest_2_.rest_3_, bf16[4,6,3,64,128]{4,3,2,1,0:T(8,128)(2,1)} %all_to_all.14.rest_0_.rest_1_.rest_2_.rest_3_, ...), custom_call_target="tpu_custom_call" | custom-call | flops 1 | bytes 1 | tf_op jit(solution)/shard_map/cond/branch_1_fun/heads2/attend/pallas_call | solution.py:205
  55.4 5.7 %all-to-all-start.2 = ((bf16[16,1,64,128]{3,2,1,0:T(8,128)(2,1)}), bf16[16,1,64,128]{3,2,1,0:T(8,128)(2,1)S(1)}, u32[]{:S(2)}, u32[]{:S(2)}) async-start(bf16[16,1,64,128]{3,2,1,0:T(8,128)(2,1)} %get-tuple-element.59), calls=%async_computation.2 | async-start | bytes 524288 | tf_op jit(solution)/shard_map/all_to_all | solution.py:299
  61.1 0.0 collective-permute-done.9.rest_3_
  61.1 0.0 collective-permute-done.8.rest_2_
  61.1 0.0 collective-permute-done.7.rest_1_
  61.1 0.1 collective-permute-start.10
  61.2 0.5 collective-permute-start.11
  61.7 0.1 collective-permute-start.12
  61.8 1.1 %collective-permute-done.10.rest_5_ = bf16[4,2,3,64,128]{4,3,2,1,0:T(8,128)(2,1)S(1)} collective-permute-done((bf16[4,2,3,64,128]{4,3,2,1,0:T(8,128)(2,1)S(1)}, bf16[4,2,3,64,128]{4,3,2,1,0:T(8,128)(2,1)S(1)}, u32[]{:S(2)}, u32[]{:S(2)}) %collective-permute-start.10) | collective-permute-done | bytes 393248 | tf_op jit(solution)/shard_map/cores01/ppermute | solution.py:234
  62.9 0.6 collective-permute-done.11.rest_6_
  63.5 0.6 collective-permute-done.12.rest_7_
  64.0 7.7 %attend.3 = bf16[16,2,64,128]{3,2,1,0:T(8,128)(2,1)S(1)} custom-call(s32[3]{0:T(128)S(1)} %pad_add_fusion.me_ref, s32[4,16,128]{2,1,0:T(8,128)S(1)} %maximum_convert_fusion.table_ref, bf16[4,6,3,64,128]{4,3,2,1,0:T(8,128)(2,1)} %get-tuple-element.58.rest_0_, bf16[4,2,3,64,128]{4,3,2,1,0:T(8,128)(2,1)S(1)} %collective-permute-done.7.rest_1_, ...), custom_call_target="tpu_custom_call" | custom-call | flops 1 | bytes 1 | tf_op jit(solution)/shard_map/heads0/attend/pallas_call | solution.py:205
  71.8 0.0 all-to-all-done.2
  71.8 22.9 %all_to_all.15 = bf16[16,2,64,128]{3,2,1,0:T(8,128)(2,1)S(1)} all-to-all(bf16[16,2,64,128]{3,2,1,0:T(8,128)(2,1)S(1)} %attend.3), channel_id=1, replica_groups=mesh['chip'=4,'core'=2,'head'=4] {'head','chip'}, dimensions={0} | all-to-all | bytes 1048576 | tf_op jit(solution)/shard_map/all_to_all | solution.py:299
  94.6 0.1 pad_maximum_fusion.1
  94.7 1.2 %copy.13 = bf16[128,3072]{1,0:T(8,128)(2,1)} copy(bf16[128,3072]{0,1:T(8,128)(2,1)S(1)} %bitcast.53) | data formatting | bytes 1572864 | tf_op jit(solution)/shard_map/transpose | solution.py:305
  (9 shorter events, 0.1 us)
Async XLA Ops:
  0.0 1.9 %copy-start = (s32[12,4,8]{0,2,1:T(8,128)S(1)}, s32[12,4,8]{0,2,1:T(8,128)}, u32[]{:S(2)}) copy-start(s32[12,4,8]{0,2,1:T(8,128)} %param.6) | copy-start | bytes 4612
  0.0 1.9 %copy-start.1 = (s32[12,4]{0,1:T(4,128)S(1)}, s32[12,4]{0,1:T(4,128)}, u32[]{:S(2)}) copy-start(s32[12,4]{0,1:T(4,128)} %param.7) | copy-start | bytes 580
  3.4 26.3 %collective-permute-start.4 = (bf16[4,1,3,64,128]{4,3,2,1,0:T(8,128)(2,1)S(1)}, bf16[4,1,3,64,128]{4,3,2,1,0:T(8,128)(2,1)S(1)}, u32[]{:S(2)}, u32[]{:S(2)}) collective-permute-start(bf16[4,1,3,64,128]{4,3,2,1,0:T(8,128)(2,1)S(1)} %get-tuple-element.50), channel_id=1, source_target_pairs={{0,1},{1,0},{2,3},{3,2},{4,5},{5,4},{6,7},{7,6},{8,9},{9,8},{10,11... | collective-permute-start | bytes 589832 | tf_op jit(solution)/shard_map/z2/ppermute | solution.py:234
  6.5 23.8 %collective-permute-start.5 = (bf16[4,1,3,64,128]{4,3,2,1,0:T(8,128)(2,1)S(1)}, bf16[4,1,3,64,128]{4,3,2,1,0:T(8,128)(2,1)S(1)}, u32[]{:S(2)}, u32[]{:S(2)}) collective-permute-start(bf16[4,1,3,64,128]{4,3,2,1,0:T(8,128)(2,1)S(1)} %get-tuple-element.51), channel_id=1, source_target_pairs={{0,2},{1,3},{2,0},{3,1},{4,6},{5,7},{6,4},{7,5},{8,10},{9,11},{10,... | collective-permute-start | bytes 589832 | tf_op jit(solution)/shard_map/z2/ppermute | solution.py:234
  9.1 21.3 %collective-permute-start.6 = (bf16[4,1,3,64,128]{4,3,2,1,0:T(8,128)(2,1)S(1)}, bf16[4,1,3,64,128]{4,3,2,1,0:T(8,128)(2,1)S(1)}, u32[]{:S(2)}, u32[]{:S(2)}) collective-permute-start(bf16[4,1,3,64,128]{4,3,2,1,0:T(8,128)(2,1)S(1)} %get-tuple-element.52), channel_id=1, source_target_pairs={{0,3},{1,2},{2,1},{3,0},{4,7},{5,6},{6,5},{7,4},{8,11},{9,10},{10,... | collective-permute-start | bytes 589832 | tf_op jit(solution)/shard_map/z2/ppermute | solution.py:234
  9.1 8.3 %collective-permute-start.1 = (bf16[1168,128]{1,0:T(8,128)(2,1)S(1)}, bf16[1168,128]{1,0:T(8,128)(2,1)S(1)}, u32[]{:S(2)}, u32[]{:S(2)}) collective-permute-start(bf16[1168,128]{1,0:T(8,128)(2,1)S(1)} %get-tuple-element.46), channel_id=1, source_target_pairs={{0,8},{8,0},{16,24},{24,16},{1,9},{9,1},{17,25},{25,17},{2,10},{10... | collective-permute-start | bytes 897032 | tf_op jit(solution)/shard_map/p01/ppermute | solution.py:234
  10.8 9.0 %collective-permute-start.2 = (bf16[1168,128]{1,0:T(8,128)(2,1)S(1)}, bf16[1168,128]{1,0:T(8,128)(2,1)S(1)}, u32[]{:S(2)}, u32[]{:S(2)}) collective-permute-start(bf16[1168,128]{1,0:T(8,128)(2,1)S(1)} %get-tuple-element.47), channel_id=1, source_target_pairs={{0,16},{8,24},{16,0},{24,8},{1,17},{9,25},{17,1},{25,9},{2,18},{10... | collective-permute-start | bytes 897032 | tf_op jit(solution)/shard_map/p01/ppermute | solution.py:234
  17.3 8.2 %collective-permute-start.3 = (bf16[1168,128]{1,0:T(8,128)(2,1)S(1)}, bf16[1168,128]{1,0:T(8,128)(2,1)S(1)}, u32[]{:S(2)}, u32[]{:S(2)}) collective-permute-start(bf16[1168,128]{1,0:T(8,128)(2,1)S(1)} %get-tuple-element.48), channel_id=1, source_target_pairs={{0,24},{8,16},{16,8},{24,0},{1,25},{9,17},{17,9},{25,1},{2,26},{10... | collective-permute-start | bytes 897032 | tf_op jit(solution)/shard_map/p01/ppermute | solution.py:234
  25.7 35.4 %collective-permute-start.7 = (bf16[4,2,3,64,128]{4,3,2,1,0:T(8,128)(2,1)S(1)}, bf16[4,2,3,64,128]{4,3,2,1,0:T(8,128)(2,1)S(1)}, u32[]{:S(2)}, u32[]{:S(2)}) collective-permute-start(bf16[4,2,3,64,128]{4,3,2,1,0:T(8,128)(2,1)S(1)} %get-tuple-element.93), channel_id=1, source_target_pairs={{0,1},{1,0},{2,3},{3,2},{4,5},{5,4},{6,7},{7,6},{8,9},{9,8},{10,11... | collective-permute-start | bytes 1179656 | tf_op jit(solution)/shard_map/z01/ppermute | solution.py:234
  26.1 35.0 %collective-permute-start.8 = (bf16[4,2,3,64,128]{4,3,2,1,0:T(8,128)(2,1)S(1)}, bf16[4,2,3,64,128]{4,3,2,1,0:T(8,128)(2,1)S(1)}, u32[]{:S(2)}, u32[]{:S(2)}) collective-permute-start(bf16[4,2,3,64,128]{4,3,2,1,0:T(8,128)(2,1)S(1)} %get-tuple-element.94), channel_id=1, source_target_pairs={{0,2},{1,3},{2,0},{3,1},{4,6},{5,7},{6,4},{7,5},{8,10},{9,11},{10,... | collective-permute-start | bytes 1179656 | tf_op jit(solution)/shard_map/z01/ppermute | solution.py:234
  29.7 31.4 %collective-permute-start.9 = (bf16[4,2,3,64,128]{4,3,2,1,0:T(8,128)(2,1)S(1)}, bf16[4,2,3,64,128]{4,3,2,1,0:T(8,128)(2,1)S(1)}, u32[]{:S(2)}, u32[]{:S(2)}) collective-permute-start(bf16[4,2,3,64,128]{4,3,2,1,0:T(8,128)(2,1)S(1)} %pad_maximum_fusion.4), channel_id=1, source_target_pairs={{0,3},{1,2},{2,1},{3,0},{4,7},{5,6},{6,5},{7,4},{8,11},{9,10},{10,... | collective-permute-start | bytes 1179656 | tf_op jit(solution)/shard_map/z01/ppermute | solution.py:234
  46.3 3.2 %collective-permute-start = (bf16[4,6,3,64,128]{4,3,2,1,0:T(8,128)(2,1)}, bf16[4,6,3,64,128]{4,3,2,1,0:T(8,128)(2,1)}, u32[]{:S(2)}, u32[]{:S(2)}) collective-permute-start(bf16[4,6,3,64,128]{4,3,2,1,0:T(8,128)(2,1)} %all_to_all.14.rest_0_.rest_1_.rest_2_.rest_3_), channel_id=1, source_target_pairs={{0,4},{4,0},{1,5},{5,1},{2,6},{6,2},{3,7},{7,3},{8,12},{12,8},{9,1... | collective-permute-start | bytes 3538952 | tf_op jit(solution)/shard_map/cond/branch_1_fun/cores2/ppermute | solution.py:234
  55.4 16.3 %all-to-all-start.2 = ((bf16[16,1,64,128]{3,2,1,0:T(8,128)(2,1)}), bf16[16,1,64,128]{3,2,1,0:T(8,128)(2,1)S(1)}, u32[]{:S(2)}, u32[]{:S(2)}) async-start(bf16[16,1,64,128]{3,2,1,0:T(8,128)(2,1)} %get-tuple-element.59), calls=%async_computation.2 | async-start | bytes 524288 | tf_op jit(solution)/shard_map/all_to_all | solution.py:299
  61.1 1.8 %collective-permute-start.10 = (bf16[4,2,3,64,128]{4,3,2,1,0:T(8,128)(2,1)S(1)}, bf16[4,2,3,64,128]{4,3,2,1,0:T(8,128)(2,1)S(1)}, u32[]{:S(2)}, u32[]{:S(2)}) collective-permute-start(bf16[4,2,3,64,128]{4,3,2,1,0:T(8,128)(2,1)S(1)} %collective-permute-done.7.rest_1_), channel_id=1, source_target_pairs={{0,4},{4,0},{1,5},{5,1},{2,6},{6,2},{3,7},{7,3},{8,12},{12,8},{9,1... | collective-permute-start | bytes 1179656 | tf_op jit(solution)/shard_map/cores01/ppermute | solution.py:234
  61.2 2.3 %collective-permute-start.11 = (bf16[4,2,3,64,128]{4,3,2,1,0:T(8,128)(2,1)S(1)}, bf16[4,2,3,64,128]{4,3,2,1,0:T(8,128)(2,1)S(1)}, u32[]{:S(2)}, u32[]{:S(2)}) collective-permute-start(bf16[4,2,3,64,128]{4,3,2,1,0:T(8,128)(2,1)S(1)} %collective-permute-done.8.rest_2_), channel_id=1, source_target_pairs={{0,4},{4,0},{1,5},{5,1},{2,6},{6,2},{3,7},{7,3},{8,12},{12,8},{9,1... | collective-permute-start | bytes 1179656 | tf_op jit(solution)/shard_map/cores01/ppermute | solution.py:234
  61.7 2.3 %collective-permute-start.12 = (bf16[4,2,3,64,128]{4,3,2,1,0:T(8,128)(2,1)S(1)}, bf16[4,2,3,64,128]{4,3,2,1,0:T(8,128)(2,1)S(1)}, u32[]{:S(2)}, u32[]{:S(2)}) collective-permute-start(bf16[4,2,3,64,128]{4,3,2,1,0:T(8,128)(2,1)S(1)} %collective-permute-done.9.rest_3_), channel_id=1, source_target_pairs={{0,4},{4,0},{1,5},{5,1},{2,6},{6,2},{3,7},{7,3},{8,12},{12,8},{9,1... | collective-permute-start | bytes 1179656 | tf_op jit(solution)/shard_map/cores01/ppermute | solution.py:234

commit v7 on v6

--- a/solution.py
+++ b/solution.py
@@ -293,7 +293,9 @@
     plane, other, held = lax.cond(seen, last_head, none, singles, own, table)
     rest = [sync(part, held)[0] for part in rest]
     mine = [(plane, head_count)] + [(part, 0) for part in rest]
-    other = [(other, head_count)] + [(over_cores(part, "cores01"), 0) for part in rest]
+    swapped = [over_cores(part, "cores01") for part in rest]
+    held = sync(held, swapped)[0]
+    other = [(other, head_count)] + [(part, 0) for part in swapped]
     held = [heads(0, mine, other, table, True), held]
     held = [
         lax.all_to_all(part, ("head", "chip"), split_axis=0, concat_axis=0, tiled=True)

time: 96.1 us -> 101 us (1.051)
  starting transfers between devices: 22.2 us -> 25.9 us
  blocking collectives: 38.6 us -> 35.9 us
  Pallas kernels: 15.1 us -> 17 us
  waiting for transfers between devices: 15 us -> 16.7 us
    all_to_all x1, starting transfers between devices: 5.65 us -> 9.28 us  [on_pair(): lax.all_to_all(part, ('head', 'chip'), split_axis=0, concat_axis=0, tiled...]
    all_to_all x1, blocking collectives: 22.9 us -> 20.1 us  [on_pair(): lax.all_to_all(part, ('head', 'chip'), split_axis=0, concat_axis=0, tiled...]
    pallas_call x2, Pallas kernels: 13.6 us -> 15.5 us  [attend(): pl.pallas_call(functools.partial(attend_kernel, scale=LOG2E / math.sqrt(h...]
    all_to_all x1, waiting for transfers between devices: 0.01 us -> 1.7 us  [on_pair(): lax.all_to_all(part, ('head', 'chip'), split_axis=0, concat_axis=0, tiled...]
  transfers between devices with their start and end apart: 14 -> 14, of which waited for: 6 -> 7; matrix products, arithmetic and copies ran while one was open for 1% -> 1% of each run, Pallas kernels for 14% -> 15%
where the time goes in v7:
time: 101 us; the launch traced here: 100 us
  blocking collectives  35.9 us (36%)
  starting transfers between devices  25.9 us (26%)
  Pallas kernels  17 us (17%)
  waiting for transfers between devices  16.7 us (17%)
  local copies, waits for them, and re-layouts  3.56 us (4%)
    all_to_all x1, blocking collectives, on_pair(): lax.all_to_all(part, ('head', 'chip'), split_axis=0, concat_axis=0, tiled...  20.1 us
    ppermute x13, starting transfers between devices, swap(): return lax.ppermute(value, axis, [(i, i ^ k) for i in range(size)])  16.6 us
    all_to_all x1, blocking collectives, over_p(): lax.all_to_all(value, 'chip', split_axis=0, concat_axis=0, tiled=True)  15.7 us
    pallas_call x2, Pallas kernels, attend(): pl.pallas_call(functools.partial(attend_kernel, scale=LOG2E / math.sqrt(h...  15.5 us
    ppermute x13, waiting for transfers between devices, swap(): return lax.ppermute(value, axis, [(i, i ^ k) for i in range(size)])  15 us
    all_to_all x1, starting transfers between devices, on_pair(): lax.all_to_all(part, ('head', 'chip'), split_axis=0, concat_axis=0, tiled...  9.28 us
  transfers between devices with their start and end apart: 14, of which 7 were waited for; matrix products, arithmetic and copies ran while one was open for 1% of the time, Pallas kernels for 15%

profile of v7, /device:TPU:0, one launch (start us, length us, event | category | flops | bytes accessed | tf_op | source)
XLA Modules:
  0.0 100.3 jit_solution(7884621472878838535)
XLA Ops:
  0.0 0.0 copy-start
  0.0 0.0 copy-start.1
  0.0 1.8 %slice_bitcast_fusion = (bf16[128,3072]{1,0:T(8,128)(2,1)S(1)}, bf16[128,3072]{1,0:T(8,128)(2,1)S(1)}, bf16[128,3072]{1,0:T(8,128)(2,1)S(1)}) fusion(bf16[128,3,3072]{2,0,1:T(8,128)(2,1)} %param.5), kind=kLoop, calls=%fused_computation.3 | loop fusion | bytes 4718592 | tf_op jit(solution)/shard_map/squeeze | solution.py:245
  1.8 0.1 pad_add_fusion.me_ref
  1.9 0.0 copy-done
  1.9 0.0 copy-done.1
  1.9 1.5 %pack.1 = (bf16[4,1,3,64,128]{4,3,2,1,0:T(8,128)(2,1)S(1)}, bf16[4,1,3,64,128]{4,3,2,1,0:T(8,128)(2,1)S(1)}, bf16[4,1,3,64,128]{4,3,2,1,0:T(8,128)(2,1)S(1)}, bf...) custom-call(s32[3]{0:T(128)S(1)} %pad_add_fusion.me_ref, ...), custom_call_target="tpu_custom_call" | custom-call | tf_op jit(solution)/shard_map/pack/pallas_call | solution.py:87
  3.4 3.1 %collective-permute-start.4 = (bf16[4,1,3,64,128]{4,3,2,1,0:T(8,128)(2,1)S(1)}, bf16[4,1,3,64,128]{4,3,2,1,0:T(8,128)(2,1)S(1)}, u32[]{:S(2)}, u32[]{:S(2)}) collective-permute-start(bf16[4,1,3,64,128]{4,3,2,1,0:T(8,128)(2,1)S(1)} %get-tuple-element.51), channel_id=1, source_target_pairs={{0,1},{1,0},{2,3},{3,2},{4,5},{5,4},{6,7},{7,6},{8,9},{9,8},{10,11... | collective-permute-start | bytes 589832 | tf_op jit(solution)/shard_map/z2/ppermute | solution.py:234
  6.5 2.6 %collective-permute-start.5 = (bf16[4,1,3,64,128]{4,3,2,1,0:T(8,128)(2,1)S(1)}, bf16[4,1,3,64,128]{4,3,2,1,0:T(8,128)(2,1)S(1)}, u32[]{:S(2)}, u32[]{:S(2)}) collective-permute-start(bf16[4,1,3,64,128]{4,3,2,1,0:T(8,128)(2,1)S(1)} %get-tuple-element.52), channel_id=1, source_target_pairs={{0,2},{1,3},{2,0},{3,1},{4,6},{5,7},{6,4},{7,5},{8,10},{9,11},{10,... | collective-permute-start | bytes 589832 | tf_op jit(solution)/shard_map/z2/ppermute | solution.py:234
  9.1 0.0 collective-permute-start.6
  9.1 1.7 %collective-permute-start.1 = (bf16[1168,128]{1,0:T(8,128)(2,1)S(1)}, bf16[1168,128]{1,0:T(8,128)(2,1)S(1)}, u32[]{:S(2)}, u32[]{:S(2)}) collective-permute-start(bf16[1168,128]{1,0:T(8,128)(2,1)S(1)} %get-tuple-element.47), channel_id=1, source_target_pairs={{0,8},{8,0},{16,24},{24,16},{1,9},{9,1},{17,25},{25,17},{2,10},{10... | collective-permute-start | bytes 897032 | tf_op jit(solution)/shard_map/p01/ppermute | solution.py:234
  10.8 1.5 %collective-permute-start.2 = (bf16[1168,128]{1,0:T(8,128)(2,1)S(1)}, bf16[1168,128]{1,0:T(8,128)(2,1)S(1)}, u32[]{:S(2)}, u32[]{:S(2)}) collective-permute-start(bf16[1168,128]{1,0:T(8,128)(2,1)S(1)} %get-tuple-element.48), channel_id=1, source_target_pairs={{0,16},{8,24},{16,0},{24,8},{1,17},{9,25},{17,1},{25,9},{2,18},{10... | collective-permute-start | bytes 897032 | tf_op jit(solution)/shard_map/p01/ppermute | solution.py:234
  12.3 0.5 slice.119
  13.5 3.8 %collective-permute-done.1 = bf16[1168,128]{1,0:T(8,128)(2,1)S(1)} collective-permute-done((bf16[1168,128]{1,0:T(8,128)(2,1)S(1)}, bf16[1168,128]{1,0:T(8,128)(2,1)S(1)}, u32[]{:S(2)}, u32[]{:S(2)}) %collective-permute-start.1) | collective-permute-done | bytes 299040 | tf_op jit(solution)/shard_map/p01/ppermute | solution.py:234
  17.3 2.4 %collective-permute-start.3 = (bf16[1168,128]{1,0:T(8,128)(2,1)S(1)}, bf16[1168,128]{1,0:T(8,128)(2,1)S(1)}, u32[]{:S(2)}, u32[]{:S(2)}) collective-permute-start(bf16[1168,128]{1,0:T(8,128)(2,1)S(1)} %get-tuple-element.49), channel_id=1, source_target_pairs={{0,24},{8,16},{16,8},{24,0},{1,25},{9,17},{17,9},{25,1},{2,26},{10... | collective-permute-start | bytes 897032 | tf_op jit(solution)/shard_map/p01/ppermute | solution.py:234
  19.8 0.0 collective-permute-done.2
  19.8 5.7 %collective-permute-done.3 = bf16[1168,128]{1,0:T(8,128)(2,1)S(1)} collective-permute-done((bf16[1168,128]{1,0:T(8,128)(2,1)S(1)}, bf16[1168,128]{1,0:T(8,128)(2,1)S(1)}, u32[]{:S(2)}, u32[]{:S(2)}) %collective-permute-start.3) | collective-permute-done | bytes 299040 | tf_op jit(solution)/shard_map/p01/ppermute | solution.py:234
  25.6 0.1 pad_maximum_fusion.2
  25.7 0.4 collective-permute-start.7
  26.1 3.5 %collective-permute-start.8 = (bf16[4,2,3,64,128]{4,3,2,1,0:T(8,128)(2,1)S(1)}, bf16[4,2,3,64,128]{4,3,2,1,0:T(8,128)(2,1)S(1)}, u32[]{:S(2)}, u32[]{:S(2)}) collective-permute-start(bf16[4,2,3,64,128]{4,3,2,1,0:T(8,128)(2,1)S(1)} %get-tuple-element.96), channel_id=1, source_target_pairs={{0,2},{1,3},{2,0},{3,1},{4,6},{5,7},{6,4},{7,5},{8,10},{9,11},{10,... | collective-permute-start | bytes 1179656 | tf_op jit(solution)/shard_map/z01/ppermute | solution.py:234
  29.6 0.1 pad_maximum_fusion.4
  29.7 0.0 collective-permute-done.4
  29.7 0.6 collective-permute-start.9
  30.3 0.0 collective-permute-done.5
  30.3 0.0 collective-permute-done.6
  30.4 26.2 %conditional.1 = (bf16[4,6,3,64,128]{4,3,2,1,0:T(8,128)(2,1)}, bf16[4,6,3,64,128]{4,3,2,1,0:T(8,128)(2,1)}, bf16[16,1,64,128]{3,2,1,0:T(8,128)(2,1)}) conditional(s32[]{:T(128)} %bitcast.25, () %tuple.18, (bf16[4,1,3,64,128]{4,3,2,1,0:T(8,128)(2,1)S(1)}, bf16[4,1,3,64,128]{4,3,2,1,0:T(8,128)(2,1)S(1)}, bf16[4,1,3,64,128]{4,3,2,1,0:T(8,128)(2,1)S(1)}, ...), branch_computations={%region_0.0_spmd, %region_1.0_spmd} | conditional | flops 1769473 | bytes 11010113 | solution.py:293
  30.4 0.1 maximum_bitcast_fusion
  30.5 0.1 pad_maximum_fusion
  30.6 15.7 %all_to_all.14.rest_0_.rest_1_.rest_2_.rest_3_ = bf16[4,6,3,64,128]{4,3,2,1,0:T(8,128)(2,1)} all-to-all(bf16[4,6,3,64,128]{4,3,2,1,0:T(8,128)(2,1)S(1)} %pad_maximum_fusion), channel_id=1, replica_groups=mesh['chip'=4,'core'=2,'head'=4] {'chip'}, dimensions={0} | all-to-all | bytes 2359296 | tf_op jit(solution)/shard_map/cond/branch_1_fun/plane/all_to_all | solution.py:254
  46.3 0.0 collective-permute-start
  46.3 3.2 %collective-permute-done.rest_4_.rest_5_.rest_6_.rest_7_ = bf16[4,6,3,64,128]{4,3,2,1,0:T(8,128)(2,1)} collective-permute-done((bf16[4,6,3,64,128]{4,3,2,1,0:T(8,128)(2,1)}, bf16[4,6,3,64,128]{4,3,2,1,0:T(8,128)(2,1)}, u32[]{:S(2)}, u32[]{:S(2)}) %collective-permute-start) | collective-permute-done | bytes 1179680 | tf_op jit(solution)/shard_map/cond/branch_1_fun/cores2/ppermute | solution.py:234
  49.5 7.0 %attend.2 = bf16[16,1,64,128]{3,2,1,0:T(8,128)(2,1)} custom-call(s32[3]{0:T(128)S(1)} %get-tuple-element.24.me_ref, s32[4,16,128]{2,1,0:T(8,128)S(1)} %get-tuple-element.25.table_ref, bf16[4,6,3,64,128]{4,3,2,1,0:T(8,128)(2,1)} %all_to_all.14.rest_0_.rest_1_.rest_2_.rest_3_, bf16[4,6,3,64,128]{4,3,2,1,0:T(8,128)(2,1)} %all_to_all.14.rest_0_.rest_1_.rest_2_.rest_3_, ...), custom_call_target="tpu_custom_call" | custom-call | flops 1 | bytes 1 | tf_op jit(solution)/shard_map/cond/branch_1_fun/heads2/attend/pallas_call | solution.py:205
  56.5 0.0 collective-permute-done.9.rest_3_
  56.5 0.0 collective-permute-done.8.rest_2_
  56.5 0.0 collective-permute-done.7.rest_1_
  56.6 0.2 collective-permute-start.10
  56.7 0.4 collective-permute-start.11
  57.1 0.1 collective-permute-start.12
  57.3 1.1 %collective-permute-done.10.rest_5_ = bf16[4,2,3,64,128]{4,3,2,1,0:T(8,128)(2,1)S(1)} collective-permute-done((bf16[4,2,3,64,128]{4,3,2,1,0:T(8,128)(2,1)S(1)}, bf16[4,2,3,64,128]{4,3,2,1,0:T(8,128)(2,1)S(1)}, u32[]{:S(2)}, u32[]{:S(2)}) %collective-permute-start.10) | collective-permute-done | bytes 393248 | tf_op jit(solution)/shard_map/cores01/ppermute | solution.py:234
  58.3 0.6 collective-permute-done.11.rest_6_
  58.9 0.6 collective-permute-done.12.rest_7_
  59.5 9.3 %all-to-all-start.2 = ((bf16[16,1,64,128]{3,2,1,0:T(8,128)(2,1)}), bf16[16,1,64,128]{3,2,1,0:T(8,128)(2,1)S(1)}, u32[]{:S(2)}, u32[]{:S(2)}) async-start(bf16[16,1,64,128]{3,2,1,0:T(8,128)(2,1)} %get-tuple-element.65), calls=%async_computation.2 | async-start | bytes 524288 | tf_op jit(solution)/shard_map/all_to_all | solution.py:301
  68.8 8.5 %attend.3 = bf16[16,2,64,128]{3,2,1,0:T(8,128)(2,1)S(1)} custom-call(s32[3]{0:T(128)S(1)} %pad_add_fusion.me_ref, s32[4,16,128]{2,1,0:T(8,128)S(1)} %maximum_convert_fusion.table_ref, bf16[4,6,3,64,128]{4,3,2,1,0:T(8,128)(2,1)} %get-tuple-element.59.rest_0_, bf16[4,2,3,64,128]{4,3,2,1,0:T(8,128)(2,1)S(1)} %collective-permute-done.7.rest_1_, ...), custom_call_target="tpu_custom_call" | custom-call | flops 1 | bytes 1 | tf_op jit(solution)/shard_map/heads0/attend/pallas_call | solution.py:205
  77.2 1.7 %all-to-all-done.2 = bf16[16,1,64,128]{3,2,1,0:T(8,128)(2,1)S(1)} async-done(((bf16[16,1,64,128]{3,2,1,0:T(8,128)(2,1)}), bf16[16,1,64,128]{3,2,1,0:T(8,128)(2,1)S(1)}, u32[]{:S(2)}, u32[]{:S(2)}) %all-to-all-start.2) | async-done | bytes 262176 | tf_op jit(solution)/shard_map/all_to_all | solution.py:301
  78.9 20.1 %all_to_all.15 = bf16[16,2,64,128]{3,2,1,0:T(8,128)(2,1)S(1)} all-to-all(bf16[16,2,64,128]{3,2,1,0:T(8,128)(2,1)S(1)} %attend.3), channel_id=1, replica_groups=mesh['chip'=4,'core'=2,'head'=4] {'head','chip'}, dimensions={0} | all-to-all | bytes 1048576 | tf_op jit(solution)/shard_map/all_to_all | solution.py:301
  99.1 0.1 pad_maximum_fusion.1
  99.1 1.2 %copy.13 = bf16[128,3072]{1,0:T(8,128)(2,1)} copy(bf16[128,3072]{0,1:T(8,128)(2,1)S(1)} %bitcast.53) | data formatting | bytes 1572864 | tf_op jit(solution)/shard_map/transpose | solution.py:307
  (9 shorter events, 0.1 us)
Async XLA Ops:
  0.0 1.9 %copy-start = (s32[12,4,8]{0,2,1:T(8,128)S(1)}, s32[12,4,8]{0,2,1:T(8,128)}, u32[]{:S(2)}) copy-start(s32[12,4,8]{0,2,1:T(8,128)} %param.6) | copy-start | bytes 4612
  0.0 1.9 %copy-start.1 = (s32[12,4]{0,1:T(4,128)S(1)}, s32[12,4]{0,1:T(4,128)}, u32[]{:S(2)}) copy-start(s32[12,4]{0,1:T(4,128)} %param.7) | copy-start | bytes 580
  3.4 26.3 %collective-permute-start.4 = (bf16[4,1,3,64,128]{4,3,2,1,0:T(8,128)(2,1)S(1)}, bf16[4,1,3,64,128]{4,3,2,1,0:T(8,128)(2,1)S(1)}, u32[]{:S(2)}, u32[]{:S(2)}) collective-permute-start(bf16[4,1,3,64,128]{4,3,2,1,0:T(8,128)(2,1)S(1)} %get-tuple-element.51), channel_id=1, source_target_pairs={{0,1},{1,0},{2,3},{3,2},{4,5},{5,4},{6,7},{7,6},{8,9},{9,8},{10,11... | collective-permute-start | bytes 589832 | tf_op jit(solution)/shard_map/z2/ppermute | solution.py:234
  6.5 23.9 %collective-permute-start.5 = (bf16[4,1,3,64,128]{4,3,2,1,0:T(8,128)(2,1)S(1)}, bf16[4,1,3,64,128]{4,3,2,1,0:T(8,128)(2,1)S(1)}, u32[]{:S(2)}, u32[]{:S(2)}) collective-permute-start(bf16[4,1,3,64,128]{4,3,2,1,0:T(8,128)(2,1)S(1)} %get-tuple-element.52), channel_id=1, source_target_pairs={{0,2},{1,3},{2,0},{3,1},{4,6},{5,7},{6,4},{7,5},{8,10},{9,11},{10,... | collective-permute-start | bytes 589832 | tf_op jit(solution)/shard_map/z2/ppermute | solution.py:234
  9.1 21.3 %collective-permute-start.6 = (bf16[4,1,3,64,128]{4,3,2,1,0:T(8,128)(2,1)S(1)}, bf16[4,1,3,64,128]{4,3,2,1,0:T(8,128)(2,1)S(1)}, u32[]{:S(2)}, u32[]{:S(2)}) collective-permute-start(bf16[4,1,3,64,128]{4,3,2,1,0:T(8,128)(2,1)S(1)} %get-tuple-element.53), channel_id=1, source_target_pairs={{0,3},{1,2},{2,1},{3,0},{4,7},{5,6},{6,5},{7,4},{8,11},{9,10},{10,... | collective-permute-start | bytes 589832 | tf_op jit(solution)/shard_map/z2/ppermute | solution.py:234
  9.1 8.3 %collective-permute-start.1 = (bf16[1168,128]{1,0:T(8,128)(2,1)S(1)}, bf16[1168,128]{1,0:T(8,128)(2,1)S(1)}, u32[]{:S(2)}, u32[]{:S(2)}) collective-permute-start(bf16[1168,128]{1,0:T(8,128)(2,1)S(1)} %get-tuple-element.47), channel_id=1, source_target_pairs={{0,8},{8,0},{16,24},{24,16},{1,9},{9,1},{17,25},{25,17},{2,10},{10... | collective-permute-start | bytes 897032 | tf_op jit(solution)/shard_map/p01/ppermute | solution.py:234
  10.8 9.0 %collective-permute-start.2 = (bf16[1168,128]{1,0:T(8,128)(2,1)S(1)}, bf16[1168,128]{1,0:T(8,128)(2,1)S(1)}, u32[]{:S(2)}, u32[]{:S(2)}) collective-permute-start(bf16[1168,128]{1,0:T(8,128)(2,1)S(1)} %get-tuple-element.48), channel_id=1, source_target_pairs={{0,16},{8,24},{16,0},{24,8},{1,17},{9,25},{17,1},{25,9},{2,18},{10... | collective-permute-start | bytes 897032 | tf_op jit(solution)/shard_map/p01/ppermute | solution.py:234
  17.3 8.2 %collective-permute-start.3 = (bf16[1168,128]{1,0:T(8,128)(2,1)S(1)}, bf16[1168,128]{1,0:T(8,128)(2,1)S(1)}, u32[]{:S(2)}, u32[]{:S(2)}) collective-permute-start(bf16[1168,128]{1,0:T(8,128)(2,1)S(1)} %get-tuple-element.49), channel_id=1, source_target_pairs={{0,24},{8,16},{16,8},{24,0},{1,25},{9,17},{17,9},{25,1},{2,26},{10... | collective-permute-start | bytes 897032 | tf_op jit(solution)/shard_map/p01/ppermute | solution.py:234
  25.7 30.8 %collective-permute-start.7 = (bf16[4,2,3,64,128]{4,3,2,1,0:T(8,128)(2,1)S(1)}, bf16[4,2,3,64,128]{4,3,2,1,0:T(8,128)(2,1)S(1)}, u32[]{:S(2)}, u32[]{:S(2)}) collective-permute-start(bf16[4,2,3,64,128]{4,3,2,1,0:T(8,128)(2,1)S(1)} %get-tuple-element.95), channel_id=1, source_target_pairs={{0,1},{1,0},{2,3},{3,2},{4,5},{5,4},{6,7},{7,6},{8,9},{9,8},{10,11... | collective-permute-start | bytes 1179656 | tf_op jit(solution)/shard_map/z01/ppermute | solution.py:234
  26.1 30.4 %collective-permute-start.8 = (bf16[4,2,3,64,128]{4,3,2,1,0:T(8,128)(2,1)S(1)}, bf16[4,2,3,64,128]{4,3,2,1,0:T(8,128)(2,1)S(1)}, u32[]{:S(2)}, u32[]{:S(2)}) collective-permute-start(bf16[4,2,3,64,128]{4,3,2,1,0:T(8,128)(2,1)S(1)} %get-tuple-element.96), channel_id=1, source_target_pairs={{0,2},{1,3},{2,0},{3,1},{4,6},{5,7},{6,4},{7,5},{8,10},{9,11},{10,... | collective-permute-start | bytes 1179656 | tf_op jit(solution)/shard_map/z01/ppermute | solution.py:234
  29.7 26.8 %collective-permute-start.9 = (bf16[4,2,3,64,128]{4,3,2,1,0:T(8,128)(2,1)S(1)}, bf16[4,2,3,64,128]{4,3,2,1,0:T(8,128)(2,1)S(1)}, u32[]{:S(2)}, u32[]{:S(2)}) collective-permute-start(bf16[4,2,3,64,128]{4,3,2,1,0:T(8,128)(2,1)S(1)} %pad_maximum_fusion.4), channel_id=1, source_target_pairs={{0,3},{1,2},{2,1},{3,0},{4,7},{5,6},{6,5},{7,4},{8,11},{9,10},{10,... | collective-permute-start | bytes 1179656 | tf_op jit(solution)/shard_map/z01/ppermute | solution.py:234
  46.3 3.2 %collective-permute-start = (bf16[4,6,3,64,128]{4,3,2,1,0:T(8,128)(2,1)}, bf16[4,6,3,64,128]{4,3,2,1,0:T(8,128)(2,1)}, u32[]{:S(2)}, u32[]{:S(2)}) collective-permute-start(bf16[4,6,3,64,128]{4,3,2,1,0:T(8,128)(2,1)} %all_to_all.14.rest_0_.rest_1_.rest_2_.rest_3_), channel_id=1, source_target_pairs={{0,4},{4,0},{1,5},{5,1},{2,6},{6,2},{3,7},{7,3},{8,12},{12,8},{9,1... | collective-permute-start | bytes 3538952 | tf_op jit(solution)/shard_map/cond/branch_1_fun/cores2/ppermute | solution.py:234
  56.6 1.8 %collective-permute-start.10 = (bf16[4,2,3,64,128]{4,3,2,1,0:T(8,128)(2,1)S(1)}, bf16[4,2,3,64,128]{4,3,2,1,0:T(8,128)(2,1)S(1)}, u32[]{:S(2)}, u32[]{:S(2)}) collective-permute-start(bf16[4,2,3,64,128]{4,3,2,1,0:T(8,128)(2,1)S(1)} %collective-permute-done.7.rest_1_), channel_id=1, source_target_pairs={{0,4},{4,0},{1,5},{5,1},{2,6},{6,2},{3,7},{7,3},{8,12},{12,8},{9,1... | collective-permute-start | bytes 1179656 | tf_op jit(solution)/shard_map/cores01/ppermute | solution.py:234
  56.7 2.2 %collective-permute-start.11 = (bf16[4,2,3,64,128]{4,3,2,1,0:T(8,128)(2,1)S(1)}, bf16[4,2,3,64,128]{4,3,2,1,0:T(8,128)(2,1)S(1)}, u32[]{:S(2)}, u32[]{:S(2)}) collective-permute-start(bf16[4,2,3,64,128]{4,3,2,1,0:T(8,128)(2,1)S(1)} %collective-permute-done.8.rest_2_), channel_id=1, source_target_pairs={{0,4},{4,0},{1,5},{5,1},{2,6},{6,2},{3,7},{7,3},{8,12},{12,8},{9,1... | collective-permute-start | bytes 1179656 | tf_op jit(solution)/shard_map/cores01/ppermute | solution.py:234
  57.1 2.3 %collective-permute-start.12 = (bf16[4,2,3,64,128]{4,3,2,1,0:T(8,128)(2,1)S(1)}, bf16[4,2,3,64,128]{4,3,2,1,0:T(8,128)(2,1)S(1)}, u32[]{:S(2)}, u32[]{:S(2)}) collective-permute-start(bf16[4,2,3,64,128]{4,3,2,1,0:T(8,128)(2,1)S(1)} %collective-permute-done.9.rest_3_), channel_id=1, source_target_pairs={{0,4},{4,0},{1,5},{5,1},{2,6},{6,2},{3,7},{7,3},{8,12},{12,8},{9,1... | collective-permute-start | bytes 1179656 | tf_op jit(solution)/shard_map/cores01/ppermute | solution.py:234
  59.5 19.5 %all-to-all-start.2 = ((bf16[16,1,64,128]{3,2,1,0:T(8,128)(2,1)}), bf16[16,1,64,128]{3,2,1,0:T(8,128)(2,1)S(1)}, u32[]{:S(2)}, u32[]{:S(2)}) async-start(bf16[16,1,64,128]{3,2,1,0:T(8,128)(2,1)} %get-tuple-element.65), calls=%async_computation.2 | async-start | bytes 524288 | tf_op jit(solution)/shard_map/all_to_all | solution.py:301
